TPU v7x, 32 devices: a whole 2x2x4 slice. The times are simulated.
32 devices in a mesh: dp: 8 (over z, x), tensor: 4 (over y, core).
Axes of the slice: x: 2, y: 2, z: 4, core: 2. Of those that a mesh axis runs over, the one named last changes fastest.
Arguments:
- tokens: bfloat16 [16, 1088, 1024], P('dp', 'tensor'), may hold values from -12 to 12
- cotangent: bfloat16 [16, 1088, 1024], P('dp', 'tensor'), may hold values from -6 to 6
- lengths: int32 [16], P('dp'), may hold values from 544 to 1088, as said below
- groups: int32 [16], P('dp'), may hold values from 0 to 3, as said below
- w_qkv: bfloat16 [1024, 3, 1024], P(None, None, 'tensor'), may hold values from -0.1875 to 0.1875
- w_out: bfloat16 [1024, 1024], P('tensor'), may hold values from -0.75 to 0.75
- w_up: bfloat16 [1024, 4096], P(None, 'tensor'), may hold values from -0.1875 to 0.1875
- w_down: bfloat16 [4096, 1024], P('tensor'), may hold values from -0.09375 to 0.09375
- gains: float32 [4, 1024], replicated, may hold values from 0.25 to 1.75
- biases: float32 [4, 1024], replicated, may hold values from -1.5 to 1.5
Outputs:
- output: bfloat16 [16, 1088, 1024], P('dp', 'tensor')
- input_grad: bfloat16 [16, 1088, 1024], P('dp', 'tensor')
- grad_qkv: float32 [1024, 3, 1024], P(None, None, 'tensor')
- grad_out: float32 [1024, 1024], P('tensor')
- grad_up: float32 [1024, 4096], P(None, 'tensor')
- grad_down: float32 [4096, 1024], P('tensor')
- grad_gains: float32 [4, 1024], replicated
- grad_biases: float32 [4, 1024], replicated
- group_rms: float32 [4, 3], replicated
Inputs may be any that keep to these rules, and one draw needn't show every extreme that they name: `lengths`: some row has all 1088 slots valid. `groups`: every group has at least one row.
All inputs are finite; a program needn't handle non-finite values.
Results may differ from a plain program's by a relative error of at most 0.013.
Values may be sent and summed in bfloat16 or wider, within the bound.
No kernel may reach another device: no remote copies, remote signals or barrier semaphores. Data moves between devices by JAX's collectives and lax.ppermute only.
A program may use at most 192 MiB of HBM per device.

v0:
```python
import jax
import jax.numpy as jnp
from jax import lax
from jax.sharding import PartitionSpec as P

HEAD_DIM = 64
QBLOCK = 544
GROUPS = 4


epsilon = 1e-05
negative_fill = -1e30
relax_alpha = 32.0


def layer_norm(values, scale_vec, shift_vec):
    center = values - jnp.mean(values, axis=-1, keepdims=True)
    spread = jnp.mean(center * center, axis=-1, keepdims=True)
    return center * lax.rsqrt(spread + epsilon) * scale_vec + shift_vec


def gelu_tanh(values):
    return jax.nn.gelu(values, approximate=True)


def matmul_rows(left, right):
    return jnp.einsum("rsd,df->rsf", left, right, preferred_element_type=jnp.float32)


def matmul_back(left, right):
    return jnp.einsum("rsf,df->rsd", left, right, preferred_element_type=jnp.float32)


def outer_sum(left, right):
    return jnp.einsum("rsd,rsf->df", left, right, preferred_element_type=jnp.float32)


def masked_scores(query_block, key_row, block_index, key_index, length):
    scores = jnp.einsum(
        "qhd,khd->hqk", query_block, key_row, preferred_element_type=jnp.float32
    ) * (1.0 / (relax_alpha * HEAD_DIM**0.5))
    query_index = block_index * QBLOCK + jnp.arange(QBLOCK, dtype=jnp.int32)
    allowed = (key_index[None, :] <= query_index[:, None]) & (key_index[None, :] < length)
    return jnp.where(allowed[None], scores, negative_fill)


def attend_row(inputs):
    query_row, key_row, value_row, length = inputs
    slot_count = query_row.shape[0]
    block_count = slot_count // QBLOCK
    key_index = jnp.arange(slot_count, dtype=jnp.int32)
    query_blocks = query_row.reshape(block_count, QBLOCK, query_row.shape[1], HEAD_DIM)

    def one_block(block_index):
        query_block = query_blocks[block_index]
        scores = masked_scores(query_block, key_row, block_index, key_index, length)
        row_max = jnp.max(scores, axis=-1, keepdims=True)
        weights = jnp.exp(relax_alpha * (scores - row_max))
        totals = jnp.sum(weights, axis=-1, keepdims=True)
        probs_low = (weights / totals).astype(jnp.bfloat16)
        output = jnp.einsum(
            "hqk,khd->qhd", probs_low, value_row, preferred_element_type=jnp.float32
        )
        return (output, (relax_alpha * row_max + jnp.log(totals))[:, :, 0])

    outputs, log_totals = lax.map(one_block, jnp.arange(block_count, dtype=jnp.int32))
    return (outputs.reshape(query_row.shape), log_totals)


def attend_row_back(inputs):
    query_row, key_row, value_row, grad_row, log_totals, length = inputs
    slot_count = query_row.shape[0]
    block_count = slot_count // QBLOCK
    key_index = jnp.arange(slot_count, dtype=jnp.int32)
    query_blocks = query_row.reshape(block_count, QBLOCK, query_row.shape[1], HEAD_DIM)
    grad_blocks = grad_row.reshape(block_count, QBLOCK, query_row.shape[1], HEAD_DIM)
    scale_factor = 1.0 / (relax_alpha * HEAD_DIM**0.5)

    def one_block(carry, block_index):
        key_grad, value_grad = carry
        query_block = query_blocks[block_index]
        grad_block = grad_blocks[block_index]
        scores = masked_scores(query_block, key_row, block_index, key_index, length)
        probs = jnp.exp(relax_alpha * scores - log_totals[block_index][:, :, None])
        probs_low = probs.astype(jnp.bfloat16)
        value_grad = value_grad + jnp.einsum(
            "hqk,qhd->khd", probs_low, grad_block, preferred_element_type=jnp.float32
        )
        probs_grad = jnp.einsum(
            "qhd,khd->hqk", grad_block, value_row, preferred_element_type=jnp.float32
        )
        inner = jnp.sum(probs * probs_grad, axis=-1, keepdims=True)
        scores_grad = (relax_alpha * probs * (probs_grad - inner)).astype(jnp.bfloat16)
        query_grad = (
            jnp.einsum("hqk,khd->qhd", scores_grad, key_row, preferred_element_type=jnp.float32)
            * scale_factor
        )
        key_grad = (
            key_grad
            + jnp.einsum(
                "hqk,qhd->khd", scores_grad, query_block, preferred_element_type=jnp.float32
            )
            * scale_factor
        )
        return ((key_grad, value_grad), query_grad)

    zeros_init = jnp.zeros(key_row.shape, jnp.float32)
    (key_grad, value_grad), query_grads = lax.scan(
        one_block, (zeros_init, zeros_init), jnp.arange(block_count, dtype=jnp.int32)
    )
    return (query_grads.reshape(query_row.shape), key_grad, value_grad)


def per_device(tokens, cotangent, lengths, groups, w_qkv, w_out, w_up, w_down, gains, biases):
    row_count, share_slots, model_width = tokens.shape
    local_cols = w_qkv.shape[2]
    local_heads = local_cols // HEAD_DIM
    slot_count = share_slots * lax.axis_size("tensor")
    positions = lax.axis_index("tensor") * share_slots + jnp.arange(share_slots, dtype=jnp.int32)
    valid_share = (positions[None, :] < lengths[:, None]).astype(jnp.float32)
    inputs_share = tokens.astype(jnp.float32)
    attn_in16 = layer_norm(inputs_share, gains[0], biases[0]).astype(jnp.bfloat16)
    attn_full = lax.all_gather(attn_in16, "tensor", axis=1, tiled=True)
    w_qkv_flat = w_qkv.reshape(model_width, 3 * local_cols)
    projected = matmul_rows(attn_full, w_qkv_flat).astype(jnp.bfloat16)
    projected = projected.reshape(row_count, slot_count, 3, local_heads, HEAD_DIM)
    queries = projected[:, :, 0]
    keys_all = projected[:, :, 1]
    values_all = projected[:, :, 2]
    attended, log_totals = lax.map(attend_row, (queries, keys_all, values_all, lengths))
    attended16 = attended.astype(jnp.bfloat16).reshape(row_count, slot_count, local_cols)
    attn_share = lax.psum_scatter(
        matmul_rows(attended16, w_out), "tensor", scatter_dimension=1, tiled=True
    )
    attn_branch = layer_norm(attn_share, gains[1], biases[1])
    middle = inputs_share + attn_branch
    ffn_in16 = layer_norm(middle, gains[2], biases[2]).astype(jnp.bfloat16)
    ffn_full = lax.all_gather(ffn_in16, "tensor", axis=1, tiled=True)
    hidden = matmul_rows(ffn_full, w_up)
    activated16 = gelu_tanh(hidden).astype(jnp.bfloat16)
    ffn_share = lax.psum_scatter(
        matmul_rows(activated16, w_down), "tensor", scatter_dimension=1, tiled=True
    )
    ffn_branch = layer_norm(ffn_share, gains[3], biases[3])
    result = middle + ffn_branch
    squares = jnp.stack(
        [
            jnp.sum(valid_share * jnp.sum(branch_out * branch_out, axis=-1), axis=1)
            for branch_out in (result, attn_branch, ffn_branch)
        ],
        axis=1,
    )
    member = (groups[:, None] == jnp.arange(GROUPS, dtype=jnp.int32)[None, :]).astype(jnp.float32)
    group_sums = jnp.dot(member.T, squares, precision=lax.Precision.HIGHEST)
    group_counts = jnp.dot(member.T, jnp.sum(valid_share, axis=1), precision=lax.Precision.HIGHEST)
    group_sums, group_counts = lax.psum((group_sums, group_counts), ("dp", "tensor"))
    attn_rows_again, ffn_rows_again = (
        lax.all_gather(
            layer_norm(inputs_share, gains[0], biases[0]).astype(jnp.bfloat16),
            "tensor",
            axis=1,
            tiled=True,
        ),
        lax.all_gather(
            layer_norm(middle, gains[2], biases[2]).astype(jnp.bfloat16),
            "tensor",
            axis=1,
            tiled=True,
        ),
    )
    out_grad = cotangent.astype(jnp.float32) * valid_share[:, :, None]
    _, norm_back = jax.vjp(layer_norm, ffn_share, gains[3], biases[3])
    ffn_sum_grad, gain_four, bias_four = norm_back(out_grad)
    ffn_out16 = lax.all_gather(ffn_sum_grad.astype(jnp.bfloat16), "tensor", axis=1, tiled=True)
    grad_down = outer_sum(activated16, ffn_out16)
    activated_grad = matmul_back(ffn_out16, w_down)
    _, gelu_back = jax.vjp(gelu_tanh, hidden)
    hidden_grad16 = gelu_back(activated_grad)[0].astype(jnp.bfloat16)
    grad_up = outer_sum(ffn_rows_again, hidden_grad16)
    ffn_in_grad = lax.psum_scatter(
        matmul_back(hidden_grad16, w_up), "tensor", scatter_dimension=1, tiled=True
    )
    _, norm_back = jax.vjp(layer_norm, middle, gains[2], biases[2])
    middle_part, gain_three, bias_three = norm_back(ffn_in_grad)
    middle_grad = out_grad + middle_part
    _, norm_back = jax.vjp(layer_norm, attn_share, gains[1], biases[1])
    attn_sum_grad, gain_two, bias_two = norm_back(middle_grad)
    attn_out16 = lax.all_gather(attn_sum_grad.astype(jnp.bfloat16), "tensor", axis=1, tiled=True)
    grad_out = outer_sum(attended16, attn_out16)
    attended_grad16 = matmul_back(attn_out16, w_out).astype(jnp.bfloat16)
    attended_grad16 = attended_grad16.reshape(row_count, slot_count, local_heads, HEAD_DIM)
    query_grad, key_grad, value_grad = lax.map(
        attend_row_back, (queries, keys_all, values_all, attended_grad16, log_totals, lengths)
    )
    projected_grad16 = jnp.stack([query_grad, key_grad, value_grad], axis=2).astype(jnp.bfloat16)
    projected_grad16 = projected_grad16.reshape(row_count, slot_count, 3 * local_cols)
    grad_qkv = outer_sum(attn_rows_again, projected_grad16).reshape(model_width, 3, local_cols)
    attn_in_grad = lax.psum_scatter(
        matmul_back(projected_grad16, w_qkv_flat), "tensor", scatter_dimension=1, tiled=True
    )
    _, norm_back = jax.vjp(layer_norm, inputs_share, gains[0], biases[0])
    input_part, gain_one, bias_one = norm_back(attn_in_grad)
    input_grad = (middle_grad + input_part).astype(jnp.bfloat16)
    grad_gains = jnp.stack([gain_one, gain_two, gain_three, gain_four])
    grad_biases = jnp.stack([bias_one, bias_two, bias_three, bias_four])
    grad_qkv, grad_out, grad_up, grad_down = lax.psum(
        (grad_qkv, grad_out, grad_up, grad_down), "dp"
    )
    grad_gains, grad_biases = lax.psum((grad_gains, grad_biases), ("dp", "tensor"))
    group_rms = jnp.sqrt(group_sums / (group_counts[:, None] * model_width))
    return (
        result.astype(jnp.bfloat16),
        input_grad,
        grad_qkv,
        grad_out,
        grad_up,
        grad_down,
        grad_gains,
        grad_biases,
        group_rms,
    )


def solution(mesh):
    placed = (
        P("dp", "tensor", None),
        P("dp", "tensor", None),
        P("dp"),
        P("dp"),
        P(None, None, "tensor"),
        P("tensor", None),
        P(None, "tensor"),
        P("tensor", None),
        P(),
        P(),
    )
    return jax.shard_map(
        per_device,
        mesh=mesh,
        in_specs=placed,
        out_specs=(
            P("dp", "tensor", None),
            P("dp", "tensor", None),
            P(None, None, "tensor"),
            P("tensor", None),
            P(None, "tensor"),
            P("tensor", None),
            P(),
            P(),
            P(),
        ),
        check_vma=False,
    )
```

profile of v0, /device:TPU:0, one launch (start us, length us, event | category | flops | bytes accessed | tf_op | source)
XLA Modules:
  0.0 1234.8 jit_solution(14047546590717724627)
XLA Ops:
  16.6 36.1 %all-gather.5.cloned.1.call-done = bf16[2,1088,1024]{2,1,0:T(8,128)(2,1)} async-done(((bf16[2,272,1024]{2,1,0:T(8,128)(2,1)}), bf16[2,1088,1024]{2,1,0:T(8,128)(2,1)}) %all-gather.5.cloned.1.call-update) | async-done | bytes 4456464 | tf_op jit(solution)/shard_map/all_gather | solution.py:123
  52.8 8.2 convolution_convert_fusion
  70.4 77.7 %while.57 = (s32[]{:T(128)}, bf16[2,1088,4,64]{3,2,1,0:T(4,128)(2,1)}, f32[2,2,4,544]{3,2,1,0:T(4,128)S(1)}, bf16[2,1088,4,64]{1,3,2,0:T(8,128)(2,1)}, bf16[2,10...) while((s32[]{:T(128)}, ...), condition=%wide.region_7.8_spmd, body=%wide.region_2.7_spmd.sunk | while | flops 640407168 | bytes 48634288 | solution.py:130
  77.4 29.2 %while.60 = (s32[]{:T(128)}, bf16[2,544,4,64]{1,3,2,0:T(8,128)(2,1)}, f32[2,4,544]{2,1,0:T(4,128)S(1)}, s32[2]{0:T(128)S(1)}, s32[]{:T(128)}, /*index=5*/bf16[2,...) while((s32[]{:T(128)}, ...), condition=%wide.region_6.6_spmd.clone.clone, body=%wide.region_3.5_spmd.clone.clone.sunk | while | flops 640407168 | bytes 40237216 | solution.py:66
  116.0 29.2 %while.60 = (s32[]{:T(128)}, bf16[2,544,4,64]{1,3,2,0:T(8,128)(2,1)}, f32[2,4,544]{2,1,0:T(4,128)S(1)}, s32[2]{0:T(128)S(1)}, s32[]{:T(128)}, /*index=5*/bf16[2,...) while((s32[]{:T(128)}, ...), condition=%wide.region_6.6_spmd.clone.clone, body=%wide.region_3.5_spmd.clone.clone.sunk | while | flops 640407168 | bytes 40237216 | solution.py:66
  158.3 75.0 %reduce-scatter.5.cloned.1.call-done = f32[2,272,1024]{2,1,0:T(8,128)} async-done(((f32[2,1088,1024]{2,1,0:T(8,128)}), f32[2,272,1024]{2,1,0:T(8,128)}) %reduce-scatter.5.cloned.1.call-update) | async-done | bytes 2228240 | tf_op jit(solution)/shard_map/reduce_scatter | solution.py:132
  241.0 36.1 %all-gather.7.cloned.1.call-done = bf16[2,1088,1024]{2,1,0:T(8,128)(2,1)} async-done(((bf16[2,272,1024]{2,1,0:T(8,128)(2,1)}), bf16[2,1088,1024]{2,1,0:T(8,128)(2,1)}) %all-gather.7.cloned.1.call-update) | async-done | bytes 4456464 | tf_op jit(solution)/shard_map/all_gather | solution.py:138
  277.1 7.3 fusion.70
  287.7 7.8 fusion.66
  295.7 75.1 %reduce-scatter.7.cloned.1.call-done = f32[2,272,1024]{2,1,0:T(8,128)} async-done(((f32[2,1088,1024]{2,1,0:T(8,128)}), f32[2,272,1024]{2,1,0:T(8,128)}) %reduce-scatter.7.cloned.1.call-update) | async-done | bytes 2228240 | tf_op jit(solution)/shard_map/reduce_scatter | solution.py:141
  381.8 35.9 %all-gather.9.cloned.1.call-done = bf16[2,1088,1024]{2,1,0:T(8,128)(2,1)} async-done(((bf16[2,272,1024]{2,1,0:T(8,128)(2,1)}), bf16[2,1088,1024]{2,1,0:T(8,128)(2,1)}) %all-gather.9.cloned.1.call-update) | async-done | bytes 4456464 | tf_op jit(solution)/shard_map/all_gather | solution.py:174
  417.7 12.9 %fusion.49 = bf16[2,1088,1024]{2,1,0:T(8,128)(2,1)S(1)} fusion(f32[2,1088,1024]{2,1,0:T(8,128)} %copy-done.65, bf16[2,1088,1024]{2,1,0:T(8,128)(2,1)} %all-gather.9.cloned.1.call-done, bf16[1024,1024]{1,0:T(8,128)(2,1)S(1)} %copy-done), kind=kOutput, calls=%fused_computation.74 | convolution fusion | flops 4607967232 | bytes 19922944 | tf_op jit(solution)/shard_map/rsf,df->rsd/dot_general | solution.py:31
  432.6 7.1 fusion.68
  439.8 75.2 %reduce-scatter.9.cloned.1.call-done = f32[2,272,1024]{2,1,0:T(8,128)} async-done(((f32[2,1088,1024]{2,1,0:T(8,128)}), f32[2,272,1024]{2,1,0:T(8,128)}) %reduce-scatter.9.cloned.1.call-update) | async-done | bytes 2228240 | tf_op jit(solution)/shard_map/reduce_scatter | solution.py:180
  529.0 36.1 %all-gather.11.cloned.1.call-done = bf16[2,1088,1024]{2,1,0:T(8,128)(2,1)} async-done(((bf16[2,272,1024]{2,1,0:T(8,128)(2,1)}), bf16[2,1088,1024]{2,1,0:T(8,128)(2,1)}) %all-gather.11.cloned.1.call-update) | async-done | bytes 4456464 | tf_op jit(solution)/shard_map/all_gather | solution.py:188
  570.5 153.8 %while.59 = (s32[]{:T(128)}, bf16[2,1088,4,64]{1,3,2,0:T(8,128)(2,1)}, bf16[2,1088,4,64]{1,3,2,0:T(8,128)(2,1)}, bf16[2,1088,4,64]{1,3,2,0:T(8,128)(2,1)}, bf16[...) while((s32[]{:T(128)}, ...), condition=%wide.region_27.28_spmd, body=%wide.region_23.27_spmd.sunk | while | flops 1543949824 | bytes 172993712 | solution.py:192
  576.9 63.6 %while.61 = (s32[]{:T(128)}, f32[1088,4,64]{0,2,1:T(8,128)S(1)}, f32[1088,4,64]{0,2,1:T(8,128)}, bf16[2,544,4,64]{1,3,2,0:T(8,128)(2,1)}, s32[2]{0:T(128)S(1)}, ...) while((s32[]{:T(128)}, f32[1088,4,64]{0,2,1:T(8,128)S(1)}, ...), condition=%wide.region_26.26_spmd.clone.clone, body=%wide.region_24.25_spmd.clone.clone.sunk | while | flops 1543949824 | bytes 147301168 | solution.py:108
  582.6 6.8 multiply_reduce_fusion.14
  589.4 10.1 multiply_convert_fusion.5
  614.3 6.8 multiply_reduce_fusion.14
  621.1 10.1 multiply_convert_fusion.5
  653.8 63.6 %while.61 = (s32[]{:T(128)}, f32[1088,4,64]{0,2,1:T(8,128)S(1)}, f32[1088,4,64]{0,2,1:T(8,128)}, bf16[2,544,4,64]{1,3,2,0:T(8,128)(2,1)}, s32[2]{0:T(128)S(1)}, ...) while((s32[]{:T(128)}, f32[1088,4,64]{0,2,1:T(8,128)S(1)}, ...), condition=%wide.region_26.26_spmd.clone.clone, body=%wide.region_24.25_spmd.clone.clone.sunk | while | flops 1543949824 | bytes 147301168 | solution.py:108
  659.5 6.8 multiply_reduce_fusion.14
  666.3 10.1 multiply_convert_fusion.5
  691.2 6.8 multiply_reduce_fusion.14
  698.0 10.1 multiply_convert_fusion.5
  708.1 6.4 fusion.165
  735.3 9.9 convolution_bitcast_fusion.1
  745.2 12.5 %convolution_bitcast_fusion = f32[1024,1024]{1,0:T(8,128)} fusion(bf16[2,1088,1024]{2,1,0:T(8,128)(2,1)} %all-gather.9.cloned.1.call-done, f32[2,1088,1024]{2,1,0:T(8,128)} %copy-done.65), kind=kOutput, calls=%fused_computation.121 | convolution fusion | flops 4583456768 | bytes 17563648 | tf_op jit(solution)/shard_map/rsd,rsf->df/dot_general | solution.py:35
  767.0 43.5 %reduce-scatter.11.cloned.1.call-done = f32[2,272,1024]{2,1,0:T(8,128)} async-done(((f32[2,1088,1024]{2,1,0:T(8,128)}), f32[2,272,1024]{2,1,0:T(8,128)}) %reduce-scatter.11.cloned.1.call-update) | async-done | bytes 2228240 | tf_op jit(solution)/shard_map/reduce_scatter | solution.py:198
  814.2 42.8 %all-reduce = (f32[4,1024]{1,0:T(4,128)}, f32[4,1024]{1,0:T(4,128)}, f32[4,3]{0,1:T(4,128)S(1)}, f32[4]{0:T(128)S(1)}) all-reduce(f32[4,1024]{1,0:T(4,128)S(1)} %pad_maximum_fusion, f32[4,1024]{1,0:T(4,128)S(1)} %pad_maximum_fusion.1, f32[4,3]{0,1:T(4,128)S(1)} %fusion.87, ...), channel_id=1, replica_groups=mesh['dp'=8,'tensor'=4] {'dp','tensor'}, use_global_device_ids=true, to_apply=%region_39.40 | all-reduce | flops 8208 | bytes 65664 | tf_op jit(solution)/shard_map/psum | solution.py:209
  861.7 355.7 %all-reduce.4.cloned.1.call-done = (f32[1024,3,256]{2,0,1:T(8,128)}, f32[256,1024]{1,0:T(8,128)}, f32[1024,1024]{1,0:T(8,128)}, f32[1024,1024]{1,0:T(8,128)}) async-done(((f32[1024,3,256]{2,0,1:T(8,128)}, f32[256,1024]{1,0:T(8,128)}, f32[1024,1024]{1,0:T(8,128)}, f32[1024,1024]{1,0:T(8,128)}), (f32[1024,3,256]{2,0,1:T(8,128)}, f32[256,1024]{1,0:T(8,128)}, f32[1024,1024]{1,0:T(8,128)}, ...) | async-done | bytes 12582928 | tf_op jit(solution)/shard_map/psum | solution.py:206
  (410 shorter events, 246.7 us)
Async XLA Ops:
  7.2 280.5 %copy-start = (bf16[1024,1024]{1,0:T(8,128)(2,1)S(1)}, bf16[1024,1024]{1,0:T(8,128)(2,1)}, u32[]{:S(2)}) copy-start(bf16[1024,1024]{1,0:T(8,128)(2,1)} %param.25) | copy-start | bytes 6291460
  7.2 45.6 %all-gather.5.cloned.1.call-start = ((), (), s32[]{:S(2)}) async-start(), calls=%async_computation.4 | async-start | bytes 5570560 | tf_op jit(solution)/shard_map/all_gather | solution.py:123
  14.0 219.3 %reduce-scatter.5.cloned.1.call-start = ((), (), s32[]{:S(2)}) async-start(), calls=%async_computation.5 | async-start | bytes 11141120 | tf_op jit(solution)/shard_map/reduce_scatter | solution.py:132
  158.0 79.3 %copy-start.13 = (bf16[2,272,1024]{2,1,0:T(8,128)(2,1)S(1)}, bf16[2,272,1024]{2,1,0:T(8,128)(2,1)}, u32[]{:S(2)}) copy-start(bf16[2,272,1024]{2,1,0:T(8,128)(2,1)} %param.18) | copy-start | bytes 3342340
  158.0 79.3 %copy-start.40 = (f32[1,1024]{1,0:T(1,128)S(1)}, f32[1,1024]{1,0:T(1,128)}, u32[]{:S(2)}) copy-start(f32[1,1024]{1,0:T(1,128)} %get-tuple-element.509) | copy-start | bytes 12292
  158.0 79.3 %copy-start.44 = (f32[1,1024]{1,0:T(1,128)S(1)}, f32[1,1024]{1,0:T(1,128)}, u32[]{:S(2)}) copy-start(f32[1,1024]{1,0:T(1,128)} %get-tuple-element.513) | copy-start | bytes 12292
  158.0 119.0 %all-gather.7.cloned.1.call-start = ((), (), s32[]{:S(2)}) async-start(), calls=%async_computation.6 | async-start | bytes 5570560 | tf_op jit(solution)/shard_map/all_gather | solution.py:138
  241.0 129.8 %reduce-scatter.7.cloned.1.call-start = ((), (), s32[]{:S(2)}) async-start(), calls=%async_computation.7 | async-start | bytes 11141120 | tf_op jit(solution)/shard_map/reduce_scatter | solution.py:141
  295.5 77.1 %copy-start.19 = (bf16[2,272,1024]{2,1,0:T(8,128)(2,1)S(1)}, bf16[2,272,1024]{2,1,0:T(8,128)(2,1)}, u32[]{:S(2)}) copy-start(bf16[2,272,1024]{2,1,0:T(8,128)(2,1)} %param.19) | copy-start | bytes 3342340
  295.5 77.1 %copy-start.41 = (f32[1,1024]{1,0:T(1,128)S(1)}, f32[1,1024]{1,0:T(1,128)}, u32[]{:S(2)}) copy-start(f32[1,1024]{1,0:T(1,128)} %get-tuple-element.511) | copy-start | bytes 12292
  295.5 122.2 %all-gather.9.cloned.1.call-start = ((), (), s32[]{:S(2)}) async-start(), calls=%async_computation.8 | async-start | bytes 5570560 | tf_op jit(solution)/shard_map/all_gather | solution.py:174
  381.6 133.5 %reduce-scatter.9.cloned.1.call-start = ((), (), s32[]{:S(2)}) async-start(), calls=%async_computation.9 | async-start | bytes 11141120 | tf_op jit(solution)/shard_map/reduce_scatter | solution.py:180
  417.7 15.0 %copy-start.62 = (bf16[1024,1024]{1,0:T(8,128)(2,1)S(1)}, bf16[1024,1024]{1,0:T(8,128)(2,1)}, u32[]{:S(2)}) copy-start(bf16[1024,1024]{1,0:T(8,128)(2,1)} %param.24) | copy-start | bytes 6291460
  439.8 125.2 %all-gather.11.cloned.1.call-start = ((), (), s32[]{:S(2)}) async-start(), calls=%async_computation.10 | async-start | bytes 5570560 | tf_op jit(solution)/shard_map/all_gather | solution.py:188
  527.3 37.8 %copy-start.34 = (bf16[256,1024]{1,0:T(8,128)(2,1)S(1)}, bf16[256,1024]{1,0:T(8,128)(2,1)}, u32[]{:S(2)}) copy-start(bf16[256,1024]{1,0:T(8,128)(2,1)} %param.23) | copy-start | bytes 1572868
  528.9 281.6 %reduce-scatter.11.cloned.1.call-start = ((), (), s32[]{:S(2)}) async-start(), calls=%async_computation.11 | async-start | bytes 11141120 | tf_op jit(solution)/shard_map/reduce_scatter | solution.py:198
  614.3 6.8 copy-start.2
  659.5 6.8 copy-start.2
  735.3 482.2 %all-reduce.4.cloned.1.call-start = ((), (), s32[]{:S(2)}) async-start(), calls=%async_computation.12 | async-start | bytes 25165824 | tf_op jit(solution)/shard_map/psum | solution.py:206
  735.3 22.4 %slice-start.2 = ((s8[4456448]{0:T(1024)(128)(4,1)}), s8[4194304]{0:T(1024)(128)(4,1)S(1)}, s32[]{:S(2)}) async-start(s8[4456448]{0:T(1024)(128)(4,1)} %bitcast.278), calls=%async_computation.15 | async-start | bytes 8388608
  735.3 24.8 %slice-start = ((s8[4456448]{0:T(1024)(128)(4,1)}), s8[4194304]{0:T(1024)(128)(4,1)S(1)}, s32[]{:S(2)}) async-start(s8[4456448]{0:T(1024)(128)(4,1)} %bitcast.276), calls=%async_computation.13 | async-start | bytes 8388608
  745.2 12.5 %copy-start.29 = (bf16[2,1088,4,64]{1,3,2,0:T(8,128)(2,1)S(1)}, bf16[2,1088,4,64]{1,3,2,0:T(8,128)(2,1)}, u32[]{:S(2)}) copy-start(bf16[2,1088,4,64]{1,3,2,0:T(8,128)(2,1)} %copy-done.28) | copy-start | bytes 3342340
  745.2 12.5 %slice-start.3 = ((s8[4456448]{0:T(1024)(128)(4,1)}), s8[262144]{0:T(1024)(128)(4,1)S(1)}, s32[]{:S(2)}) async-start(s8[4456448]{0:T(1024)(128)(4,1)} %bitcast.278), calls=%async_computation.16 | async-start | bytes 524288
  745.2 15.0 %slice-start.1 = ((s8[4456448]{0:T(1024)(128)(4,1)}), s8[262144]{0:T(1024)(128)(4,1)S(1)}, s32[]{:S(2)}) async-start(s8[4456448]{0:T(1024)(128)(4,1)} %bitcast.276), calls=%async_computation.14 | async-start | bytes 524288
  766.0 44.5 %copy-start.14 = (bf16[2,272,1024]{2,1,0:T(8,128)(2,1)S(1)}, bf16[2,272,1024]{2,1,0:T(8,128)(2,1)}, u32[]{:S(2)}) copy-start(bf16[2,272,1024]{2,1,0:T(8,128)(2,1)} %param.18) | copy-start | bytes 3342340
  766.0 44.5 %copy-start.36 = (f32[2,272]{1,0:T(2,128)S(1)}, f32[2,272]{1,0:T(2,128)}, u32[]{:S(2)}) copy-start(f32[2,272]{1,0:T(2,128)} %copy-done.35) | copy-start | bytes 6532
  766.0 44.5 %copy-start.38 = (f32[1,1024]{1,0:T(1,128)S(1)}, f32[1,1024]{1,0:T(1,128)}, u32[]{:S(2)}) copy-start(f32[1,1024]{1,0:T(1,128)} %copy-done.37) | copy-start | bytes 12292
  766.0 46.8 %copy-start.48 = (f32[1024]{0:T(1024)S(1)}, f32[1024]{0:T(1024)}, u32[]{:S(2)}) copy-start(f32[1024]{0:T(1024)} %get-tuple-element.408) | copy-start | bytes 12292
  766.1 46.8 %copy-start.50 = (f32[1024]{0:T(1024)S(1)}, f32[1024]{0:T(1024)}, u32[]{:S(2)}) copy-start(f32[1024]{0:T(1024)} %get-tuple-element.406) | copy-start | bytes 12292
  766.1 46.8 %copy-start.51 = (f32[1024]{0:T(1024)S(1)}, f32[1024]{0:T(1024)}, u32[]{:S(2)}) copy-start(f32[1024]{0:T(1024)} %get-tuple-element.404) | copy-start | bytes 12292
  766.1 46.9 %copy-start.46 = (f32[2,272]{1,0:T(2,128)S(1)}, f32[2,272]{1,0:T(2,128)}, u32[]{:S(2)}) copy-start(f32[2,272]{1,0:T(2,128)} %copy-done.45) | copy-start | bytes 6532
  766.1 46.9 %copy-start.43 = (f32[2,272]{1,0:T(2,128)S(1)}, f32[2,272]{1,0:T(2,128)}, u32[]{:S(2)}) copy-start(f32[2,272]{1,0:T(2,128)} %copy-done.42) | copy-start | bytes 6532
  (76 other events, 228.5 us)
Sparse Core Ops, SparseCore 0:
  14.1 38.6 all-gather.4
  158.1 75.0 reduce-scatter.4
  241.1 35.9 all-gather.6
  295.6 75.0 reduce-scatter.6
  381.7 35.9 all-gather.8
  439.9 75.0 reduce-scatter.8
  529.0 35.9 all-gather.10
  735.4 75.0 reduce-scatter.10
  815.8 401.5 all-reduce.3
where the time goes:
time: 1240 us; the launch traced here: 1230 us
  waiting for transfers between devices  769 us (62%)
  matrix products  183 us (15%)
  other arithmetic  108 us (9%)
  local copies, waits for them, and re-layouts  94.3 us (8%)
  blocking collectives  42.8 us (3%)
  loops' own time  22.4 us (2%)
  between operations  14.7 us (1%)
    psum x1, waiting for transfers between devices, per_device(): lax.psum((grad_qkv, grad_out, grad_up, grad_down), 'dp')  356 us
    reduce_scatter x1, waiting for transfers between devices, per_device(): lax.psum_scatter(matmul_back(hidden_grad16, w_up), 'tensor', scatter_dime...  75.2 us
    reduce_scatter x1, waiting for transfers between devices, per_device(): lax.psum_scatter(matmul_rows(activated16, w_down), 'tensor', scatter_dime...  75.1 us
    reduce_scatter x1, waiting for transfers between devices, per_device(): lax.psum_scatter(matmul_rows(attended16, w_out), 'tensor', scatter_dimens...  75 us
    reduce_scatter x1, waiting for transfers between devices, per_device(): lax.psum_scatter(matmul_back(projected_grad16, w_qkv_flat), 'tensor', sca...  43.5 us
    psum x1, blocking collectives, per_device(): lax.psum((grad_gains, grad_biases), ('dp', 'tensor'))  42.8 us
    convert_element_type x4, other arithmetic, one_block(): (relax_alpha * probs * (probs_grad - inner)).astype(jnp.bfloat16)  40.5 us
    dot_general x8, matrix products, masked_scores(): jnp.einsum('qhd,khd->hqk', query_block, key_row, preferred_element_type=j...  36.4 us
  transfers between devices with their start and end apart: 9, of which 9 were waited for; matrix products, arithmetic and copies ran while one was open for 3% of the time, Pallas kernels for 0%

commit v1 on v0

v1 whole, which is shorter than its diff:
```python
import functools

import jax
import jax.numpy as jnp
from jax import lax
from jax.experimental import pallas as pl
from jax.experimental.pallas import tpu as pltpu
from jax.sharding import PartitionSpec as P

HEAD_DIM = 64
GROUPS = 4
MIN_LENGTH = 544
F32 = jnp.float32
B16 = jnp.bfloat16

epsilon = 1e-05
negative_fill = -1e30
log2_e = 1.4426950408889634
gelu_scale = 0.7978845608028654
gelu_cubic = 0.044715


def nt(left, right):
    return lax.dot_general(
        left, right, (((1,), (1,)), ((), ())), preferred_element_type=F32
    )


def nn(left, right):
    return lax.dot_general(
        left, right, (((1,), (0,)), ((), ())), preferred_element_type=F32
    )


def tn(left, right):
    return lax.dot_general(
        left, right, (((0,), (0,)), ((), ())), preferred_element_type=F32
    )


def tiles(extent, size):
    return [(start, min(size, extent - start)) for start in range(0, extent, size)]


def lane_half(shape, half):
    return (lax.broadcasted_iota(jnp.int32, shape, 1) // HEAD_DIM) == half


def mask_tile(scores, key_start, query_start, length):
    key_count, query_count = scores.shape
    key_index = key_start + lax.broadcasted_iota(jnp.int32, scores.shape, 0)
    allowed = None
    if key_start + key_count - 1 > query_start:
        query_index = query_start + lax.broadcasted_iota(jnp.int32, scores.shape, 1)
        allowed = key_index <= query_index
    if key_start + key_count > MIN_LENGTH:
        inside = key_index < length
        allowed = inside if allowed is None else allowed & inside
    return scores if allowed is None else jnp.where(allowed, scores, negative_fill)


def attend_kernel(slots, chunk, parts, query_tile, key_tile, meta, *refs):
    inputs = refs[:parts]
    outputs = refs[parts : 2 * parts]
    lse_ref = refs[2 * parts]
    q_ref, k_ref, vt_ref, s_ref, p_ref, ot_ref = refs[2 * parts + 1 :]
    half = pl.program_id(0) % 2
    length = meta[0]
    per = inputs[0].shape[0] // chunk

    @pl.when(half == 0)
    def _():
        for part, source in enumerate(inputs):
            for piece in range(per):
                place = pl.multiple_of(meta[1 + part * per + piece], 16)
                rows = pl.ds(piece * chunk, chunk)
                q_ref[pl.ds(place, chunk), :] = source[rows, 0:128]
                k_ref[pl.ds(place, chunk), :] = source[rows, 128:256]
                p_ref[pl.ds(place, chunk), 0:128] = source[rows, 256:384]
        vt_ref[...] = p_ref[0:slots, 0:128].T

    scale = log2_e / HEAD_DIM**0.5
    base = pl.multiple_of(half * HEAD_DIM, HEAD_DIM)
    for q0, qn in tiles(slots, query_tile):
        query = q_ref[q0 : q0 + qn, :]
        query = jnp.where(lane_half(query.shape, half), query, jnp.zeros_like(query))
        extent = q0 + qn
        top = jnp.full((1, qn), negative_fill, F32)
        for k0, kn in tiles(extent, key_tile):
            scores = mask_tile(nt(k_ref[k0 : k0 + kn, :], query), k0, q0, length)
            s_ref[k0 : k0 + kn, 0:qn] = scores
            top = jnp.maximum(top, jnp.max(scores, axis=0, keepdims=True))
        total = jnp.zeros((1, qn), F32)
        for k0, kn in tiles(extent, key_tile):
            weights = jnp.exp2((s_ref[k0 : k0 + kn, 0:qn] - top) * scale)
            total = total + jnp.sum(weights, axis=0, keepdims=True)
            p_ref[k0 : k0 + kn, 0:qn] = weights.astype(B16)
        out_t = nn(vt_ref[pl.ds(base, HEAD_DIM), 0:extent], p_ref[0:extent, 0:qn])
        ot_ref[pl.ds(base, HEAD_DIM), q0 : q0 + qn] = out_t * (1.0 / total)
        lse_ref[0, :, q0 : q0 + qn] = top * scale + jnp.log2(total)

    @pl.when(half == 1)
    def _():
        q_ref[...] = ot_ref[...].T.astype(B16)
        for part, target in enumerate(outputs):
            for piece in range(per):
                place = pl.multiple_of(meta[1 + part * per + piece], 16)
                target[pl.ds(piece * chunk, chunk), :] = q_ref[pl.ds(place, chunk), :]


def attend(meta, projected, chunk):
    parts = len(projected)
    rows, width = projected[0].shape
    pairs = width // 384
    slots, heads = rows * parts, 2 * pairs
    return pl.pallas_call(
        functools.partial(attend_kernel, slots, chunk, parts, 256, 128),
        out_shape=[jax.ShapeDtypeStruct((rows, pairs * 128), B16)] * parts
        + [jax.ShapeDtypeStruct((heads, 1, slots), F32)],
        grid_spec=pltpu.PrefetchScalarGridSpec(
            num_scalar_prefetch=1,
            grid=(heads,),
            in_specs=[pl.BlockSpec((rows, 384), lambda h, m: (0, h // 2))] * parts,
            out_specs=[pl.BlockSpec((rows, 128), lambda h, m: (0, h // 2))] * parts
            + [pl.BlockSpec((1, 1, slots), lambda h, m: (h, 0, 0))],
            scratch_shapes=[
                pltpu.VMEM((slots, 128), B16),
                pltpu.VMEM((slots, 128), B16),
                pltpu.VMEM((128, slots), B16),
                pltpu.VMEM((slots, 256), F32),
                pltpu.VMEM((slots, 256), B16),
                pltpu.VMEM((128, slots), F32),
            ],
        ),
        compiler_params=pltpu.CompilerParams(
            dimension_semantics=("arbitrary",), vmem_limit_bytes=24 << 20
        ),
        cost_estimate=pl.CostEstimate(
            flops=heads * slots * slots * HEAD_DIM * 16,
            bytes_accessed=slots * pairs * 1024,
            transcendentals=heads * slots * slots // 2,
        ),
        name="attend",
    )(meta, *projected)


def attend_back_kernel(slots, chunk, parts, query_tile, key_tile, meta, *refs):
    inputs = refs[:parts]
    attended = refs[parts : 2 * parts]
    grads = refs[2 * parts : 3 * parts]
    lse_ref = refs[3 * parts]
    outputs = refs[3 * parts + 1 : 4 * parts + 1]
    q_ref, k_ref, v_ref, g_ref, kt_ref, inner_ref, dk_ref, dv_ref, dqt_ref, t_ref = refs[
        4 * parts + 1 :
    ]
    half = pl.program_id(0) % 2
    length = meta[0]
    per = inputs[0].shape[0] // chunk

    @pl.when(half == 0)
    def _():
        for part, source in enumerate(inputs):
            for piece in range(per):
                place = pl.multiple_of(meta[1 + part * per + piece], 16)
                rows, target = pl.ds(piece * chunk, chunk), pl.ds(place, chunk)
                q_ref[target, :] = source[rows, 0:128]
                k_ref[target, :] = source[rows, 128:256]
                v_ref[target, :] = source[rows, 256:384]
                g_ref[target, :] = grads[part][rows, :]
                t_ref[target, :] = attended[part][rows, :].astype(F32) * grads[part][
                    rows, :
                ].astype(F32)
        kt_ref[...] = k_ref[...].T
        products = t_ref[...].T
        inner_ref[0:1, :] = jnp.sum(products[0:HEAD_DIM], axis=0, keepdims=True)
        inner_ref[1:2, :] = jnp.sum(products[HEAD_DIM:], axis=0, keepdims=True)
        dk_ref[...] = jnp.zeros_like(dk_ref)
        dv_ref[...] = jnp.zeros_like(dv_ref)

    scale = log2_e / HEAD_DIM**0.5
    base = pl.multiple_of(half * HEAD_DIM, HEAD_DIM)
    for q0, qn in tiles(slots, query_tile):
        keep = lane_half((qn, 128), half)
        query = q_ref[q0 : q0 + qn, :]
        query = jnp.where(keep, query, jnp.zeros_like(query))
        grad = g_ref[q0 : q0 + qn, :]
        grad = jnp.where(keep, grad, jnp.zeros_like(grad))
        lse = lse_ref[0, :, q0 : q0 + qn]
        inner = jnp.where(
            half == 0, inner_ref[0:1, q0 : q0 + qn], inner_ref[1:2, q0 : q0 + qn]
        )
        dq_t = jnp.zeros((HEAD_DIM, qn), F32)
        for k0, kn in tiles(q0 + qn, key_tile):
            scores = mask_tile(nt(k_ref[k0 : k0 + kn, :], query), k0, q0, length)
            probs = jnp.exp2(scores * scale - lse)
            dv_ref[k0 : k0 + kn, :] += nn(probs.astype(B16), grad)
            probs_grad = nt(v_ref[k0 : k0 + kn, :], grad)
            scores_grad = (probs * (probs_grad - inner)).astype(B16)
            dk_ref[k0 : k0 + kn, :] += nn(scores_grad, query)
            dq_t = dq_t + nn(kt_ref[pl.ds(base, HEAD_DIM), k0 : k0 + kn], scores_grad)
        dqt_ref[pl.ds(base, HEAD_DIM), q0 : q0 + qn] = dq_t

    @pl.when(half == 1)
    def _():
        factor = 1.0 / HEAD_DIM**0.5
        q_ref[...] = (dqt_ref[...].T * factor).astype(B16)
        k_ref[...] = (dk_ref[...] * factor).astype(B16)
        v_ref[...] = dv_ref[...].astype(B16)
        for part, target in enumerate(outputs):
            for piece in range(per):
                place = pl.multiple_of(meta[1 + part * per + piece], 16)
                rows, source = pl.ds(piece * chunk, chunk), pl.ds(place, chunk)
                target[rows, 0:128] = q_ref[source, :]
                target[rows, 128:256] = k_ref[source, :]
                target[rows, 256:384] = v_ref[source, :]


def attend_back(meta, projected, attended, grads, lse, chunk):
    parts = len(projected)
    rows, width = projected[0].shape
    pairs = width // 384
    slots, heads = rows * parts, 2 * pairs
    wide = pl.BlockSpec((rows, 384), lambda h, m: (0, h // 2))
    narrow = pl.BlockSpec((rows, 128), lambda h, m: (0, h // 2))
    return pl.pallas_call(
        functools.partial(attend_back_kernel, slots, chunk, parts, 256, 128),
        out_shape=[jax.ShapeDtypeStruct((rows, width), B16)] * parts,
        grid_spec=pltpu.PrefetchScalarGridSpec(
            num_scalar_prefetch=1,
            grid=(heads,),
            in_specs=[wide] * parts
            + [narrow] * (2 * parts)
            + [pl.BlockSpec((1, 1, slots), lambda h, m: (h, 0, 0))],
            out_specs=[wide] * parts,
            scratch_shapes=[pltpu.VMEM((slots, 128), B16)] * 4
            + [
                pltpu.VMEM((128, slots), B16),
                pltpu.VMEM((8, slots), F32),
                pltpu.VMEM((slots, 128), F32),
                pltpu.VMEM((slots, 128), F32),
                pltpu.VMEM((128, slots), F32),
                pltpu.VMEM((slots, 128), F32),
            ],
        ),
        compiler_params=pltpu.CompilerParams(
            dimension_semantics=("arbitrary",), vmem_limit_bytes=24 << 20
        ),
        cost_estimate=pl.CostEstimate(
            flops=heads * slots * slots * HEAD_DIM * 32,
            bytes_accessed=slots * pairs * 2560,
            transcendentals=heads * slots * slots // 2,
        ),
        name="attend_back",
    )(meta, *projected, *attended, *grads, lse)


def up_kernel(x_ref, w_ref, act_ref, slope_ref):
    hidden = nn(x_ref[...], w_ref[...])
    square = hidden * hidden
    bent = jnp.tanh(gelu_scale * hidden * (1.0 + gelu_cubic * square))
    upper = 0.5 * (1.0 + bent)
    act_ref[...] = (hidden * upper).astype(B16)
    slope = upper + (0.5 * gelu_scale) * hidden * (1.0 - bent * bent) * (
        1.0 + (3.0 * gelu_cubic) * square
    )
    slope_ref[...] = slope.astype(B16)


def up_project(x, w):
    rows, depth = x.shape
    width = w.shape[1]
    step = min(256, width)
    return pl.pallas_call(
        up_kernel,
        out_shape=[jax.ShapeDtypeStruct((rows, width), B16)] * 2,
        grid=(width // step,),
        in_specs=[
            pl.BlockSpec((rows, depth), lambda i: (0, 0)),
            pl.BlockSpec((depth, step), lambda i: (0, i)),
        ],
        out_specs=[pl.BlockSpec((rows, step), lambda i: (0, i))] * 2,
        compiler_params=pltpu.CompilerParams(vmem_limit_bytes=24 << 20),
        cost_estimate=pl.CostEstimate(
            flops=2 * rows * depth * width * 2,
            bytes_accessed=2 * (rows * depth + depth * width + 2 * rows * width),
            transcendentals=rows * width,
        ),
        name="up_project",
    )(x, w)


def outer_kernel(count, *refs):
    total = None
    for left, right in zip(refs[:count], refs[count : 2 * count]):
        term = tn(left[...], right[...])
        total = term if total is None else total + term
    refs[2 * count][...] = total.astype(B16)


def outer_sum(lefts, rights):
    count = len(lefts)
    rows, height = lefts[0].shape
    width = rights[0].shape[1]
    step = min(256, height)
    return pl.pallas_call(
        functools.partial(outer_kernel, count),
        out_shape=jax.ShapeDtypeStruct((height, width), B16),
        grid=(height // step,),
        in_specs=[pl.BlockSpec((rows, step), lambda i: (0, i))] * count
        + [pl.BlockSpec((rows, width), lambda i: (0, 0))] * count,
        out_specs=pl.BlockSpec((step, width), lambda i: (i, 0)),
        compiler_params=pltpu.CompilerParams(vmem_limit_bytes=32 << 20),
        cost_estimate=pl.CostEstimate(
            flops=2 * count * rows * height * width * 2,
            bytes_accessed=2 * (count * rows * (height + width) + height * width),
            transcendentals=0,
        ),
        name="outer_sum",
    )(*lefts, *rights)


def place_kernel(order, *refs):
    pieces, out_ref = refs[:-1], refs[-1]
    which = order[pl.program_id(0)]
    for index, piece in enumerate(pieces):

        @pl.when(which == index)
        def _(piece=piece):
            out_ref[...] = piece[...].astype(F32)


def place(order, pieces):
    count = len(pieces)
    rows, width = pieces[0].shape
    return pl.pallas_call(
        place_kernel,
        out_shape=jax.ShapeDtypeStruct((count * rows, width), F32),
        grid_spec=pltpu.PrefetchScalarGridSpec(
            num_scalar_prefetch=1,
            grid=(count,),
            in_specs=[pl.BlockSpec((rows, width), lambda i, o: (0, 0))] * count,
            out_specs=pl.BlockSpec((rows, width), lambda i, o: (i, 0)),
        ),
        compiler_params=pltpu.CompilerParams(vmem_limit_bytes=32 << 20),
        cost_estimate=pl.CostEstimate(
            flops=0, bytes_accessed=count * rows * width * 6, transcendentals=0
        ),
        name="place",
    )(order, *pieces)


def shift_dp(value, shift, size):
    return lax.ppermute(value, "dp", [(d, (d + shift) % size) for d in range(size)])


def block(value, index, rows):
    return lax.dynamic_slice_in_dim(value, index * rows, rows, axis=0)


def sum_over_dp(partial):
    size = lax.axis_size("dp")
    if size != 8:
        return lax.psum(partial, "dp").astype(F32)
    d = lax.axis_index("dp")
    z, x = d // 2, d % 2
    rows = partial.shape[0] // 8
    swap = [(i, i ^ 1) for i in range(8)]
    sent = block(partial, 1 - x, 4 * rows)
    got = lax.ppermute(sent, "dp", swap)
    mine = (block(partial, x, 4 * rows).astype(F32) + got.astype(F32)).astype(B16)
    total = block(mine, z, rows).astype(F32)
    for s in (1, 2, 3):
        total = total + shift_dp(block(mine, (z + s) % 4, rows), 2 * s, 8).astype(F32)
    total = total.astype(B16)
    quarter = [total] + [shift_dp(total, 2 * s, 8) for s in (1, 2, 3)]
    other = [lax.ppermute(piece, "dp", swap) for piece in quarter]
    slot = jnp.arange(8, dtype=jnp.int32)
    order = (z - slot % 4) % 4 + 4 * (slot // 4 != x).astype(jnp.int32)
    return place(order, quarter + other)


def sum_over_all(values):
    t_size, d_size = lax.axis_size("tensor"), lax.axis_size("dp")
    if t_size & (t_size - 1) or d_size & (d_size - 1):
        return lax.psum(values, ("dp", "tensor"))
    for axis, size in (("tensor", t_size), ("dp", d_size)):
        step = 1
        while step < size:
            values = values + lax.ppermute(
                values, axis, [(i, i ^ step) for i in range(size)]
            )
            step *= 2
    return values


class Tensor:
    def __init__(self, share):
        self.share = share
        self.size = lax.axis_size("tensor")
        self.split = self.size == 4 and share % 16 == 0
        t = lax.axis_index("tensor")
        if self.split:
            self.order = jnp.stack([t, t ^ 1, t ^ 2, t ^ 3]) * share
            self.chunk = share
        else:
            self.order = jnp.zeros((1,), jnp.int32)
            self.chunk = share * self.size

    def core(self, value):
        return lax.ppermute(value, "tensor", [(0, 1), (1, 0), (2, 3), (3, 2)])

    def chip(self, value):
        return lax.ppermute(value, "tensor", [(0, 2), (2, 0), (1, 3), (3, 1)])

    def gather(self, own):
        if not self.split:
            return [lax.all_gather(own, "tensor", axis=0, tiled=True)]
        far = self.chip(own)
        near = jnp.concatenate([own, self.core(own)], axis=0)
        return [near, jnp.concatenate([far, self.core(far)], axis=0)]

    def reduce(self, terms):
        if not self.split:
            return lax.psum_scatter(
                terms[0](), "tensor", scatter_dimension=0, tiled=True
            )
        share = self.share
        far = terms[1]()
        far_sum = far[:share] + self.core(far[share:].astype(B16)).astype(F32)
        arriving = self.chip(far_sum.astype(B16))
        near = terms[0]()
        near_sum = near[:share] + self.core(near[share:].astype(B16)).astype(F32)
        return near_sum + arriving.astype(F32)


def normalize(values):
    center = values - jnp.mean(values, axis=-1, keepdims=True)
    inverse = lax.rsqrt(jnp.mean(center * center, axis=-1, keepdims=True) + epsilon)
    return center * inverse, inverse


def normalize_back(grad, gain, vhat, inverse):
    scaled = grad * gain
    mean_scaled = jnp.mean(scaled, axis=-1, keepdims=True)
    mean_product = jnp.mean(scaled * vhat, axis=-1, keepdims=True)
    values_grad = (scaled - mean_scaled - vhat * mean_product) * inverse
    return values_grad, jnp.sum(grad * vhat, axis=0), jnp.sum(grad, axis=0)


def per_device(tokens, cotangent, lengths, groups, w_qkv, w_out, w_up, w_down, gains, biases):
    row_count, share, width = tokens.shape
    cols = w_qkv.shape[2]
    pairs = cols // 128
    tensor = Tensor(share)
    t = lax.axis_index("tensor")
    positions = t * share + jnp.arange(share, dtype=jnp.int32)
    w_qkv = w_qkv.reshape(width, 3, pairs, 128).transpose(0, 2, 1, 3)
    w_qkv = w_qkv.reshape(width, 3 * cols)
    rows = range(row_count)

    def product(weight):
        return lambda part: nn(part, weight)

    def product_back(weight):
        return lambda part: nt(part, weight)

    def reduce(parts, function):
        return tensor.reduce([functools.partial(function, part) for part in parts])

    x, valid, meta = [], [], []
    for r in rows:
        x.append(tokens[r].astype(F32))
        valid.append((positions < lengths[r]).astype(F32)[:, None])
        meta.append(jnp.concatenate([lengths[r][None], tensor.order]).astype(jnp.int32))

    xhat, xinv, attn_in, projected, attended, lse = [], [], [], [], [], []
    for r in rows:
        hat, inv = normalize(x[r])
        xhat.append(hat)
        xinv.append(inv)
        attn_in.append(tensor.gather((hat * gains[0] + biases[0]).astype(B16)))
    for r in rows:
        projected.append([nn(part, w_qkv).astype(B16) for part in attn_in[r]])
        *parts, row_lse = attend(meta[r], projected[r], tensor.chunk)
        attended.append(parts)
        lse.append(row_lse)
    middle, ahat, ainv, mhat, minv, ffn_in = [], [], [], [], [], []
    squares = [[] for _ in rows]
    for r in rows:
        attn_sum = reduce(attended[r], product(w_out))
        hat, inv = normalize(attn_sum)
        ahat.append(hat)
        ainv.append(inv)
        branch = hat * gains[1] + biases[1]
        squares[r].append(jnp.sum(branch * branch * valid[r]))
        middle.append(x[r] + branch)
        hat, inv = normalize(middle[r])
        mhat.append(hat)
        minv.append(inv)
        ffn_in.append(tensor.gather((hat * gains[2] + biases[2]).astype(B16)))
    activated, slope, fhat, finv, output = [], [], [], [], []
    for r in rows:
        pieces = [up_project(part, w_up) for part in ffn_in[r]]
        activated.append([piece[0] for piece in pieces])
        slope.append([piece[1] for piece in pieces])
        ffn_sum = reduce(activated[r], product(w_down))
        hat, inv = normalize(ffn_sum)
        fhat.append(hat)
        finv.append(inv)
        branch = hat * gains[3] + biases[3]
        result = middle[r] + branch
        output.append(result.astype(B16))
        squares[r].append(jnp.sum(branch * branch * valid[r]))
        squares[r].insert(0, jnp.sum(result * result * valid[r]))

    gain_grads = [[0.0] * 4 for _ in rows]
    bias_grads = [[0.0] * 4 for _ in rows]
    out_grad, ffn_grad, hidden_grad, middle_grad, attn_grad = [], [], [], [], []
    for r in rows:
        out_grad.append(cotangent[r].astype(F32) * valid[r])
        grad, gain_grads[r][3], bias_grads[r][3] = normalize_back(
            out_grad[r], gains[3], fhat[r], finv[r]
        )
        ffn_grad.append(tensor.gather(grad.astype(B16)))
    grad_down = outer_sum(sum(activated, []), sum(ffn_grad, []))
    for r in rows:
        hidden_grad.append(
            [
                (nt(part, w_down) * bend.astype(F32)).astype(B16)
                for part, bend in zip(ffn_grad[r], slope[r])
            ]
        )
        ffn_in_grad = reduce(hidden_grad[r], product_back(w_up))
        grad, gain_grads[r][2], bias_grads[r][2] = normalize_back(
            ffn_in_grad, gains[2], mhat[r], minv[r]
        )
        middle_grad.append(out_grad[r] + grad)
        grad, gain_grads[r][1], bias_grads[r][1] = normalize_back(
            middle_grad[r], gains[1], ahat[r], ainv[r]
        )
        attn_grad.append(tensor.gather(grad.astype(B16)))
    grad_up = outer_sum(sum(ffn_in, []), sum(hidden_grad, []))
    grad_down = sum_over_dp(grad_down)
    grad_up = sum_over_dp(grad_up)
    grad_out = outer_sum(sum(attended, []), sum(attn_grad, []))
    projected_grad, input_grad = [], []
    for r in rows:
        grads = [nt(part, w_out).astype(B16) for part in attn_grad[r]]
        projected_grad.append(
            list(attend_back(meta[r], projected[r], attended[r], grads, lse[r], tensor.chunk))
        )
        attn_in_grad = reduce(projected_grad[r], product_back(w_qkv))
        grad, gain_grads[r][0], bias_grads[r][0] = normalize_back(
            attn_in_grad, gains[0], xhat[r], xinv[r]
        )
        input_grad.append((middle_grad[r] + grad).astype(B16))
    grad_qkv = outer_sum(sum(attn_in, []), sum(projected_grad, []))
    grad_out = sum_over_dp(grad_out)
    grad_qkv = sum_over_dp(grad_qkv)
    grad_qkv = grad_qkv.reshape(width, pairs, 3, 128).transpose(0, 2, 1, 3)
    grad_qkv = grad_qkv.reshape(width, 3, cols)

    member = (groups[:, None] == jnp.arange(GROUPS, dtype=jnp.int32)[None, :]).astype(F32)
    sums = jnp.stack([jnp.stack(row) for row in squares])
    counts = jnp.stack([jnp.sum(v) for v in valid])
    sums = jnp.concatenate([sums, counts[:, None]], axis=1)
    sums = jnp.sum(member[:, :, None] * sums[:, None, :], axis=0).reshape(1, GROUPS * 4)
    sums = jnp.pad(sums, ((0, 0), (0, width - GROUPS * 4)))
    small = jnp.stack(
        [sum(gain_grads[r][n] for r in rows) for n in range(4)]
        + [sum(bias_grads[r][n] for r in rows) for n in range(4)]
    )
    small = sum_over_all(jnp.concatenate([small, sums], axis=0))
    sums = small[8, : GROUPS * 4].reshape(GROUPS, 4)
    group_rms = jnp.sqrt(sums[:, :3] / (sums[:, 3:] * width))
    return (
        jnp.stack(output),
        jnp.stack(input_grad),
        grad_qkv,
        grad_out,
        grad_up,
        grad_down,
        small[:4],
        small[4:8],
        group_rms,
    )


def solution(mesh):
    placed = (
        P("dp", "tensor", None),
        P("dp", "tensor", None),
        P("dp"),
        P("dp"),
        P(None, None, "tensor"),
        P("tensor", None),
        P(None, "tensor"),
        P("tensor", None),
        P(),
        P(),
    )
    return jax.shard_map(
        per_device,
        mesh=mesh,
        in_specs=placed,
        out_specs=(
            P("dp", "tensor", None),
            P("dp", "tensor", None),
            P(None, None, "tensor"),
            P("tensor", None),
            P(None, "tensor"),
            P("tensor", None),
            P(),
            P(),
            P(),
        ),
        check_vma=False,
    )
```

time: 1240 us -> 584 us (0.47)
  waiting for transfers between devices: 769 us -> 211 us
  matrix products: 183 us -> 34.2 us
  Pallas kernels: 0 us -> 113 us
  starting transfers between devices: 0.76 us -> 97.2 us
  other arithmetic: 108 us -> 60.8 us
  blocking collectives: 42.8 us -> 0 us
  local copies, waits for them, and re-layouts: 94.3 us -> 54.1 us
  loops' own time: 22.4 us -> 0 us
    psum x1 -> x0, waiting for transfers between devices: 356 us -> none  [per_device(): lax.psum((grad_qkv, grad_out, grad_up, grad_down), 'dp')]
    reduce_scatter x4 -> x0, waiting for transfers between devices: 269 us -> none  [the longest x1 75.2 us: per_device(): lax.psum_scatter(matmul_back(hidden_grad16, w_up), 'tensor', scatter_dime...]
    ppermute x0 -> x97, waiting for transfers between devices: none -> 211 us  [the longest x16 102 us: chip(): return lax.ppermute(value, 'tensor', [(0, 2), (2, 0), (1, 3), (3, 1)])]
    dot_general x42 -> x28, matrix products: 183 us -> 34.2 us  [the longest x16 20.7 us: nt(): lax.dot_general(left, right, (((1,), (1,)), ((), ())), preferred_element_...]
    all_gather x4 -> x0, waiting for transfers between devices: 144 us -> none  [the longest x1 36.1 us: per_device(): attn_full = lax.all_gather(attn_in16, 'tensor', axis=1, tiled=True)]
    pallas_call x0 -> x16, Pallas kernels: none -> 113 us  [the longest x2 41.8 us: attend_back(): pl.pallas_call(functools.partial(attend_back_kernel, slots, chunk, parts,...]
    ppermute x0 -> x97, starting transfers between devices: none -> 97.2 us  [the longest x24 47.2 us: shift_dp(): lax.ppermute(value, 'dp', [(d, (d + shift) % size) for d in range(size)])]
    psum x1 -> x0, blocking collectives: 42.8 us -> none  [per_device(): lax.psum((grad_gains, grad_biases), ('dp', 'tensor'))]
  transfers between devices with their start and end apart: 9 -> 97, of which waited for: 9 -> 34; matrix products, arithmetic and copies ran while one was open for 3% -> 17% of each run, Pallas kernels for 0% -> 16%
where the time goes in v1:
time: 584 us; the launch traced here: 574 us
  waiting for transfers between devices  211 us (36%)
  Pallas kernels  113 us (19%)
  starting transfers between devices  97.2 us (17%)
  other arithmetic  60.8 us (10%)
  local copies, waits for them, and re-layouts  54.1 us (9%)
  matrix products  34.2 us (6%)
    ppermute x16, waiting for transfers between devices, chip(): return lax.ppermute(value, 'tensor', [(0, 2), (2, 0), (1, 3), (3, 1)])  102 us
    ppermute x24, starting transfers between devices, shift_dp(): lax.ppermute(value, 'dp', [(d, (d + shift) % size) for d in range(size)])  47.2 us
    pallas_call x2, Pallas kernels, attend_back(): pl.pallas_call(functools.partial(attend_back_kernel, slots, chunk, parts,...  41.8 us
    ppermute x4, waiting for transfers between devices, sum_over_dp(): got = lax.ppermute(sent, 'dp', swap)  39 us
    unnamed x328, local copies, waits for them, and re-layouts  35.3 us
    ppermute x16, waiting for transfers between devices, sum_over_dp(): other = [lax.ppermute(piece, 'dp', swap) for piece in quarter]  31.2 us
    ppermute x24, waiting for transfers between devices, shift_dp(): lax.ppermute(value, 'dp', [(d, (d + shift) % size) for d in range(size)])  28.4 us
    pallas_call x4, Pallas kernels, outer_sum(): pl.pallas_call(functools.partial(outer_kernel, count), out_shape=jax.Shap...  24.6 us
  transfers between devices with their start and end apart: 97, of which 34 were waited for; matrix products, arithmetic and copies ran while one was open for 17% of the time, Pallas kernels for 16%

profile of v1, /device:TPU:0, one launch (start us, length us, event | category | flops | bytes accessed | tf_op | source)
XLA Modules:
  0.0 574.0 jit_solution(11473519303444556513)
XLA Ops:
  14.5 6.8 %collective-permute-done.1 = bf16[272,1024]{1,0:T(8,128)(2,1)} collective-permute-done((bf16[272,1024]{1,0:T(8,128)(2,1)S(1)}, bf16[272,1024]{1,0:T(8,128)(2,1)}, u32[]{:S(2)}, u32[]{:S(2)}) %collective-permute-start.1) | collective-permute-done | bytes 557088 | tf_op jit(solution)/shard_map/ppermute | solution.py:413
  21.2 11.1 %collective-permute-done.13 = bf16[272,1024]{1,0:T(8,128)(2,1)} collective-permute-done((bf16[272,1024]{1,0:T(8,128)(2,1)S(1)}, bf16[272,1024]{1,0:T(8,128)(2,1)}, u32[]{:S(2)}, u32[]{:S(2)}) %collective-permute-start.13) | collective-permute-done | bytes 557088 | tf_op jit(solution)/shard_map/ppermute | solution.py:413
  41.8 10.2 %attend.2 = (bf16[544,256]{1,0:T(8,128)(2,1)S(1)}, bf16[544,256]{1,0:T(8,128)(2,1)S(1)}, f32[4,1,1088]{2,1,0:T(1,128)S(1)}) custom-call(s32[5]{0:T(128)S(1)} %get-tuple-element.174.meta, bf16[544,768]{1,0:T(8,128)(2,1)S(1)} %convolution_convert_fusion.3.refs_0_, bf16[544,768]{1,0:T(8,128)(2,1)S(1)} %convolution_convert_fusion.2.refs_1_), custom_call_target="tpu_custom_call" | custom-call | flops 4848615424 | bytes 2228224 | tf_op jit(solution)/shard_map/attend/pallas_call | solution.py:116
  53.9 10.5 %attend.3 = (bf16[544,256]{1,0:T(8,128)(2,1)S(1)}, bf16[544,256]{1,0:T(8,128)(2,1)S(1)}, f32[4,1,1088]{2,1,0:T(1,128)S(1)}) custom-call(s32[5]{0:T(128)S(1)} %get-tuple-element.175.meta, bf16[544,768]{1,0:T(8,128)(2,1)S(1)} %convolution_convert_fusion.1.refs_0_, bf16[544,768]{1,0:T(8,128)(2,1)S(1)} %convolution_convert_fusion.refs_1_), custom_call_target="tpu_custom_call" | custom-call | flops 4848615424 | bytes 2228224 | tf_op jit(solution)/shard_map/attend/pallas_call | solution.py:116
  69.3 12.1 %collective-permute-done.5 = bf16[272,1024]{1,0:T(8,128)(2,1)S(1)} collective-permute-done((bf16[272,1024]{1,0:T(8,128)(2,1)S(1)}, bf16[272,1024]{1,0:T(8,128)(2,1)S(1)}, u32[]{:S(2)}, u32[]{:S(2)}) %collective-permute-start.5) | collective-permute-done | bytes 557088 | tf_op jit(solution)/shard_map/ppermute | solution.py:413
  82.1 10.5 %collective-permute-done.17 = bf16[272,1024]{1,0:T(8,128)(2,1)S(1)} collective-permute-done((bf16[272,1024]{1,0:T(8,128)(2,1)S(1)}, bf16[272,1024]{1,0:T(8,128)(2,1)S(1)}, u32[]{:S(2)}, u32[]{:S(2)}) %collective-permute-start.17) | collective-permute-done | bytes 557088 | tf_op jit(solution)/shard_map/ppermute | solution.py:413
  108.5 7.3 %collective-permute-done.8 = bf16[272,1024]{1,0:T(8,128)(2,1)S(1)} collective-permute-done((bf16[272,1024]{1,0:T(8,128)(2,1)}, bf16[272,1024]{1,0:T(8,128)(2,1)S(1)}, u32[]{:S(2)}, u32[]{:S(2)}) %collective-permute-start.8) | collective-permute-done | bytes 557088 | tf_op jit(solution)/shard_map/ppermute | solution.py:413
  115.8 11.5 %collective-permute-done.20 = bf16[272,1024]{1,0:T(8,128)(2,1)S(1)} collective-permute-done((bf16[272,1024]{1,0:T(8,128)(2,1)}, bf16[272,1024]{1,0:T(8,128)(2,1)S(1)}, u32[]{:S(2)}, u32[]{:S(2)}) %collective-permute-start.20) | collective-permute-done | bytes 557088 | tf_op jit(solution)/shard_map/ppermute | solution.py:413
  147.2 11.5 %collective-permute-done.23 = bf16[272,1024]{1,0:T(8,128)(2,1)S(1)} collective-permute-done((bf16[272,1024]{1,0:T(8,128)(2,1)S(1)}, bf16[272,1024]{1,0:T(8,128)(2,1)S(1)}, u32[]{:S(2)}, u32[]{:S(2)}) %collective-permute-start.23) | collective-permute-done | bytes 557088 | tf_op jit(solution)/shard_map/ppermute | solution.py:413
  159.3 10.9 %collective-permute-done.11 = bf16[272,1024]{1,0:T(8,128)(2,1)S(1)} collective-permute-done((bf16[272,1024]{1,0:T(8,128)(2,1)S(1)}, bf16[272,1024]{1,0:T(8,128)(2,1)S(1)}, u32[]{:S(2)}, u32[]{:S(2)}) %collective-permute-start.11) | collective-permute-done | bytes 557088 | tf_op jit(solution)/shard_map/ppermute | solution.py:413
  189.5 3.9 collective-permute-done.26
  193.4 10.6 %collective-permute-done.38 = bf16[272,1024]{1,0:T(8,128)(2,1)} collective-permute-done((bf16[272,1024]{1,0:T(8,128)(2,1)}, bf16[272,1024]{1,0:T(8,128)(2,1)}, u32[]{:S(2)}, u32[]{:S(2)}) %collective-permute-start.38) | collective-permute-done | bytes 557088 | tf_op jit(solution)/shard_map/ppermute | solution.py:413
  225.6 7.9 %outer_sum.6 = bf16[1024,1024]{1,0:T(8,128)(2,1)S(1)} custom-call(bf16[544,1024]{1,0:T(8,128)(2,1)S(1)} %copy-done.3, bf16[544,1024]{1,0:T(8,128)(2,1)S(1)} %copy-done.11, bf16[544,1024]{1,0:T(8,128)(2,1)S(1)} %pad_maximum_fusion.3.x_ref.refs_2_, bf16[544,1024]{1,0:T(8,128)(2,1)S(1)} %copy-done.13, bf16[544,1024]{1,0:T(8,128)(2,1)S(1)} %multiply_convert_fusion.3.refs_4_, ...), custom_call_target="tpu_custom_call" | custom-call | flops 9126805504 | bytes 11010048 | tf_op jit(solution)/shard_map/outer_sum/pallas_call | solution.py:305
  234.8 8.3 %outer_sum.7 = bf16[1024,1024]{1,0:T(8,128)(2,1)S(1)} custom-call(bf16[544,1024]{1,0:T(8,128)(2,1)S(1)} %copy-done.57, bf16[544,1024]{1,0:T(8,128)(2,1)S(1)} %copy-done.61, bf16[544,1024]{1,0:T(8,128)(2,1)S(1)} %copy-done.55, bf16[544,1024]{1,0:T(8,128)(2,1)S(1)} %copy-done.59, bf16[544,1024]{1,0:T(8,128)(2,1)S(1)} %pad_maximum_fusion.5.refs_4_, ...), custom_call_target="tpu_custom_call" | custom-call | flops 9126805504 | bytes 11010048 | tf_op jit(solution)/shard_map/outer_sum/pallas_call | solution.py:305
  250.0 19.1 %collective-permute-done.81 = bf16[512,1024]{1,0:T(8,128)(2,1)S(1)} collective-permute-done((bf16[512,1024]{1,0:T(8,128)(2,1)S(1)}, bf16[512,1024]{1,0:T(8,128)(2,1)S(1)}, u32[]{:S(2)}, u32[]{:S(2)}) %collective-permute-start.81) | collective-permute-done | bytes 1048608 | tf_op jit(solution)/shard_map/ppermute | solution.py:369
  271.4 19.9 %collective-permute-done.70 = bf16[512,1024]{1,0:T(8,128)(2,1)S(1)} collective-permute-done((bf16[512,1024]{1,0:T(8,128)(2,1)S(1)}, bf16[512,1024]{1,0:T(8,128)(2,1)S(1)}, u32[]{:S(2)}, u32[]{:S(2)}) %collective-permute-start.70) | collective-permute-done | bytes 1048608 | tf_op jit(solution)/shard_map/ppermute | solution.py:369
  307.8 6.7 %collective-permute-start.72 = (bf16[128,1024]{1,0:T(8,128)(2,1)S(1)}, bf16[128,1024]{1,0:T(8,128)(2,1)S(1)}, u32[]{:S(2)}, u32[]{:S(2)}) collective-permute-start(bf16[128,1024]{1,0:T(8,128)(2,1)S(1)} %get-tuple-element.148), channel_id=1, source_target_pairs={{0,16},{4,20},{8,24},{12,28},{16,0},{20,4},{24,8},{28,12},{1,17},{... | collective-permute-start | bytes 786440 | tf_op jit(solution)/shard_map/ppermute | solution.py:353
  314.5 10.3 %collective-permute-done.83 = bf16[128,1024]{1,0:T(8,128)(2,1)S(1)} collective-permute-done((bf16[128,1024]{1,0:T(8,128)(2,1)S(1)}, bf16[128,1024]{1,0:T(8,128)(2,1)S(1)}, u32[]{:S(2)}, u32[]{:S(2)}) %collective-permute-start.83) | collective-permute-done | bytes 262176 | tf_op jit(solution)/shard_map/ppermute | solution.py:353
  329.0 11.6 %collective-permute-done.72 = bf16[128,1024]{1,0:T(8,128)(2,1)S(1)} collective-permute-done((bf16[128,1024]{1,0:T(8,128)(2,1)S(1)}, bf16[128,1024]{1,0:T(8,128)(2,1)S(1)}, u32[]{:S(2)}, u32[]{:S(2)}) %collective-permute-start.72) | collective-permute-done | bytes 262176 | tf_op jit(solution)/shard_map/ppermute | solution.py:353
  344.8 6.2 %collective-permute-done.43 = bf16[272,1024]{1,0:T(8,128)(2,1)S(1)} collective-permute-done((bf16[272,1024]{1,0:T(8,128)(2,1)S(1)}, bf16[272,1024]{1,0:T(8,128)(2,1)S(1)}, u32[]{:S(2)}, u32[]{:S(2)}) %collective-permute-start.43) | collective-permute-done | bytes 557088 | tf_op jit(solution)/shard_map/ppermute | solution.py:413
  357.8 20.9 %attend_back.3 = (bf16[544,768]{1,0:T(8,128)(2,1)S(1)}, bf16[544,768]{1,0:T(8,128)(2,1)S(1)}) custom-call(s32[5]{0:T(128)S(1)} %get-tuple-element.175.meta, bf16[544,768]{1,0:T(8,128)(2,1)S(1)} %copy-done.53, bf16[544,768]{1,0:T(8,128)(2,1)S(1)} %copy-done.73, bf16[544,256]{1,0:T(8,128)(2,1)S(1)} %copy-done.7, bf16[544,256]{1,0:T(8,128)(2,1)S(1)} %copy-done.9, ...), custom_call_target="tpu_custom_call" | custom-call | flops 9697230848 | bytes 5570560 | tf_op jit(solution)/shard_map/attend_back/pallas_call | solution.py:225
  381.1 20.9 %attend_back.2 = (bf16[544,768]{1,0:T(8,128)(2,1)S(1)}, bf16[544,768]{1,0:T(8,128)(2,1)S(1)}) custom-call(s32[5]{0:T(128)S(1)} %get-tuple-element.174.meta, bf16[544,768]{1,0:T(8,128)(2,1)S(1)} %copy-done.51, bf16[544,768]{1,0:T(8,128)(2,1)S(1)} %copy-done.71, bf16[544,256]{1,0:T(8,128)(2,1)S(1)} %get-tuple-element.27.refs_2_.refs_0_, ...), custom_call_target="tpu_custom_call" | custom-call | flops 9697230848 | bytes 5570560 | tf_op jit(solution)/shard_map/attend_back/pallas_call | solution.py:225
  402.0 6.6 %outer_sum.4 = bf16[1024,768]{1,0:T(8,128)(2,1)S(1)} custom-call(bf16[544,1024]{1,0:T(8,128)(2,1)S(1)} %pad_maximum_fusion.refs_0_, bf16[544,1024]{1,0:T(8,128)(2,1)S(1)} %copy-done.15, bf16[544,1024]{1,0:T(8,128)(2,1)S(1)} %pad_maximum_fusion.2.refs_2_, bf16[544,1024]{1,0:T(8,128)(2,1)S(1)} %copy-done.17, bf16[544,768]{1,0:T(8,128)(2,1)S(1)} %get-tuple-element.38.refs_4_, ...), custom_call_target="tpu_custom_call" | custom-call | flops 6845104128 | bytes 9371648 | tf_op jit(solution)/shard_map/outer_sum/pallas_call | solution.py:305
  424.3 9.9 %collective-permute-start.74 = (bf16[128,1024]{1,0:T(8,128)(2,1)S(1)}, bf16[128,1024]{1,0:T(8,128)(2,1)S(1)}, u32[]{:S(2)}, u32[]{:S(2)}) collective-permute-start(bf16[128,1024]{1,0:T(8,128)(2,1)S(1)} %add_convert_fusion.6.refs_0_), channel_id=1, source_target_pairs={{0,8},{4,12},{8,16},{12,20},{16,24},{20,28},{24,0},{28,4},{1,9},{5... | collective-permute-start | bytes 786440 | tf_op jit(solution)/shard_map/ppermute | solution.py:353
  436.8 5.9 %collective-permute-start.90 = (bf16[128,1024]{1,0:T(8,128)(2,1)S(1)}, bf16[128,1024]{1,0:T(8,128)(2,1)S(1)}, u32[]{:S(2)}, u32[]{:S(2)}) collective-permute-start(bf16[128,1024]{1,0:T(8,128)(2,1)S(1)} %collective-permute-done.86.refs_2_), channel_id=1, source_target_pairs={{0,4},{4,0},{8,12},{12,8},{16,20},{20,16},{24,28},{28,24},{1,5},{5... | collective-permute-start | bytes 786440 | tf_op jit(solution)/shard_map/ppermute | solution.py:376
  446.3 5.6 collective-permute-done.90.refs_6_
  457.6 5.5 collective-permute-done.80.refs_7_
  469.4 4.1 collective-permute-done.78.refs_5_
  502.6 4.1 place.6
  506.8 4.1 place.7
  522.5 4.3 fusion.32
  566.0 4.0 copy.32
  (686 shorter events, 267.6 us)
Async XLA Ops:
  7.7 28.1 %collective-permute-start = (bf16[272,1024]{1,0:T(8,128)(2,1)S(1)}, bf16[272,1024]{1,0:T(8,128)(2,1)}, u32[]{:S(2)}, u32[]{:S(2)}) collective-permute-start(bf16[272,1024]{1,0:T(8,128)(2,1)S(1)} %get-tuple-element.137), channel_id=1, source_target_pairs={{0,1},{1,0},{2,3},{3,2},{4,5},{5,4},{6,7},{7,6},{8,9},{9,8},{10,11... | collective-permute-start | bytes 1671176 | tf_op jit(solution)/shard_map/ppermute | solution.py:410
  101.8 25.5 %collective-permute-start.6 = (bf16[272,1024]{1,0:T(8,128)(2,1)}, bf16[272,1024]{1,0:T(8,128)(2,1)S(1)}, u32[]{:S(2)}, u32[]{:S(2)}) collective-permute-start(bf16[272,1024]{1,0:T(8,128)(2,1)} %get-tuple-element.165), channel_id=1, source_target_pairs={{0,1},{1,0},{2,3},{3,2},{4,5},{5,4},{6,7},{7,6},{8,9},{9,8},{10,11... | collective-permute-start | bytes 1671176 | tf_op jit(solution)/shard_map/ppermute | solution.py:410
  102.0 25.2 %collective-permute-start.20 = (bf16[272,1024]{1,0:T(8,128)(2,1)}, bf16[272,1024]{1,0:T(8,128)(2,1)S(1)}, u32[]{:S(2)}, u32[]{:S(2)}) collective-permute-start(bf16[272,1024]{1,0:T(8,128)(2,1)} %get-tuple-element.166), channel_id=1, source_target_pairs={{0,2},{2,0},{1,3},{3,1},{4,6},{6,4},{5,7},{7,5},{8,10},{10,8},{9,1... | collective-permute-start | bytes 1671176 | tf_op jit(solution)/shard_map/ppermute | solution.py:413
  108.4 38.8 %collective-permute-start.19 = (bf16[272,1024]{1,0:T(8,128)(2,1)S(1)}, bf16[272,1024]{1,0:T(8,128)(2,1)S(1)}, u32[]{:S(2)}, u32[]{:S(2)}) collective-permute-start(bf16[272,1024]{1,0:T(8,128)(2,1)S(1)} %slice.375), channel_id=1, source_target_pairs={{0,1},{1,0},{2,3},{3,2},{4,5},{5,4},{6,7},{7,6},{8,9},{9,8},{10,11... | collective-permute-start | bytes 1671176 | tf_op jit(solution)/shard_map/ppermute | solution.py:410
  187.3 26.1 %collective-permute-start.24 = (bf16[272,1024]{1,0:T(8,128)(2,1)}, bf16[272,1024]{1,0:T(8,128)(2,1)S(1)}, u32[]{:S(2)}, u32[]{:S(2)}) collective-permute-start(bf16[272,1024]{1,0:T(8,128)(2,1)} %get-tuple-element.141), channel_id=1, source_target_pairs={{0,1},{1,0},{2,3},{3,2},{4,5},{5,4},{6,7},{7,6},{8,9},{9,8},{10,11... | collective-permute-start | bytes 1671176 | tf_op jit(solution)/shard_map/ppermute | solution.py:410
  193.4 27.7 %collective-permute-start.27 = (bf16[272,1024]{1,0:T(8,128)(2,1)}, bf16[272,1024]{1,0:T(8,128)(2,1)S(1)}, u32[]{:S(2)}, u32[]{:S(2)}) collective-permute-start(bf16[272,1024]{1,0:T(8,128)(2,1)} %collective-permute-done.26), channel_id=1, source_target_pairs={{0,1},{1,0},{2,3},{3,2},{4,5},{5,4},{6,7},{7,6},{8,9},{9,8},{10,11... | collective-permute-start | bytes 1671176 | tf_op jit(solution)/shard_map/ppermute | solution.py:410
  243.1 26.0 %collective-permute-start.81 = (bf16[512,1024]{1,0:T(8,128)(2,1)S(1)}, bf16[512,1024]{1,0:T(8,128)(2,1)S(1)}, u32[]{:S(2)}, u32[]{:S(2)}) collective-permute-start(bf16[512,1024]{1,0:T(8,128)(2,1)S(1)} %constant_dynamic-slice_fusion.3), channel_id=1, source_target_pairs={{0,4},{4,0},{8,12},{12,8},{16,20},{20,16},{24,28},{28,24},{1,5},{5... | collective-permute-start | bytes 3145736 | tf_op jit(solution)/shard_map/ppermute | solution.py:369
  245.0 46.3 %collective-permute-start.70 = (bf16[512,1024]{1,0:T(8,128)(2,1)S(1)}, bf16[512,1024]{1,0:T(8,128)(2,1)S(1)}, u32[]{:S(2)}, u32[]{:S(2)}) collective-permute-start(bf16[512,1024]{1,0:T(8,128)(2,1)S(1)} %constant_dynamic-slice_fusion.7), channel_id=1, source_target_pairs={{0,4},{4,0},{8,12},{12,8},{16,20},{20,16},{24,28},{28,24},{1,5},{5... | collective-permute-start | bytes 3145736 | tf_op jit(solution)/shard_map/ppermute | solution.py:369
  247.2 46.4 %collective-permute-start.37 = (bf16[272,1024]{1,0:T(8,128)(2,1)S(1)}, bf16[272,1024]{1,0:T(8,128)(2,1)S(1)}, u32[]{:S(2)}, u32[]{:S(2)}) collective-permute-start(bf16[272,1024]{1,0:T(8,128)(2,1)S(1)} %slice.369), channel_id=1, source_target_pairs={{0,1},{1,0},{2,3},{3,2},{4,5},{5,4},{6,7},{7,6},{8,9},{9,8},{10,11... | collective-permute-start | bytes 1671176 | tf_op jit(solution)/shard_map/ppermute | solution.py:410
  247.6 48.0 %collective-permute-start.25 = (bf16[272,1024]{1,0:T(8,128)(2,1)S(1)}, bf16[272,1024]{1,0:T(8,128)(2,1)S(1)}, u32[]{:S(2)}, u32[]{:S(2)}) collective-permute-start(bf16[272,1024]{1,0:T(8,128)(2,1)S(1)} %slice.373), channel_id=1, source_target_pairs={{0,1},{1,0},{2,3},{3,2},{4,5},{5,4},{6,7},{7,6},{8,9},{9,8},{10,11... | collective-permute-start | bytes 1671176 | tf_op jit(solution)/shard_map/ppermute | solution.py:410
  248.1 48.6 %collective-permute-start.41 = (bf16[272,1024]{1,0:T(8,128)(2,1)S(1)}, bf16[272,1024]{1,0:T(8,128)(2,1)S(1)}, u32[]{:S(2)}, u32[]{:S(2)}) collective-permute-start(bf16[272,1024]{1,0:T(8,128)(2,1)S(1)} %fusion.36), channel_id=1, source_target_pairs={{0,2},{2,0},{1,3},{3,1},{4,6},{6,4},{5,7},{7,5},{8,10},{10,8},{9,1... | collective-permute-start | bytes 1671176 | tf_op jit(solution)/shard_map/ppermute | solution.py:413
  269.2 29.1 %collective-permute-start.29 = (bf16[272,1024]{1,0:T(8,128)(2,1)S(1)}, bf16[272,1024]{1,0:T(8,128)(2,1)S(1)}, u32[]{:S(2)}, u32[]{:S(2)}) collective-permute-start(bf16[272,1024]{1,0:T(8,128)(2,1)S(1)} %fusion.40), channel_id=1, source_target_pairs={{0,2},{2,0},{1,3},{3,1},{4,6},{6,4},{5,7},{7,5},{8,10},{10,8},{9,1... | collective-permute-start | bytes 1671176 | tf_op jit(solution)/shard_map/ppermute | solution.py:413
  295.7 29.1 %collective-permute-start.83 = (bf16[128,1024]{1,0:T(8,128)(2,1)S(1)}, bf16[128,1024]{1,0:T(8,128)(2,1)S(1)}, u32[]{:S(2)}, u32[]{:S(2)}) collective-permute-start(bf16[128,1024]{1,0:T(8,128)(2,1)S(1)} %get-tuple-element.145), channel_id=1, source_target_pairs={{0,16},{4,20},{8,24},{12,28},{16,0},{20,4},{24,8},{28,12},{1,17},{... | collective-permute-start | bytes 786440 | tf_op jit(solution)/shard_map/ppermute | solution.py:353
  296.7 32.0 %collective-permute-start.71 = (bf16[128,1024]{1,0:T(8,128)(2,1)S(1)}, bf16[128,1024]{1,0:T(8,128)(2,1)S(1)}, u32[]{:S(2)}, u32[]{:S(2)}) collective-permute-start(bf16[128,1024]{1,0:T(8,128)(2,1)S(1)} %get-tuple-element.146), channel_id=1, source_target_pairs={{0,8},{4,12},{8,16},{12,20},{16,24},{20,28},{24,0},{28,4},{1,9},{5... | collective-permute-start | bytes 786440 | tf_op jit(solution)/shard_map/ppermute | solution.py:353
  298.3 30.7 %collective-permute-start.73 = (bf16[128,1024]{1,0:T(8,128)(2,1)S(1)}, bf16[128,1024]{1,0:T(8,128)(2,1)S(1)}, u32[]{:S(2)}, u32[]{:S(2)}) collective-permute-start(bf16[128,1024]{1,0:T(8,128)(2,1)S(1)} %get-tuple-element.147), channel_id=1, source_target_pairs={{0,24},{4,28},{8,0},{12,4},{16,8},{20,12},{24,16},{28,20},{1,25},{... | collective-permute-start | bytes 786440 | tf_op jit(solution)/shard_map/ppermute | solution.py:353
  307.8 32.7 %collective-permute-start.72 = (bf16[128,1024]{1,0:T(8,128)(2,1)S(1)}, bf16[128,1024]{1,0:T(8,128)(2,1)S(1)}, u32[]{:S(2)}, u32[]{:S(2)}) collective-permute-start(bf16[128,1024]{1,0:T(8,128)(2,1)S(1)} %get-tuple-element.148), channel_id=1, source_target_pairs={{0,16},{4,20},{8,24},{12,28},{16,0},{20,4},{24,8},{28,12},{1,17},{... | collective-permute-start | bytes 786440 | tf_op jit(solution)/shard_map/ppermute | solution.py:353
  314.5 27.8 %collective-permute-start.42 = (bf16[272,1024]{1,0:T(8,128)(2,1)S(1)}, bf16[272,1024]{1,0:T(8,128)(2,1)S(1)}, u32[]{:S(2)}, u32[]{:S(2)}) collective-permute-start(bf16[272,1024]{1,0:T(8,128)(2,1)S(1)} %get-tuple-element.167), channel_id=1, source_target_pairs={{0,1},{1,0},{2,3},{3,2},{4,5},{5,4},{6,7},{7,6},{8,9},{9,8},{10,11... | collective-permute-start | bytes 1671176 | tf_op jit(solution)/shard_map/ppermute | solution.py:410
  340.6 72.1 %collective-permute-start.88 = (bf16[128,1024]{1,0:T(8,128)(2,1)S(1)}, bf16[128,1024]{1,0:T(8,128)(2,1)S(1)}, u32[]{:S(2)}, u32[]{:S(2)}) collective-permute-start(bf16[128,1024]{1,0:T(8,128)(2,1)S(1)} %add_convert_fusion.5.refs_0_), channel_id=1, source_target_pairs={{0,4},{4,0},{8,12},{12,8},{16,20},{20,16},{24,28},{28,24},{1,5},{5... | collective-permute-start | bytes 786440 | tf_op jit(solution)/shard_map/ppermute | solution.py:376
  342.3 71.4 %collective-permute-start.87 = (bf16[128,1024]{1,0:T(8,128)(2,1)S(1)}, bf16[128,1024]{1,0:T(8,128)(2,1)S(1)}, u32[]{:S(2)}, u32[]{:S(2)}) collective-permute-start(bf16[128,1024]{1,0:T(8,128)(2,1)S(1)} %add_convert_fusion.5.refs_0_), channel_id=1, source_target_pairs={{0,24},{4,28},{8,0},{12,4},{16,8},{20,12},{24,16},{28,20},{1,25},{... | collective-permute-start | bytes 786440 | tf_op jit(solution)/shard_map/ppermute | solution.py:353
  351.0 63.9 %collective-permute-start.86 = (bf16[128,1024]{1,0:T(8,128)(2,1)S(1)}, bf16[128,1024]{1,0:T(8,128)(2,1)S(1)}, u32[]{:S(2)}, u32[]{:S(2)}) collective-permute-start(bf16[128,1024]{1,0:T(8,128)(2,1)S(1)} %add_convert_fusion.5.refs_0_), channel_id=1, source_target_pairs={{0,16},{4,20},{8,24},{12,28},{16,0},{20,4},{24,8},{28,12},{1,17},{... | collective-permute-start | bytes 786440 | tf_op jit(solution)/shard_map/ppermute | solution.py:353
  351.7 63.7 %collective-permute-start.85 = (bf16[128,1024]{1,0:T(8,128)(2,1)S(1)}, bf16[128,1024]{1,0:T(8,128)(2,1)S(1)}, u32[]{:S(2)}, u32[]{:S(2)}) collective-permute-start(bf16[128,1024]{1,0:T(8,128)(2,1)S(1)} %add_convert_fusion.5.refs_0_), channel_id=1, source_target_pairs={{0,8},{4,12},{8,16},{12,20},{16,24},{20,28},{24,0},{28,4},{1,9},{5... | collective-permute-start | bytes 786440 | tf_op jit(solution)/shard_map/ppermute | solution.py:353
  356.0 53.7 %collective-permute-start.59 = (bf16[128,1024]{1,0:T(8,128)(2,1)S(1)}, bf16[128,1024]{1,0:T(8,128)(2,1)S(1)}, u32[]{:S(2)}, u32[]{:S(2)}) collective-permute-start(bf16[128,1024]{1,0:T(8,128)(2,1)S(1)} %constant_dynamic-slice_fusion.11), channel_id=1, source_target_pairs={{0,4},{4,0},{8,12},{12,8},{16,20},{20,16},{24,28},{28,24},{1,5},{5... | collective-permute-start | bytes 786440 | tf_op jit(solution)/shard_map/ppermute | solution.py:369
  418.0 34.0 %collective-permute-start.48 = (bf16[512,768]{1,0:T(8,128)(2,1)S(1)}, bf16[512,768]{1,0:T(8,128)(2,1)S(1)}, u32[]{:S(2)}, u32[]{:S(2)}) collective-permute-start(bf16[512,768]{1,0:T(8,128)(2,1)S(1)} %constant_dynamic-slice_fusion.15), channel_id=1, source_target_pairs={{0,4},{4,0},{8,12},{12,8},{16,20},{20,16},{24,28},{28,24},{1,5},{5... | collective-permute-start | bytes 2359304 | tf_op jit(solution)/shard_map/ppermute | solution.py:369
  442.8 37.1 %collective-permute-start.34 = (bf16[272,1024]{1,0:T(8,128)(2,1)S(1)}, bf16[272,1024]{1,0:T(8,128)(2,1)S(1)}, u32[]{:S(2)}, u32[]{:S(2)}) collective-permute-start(bf16[272,1024]{1,0:T(8,128)(2,1)S(1)} %slice.370), channel_id=1, source_target_pairs={{0,1},{1,0},{2,3},{3,2},{4,5},{5,4},{6,7},{7,6},{8,9},{9,8},{10,11... | collective-permute-start | bytes 1671176 | tf_op jit(solution)/shard_map/ppermute | solution.py:410
  485.5 32.0 %collective-permute-start.45 = (bf16[272,1024]{1,0:T(8,128)(2,1)}, bf16[272,1024]{1,0:T(8,128)(2,1)}, u32[]{:S(2)}, u32[]{:S(2)}) collective-permute-start(bf16[272,1024]{1,0:T(8,128)(2,1)} %slice.367), channel_id=1, source_target_pairs={{0,1},{1,0},{2,3},{3,2},{4,5},{5,4},{6,7},{7,6},{8,9},{9,8},{10,11... | collective-permute-start | bytes 1671176 | tf_op jit(solution)/shard_map/ppermute | solution.py:410
  486.1 32.4 %collective-permute-start.33 = (bf16[272,1024]{1,0:T(8,128)(2,1)}, bf16[272,1024]{1,0:T(8,128)(2,1)}, u32[]{:S(2)}, u32[]{:S(2)}) collective-permute-start(bf16[272,1024]{1,0:T(8,128)(2,1)} %slice.371), channel_id=1, source_target_pairs={{0,1},{1,0},{2,3},{3,2},{4,5},{5,4},{6,7},{7,6},{8,9},{9,8},{10,11... | collective-permute-start | bytes 1671176 | tf_op jit(solution)/shard_map/ppermute | solution.py:410
  487.2 33.3 %collective-permute-start.47 = (bf16[272,1024]{1,0:T(8,128)(2,1)}, bf16[272,1024]{1,0:T(8,128)(2,1)}, u32[]{:S(2)}, u32[]{:S(2)}) collective-permute-start(bf16[272,1024]{1,0:T(8,128)(2,1)} %fusion.34), channel_id=1, source_target_pairs={{0,2},{2,0},{1,3},{3,1},{4,6},{6,4},{5,7},{7,5},{8,10},{10,8},{9,1... | collective-permute-start | bytes 1671176 | tf_op jit(solution)/shard_map/ppermute | solution.py:413
  489.0 33.5 %collective-permute-start.35 = (bf16[272,1024]{1,0:T(8,128)(2,1)}, bf16[272,1024]{1,0:T(8,128)(2,1)}, u32[]{:S(2)}, u32[]{:S(2)}) collective-permute-start(bf16[272,1024]{1,0:T(8,128)(2,1)} %fusion.38), channel_id=1, source_target_pairs={{0,2},{2,0},{1,3},{3,1},{4,6},{6,4},{5,7},{7,5},{8,10},{10,8},{9,1... | collective-permute-start | bytes 1671176 | tf_op jit(solution)/shard_map/ppermute | solution.py:413
  515.8 33.0 %collective-permute-start.55 = (bf16[128,768]{1,0:T(8,128)(2,1)S(1)}, bf16[128,768]{1,0:T(8,128)(2,1)S(1)}, u32[]{:S(2)}, u32[]{:S(2)}) collective-permute-start(bf16[128,768]{1,0:T(8,128)(2,1)S(1)} %add_convert_fusion.8.refs_0_), channel_id=1, source_target_pairs={{0,4},{4,0},{8,12},{12,8},{16,20},{20,16},{24,28},{28,24},{1,5},{5... | collective-permute-start | bytes 589832 | tf_op jit(solution)/shard_map/ppermute | solution.py:376
  517.5 25.9 %collective-permute-start.54 = (bf16[128,768]{1,0:T(8,128)(2,1)S(1)}, bf16[128,768]{1,0:T(8,128)(2,1)S(1)}, u32[]{:S(2)}, u32[]{:S(2)}) collective-permute-start(bf16[128,768]{1,0:T(8,128)(2,1)S(1)} %add_convert_fusion.8.refs_0_), channel_id=1, source_target_pairs={{0,24},{4,28},{8,0},{12,4},{16,8},{20,12},{24,16},{28,20},{1,25},{... | collective-permute-start | bytes 589832 | tf_op jit(solution)/shard_map/ppermute | solution.py:353
  518.5 25.3 %collective-permute-start.53 = (bf16[128,768]{1,0:T(8,128)(2,1)S(1)}, bf16[128,768]{1,0:T(8,128)(2,1)S(1)}, u32[]{:S(2)}, u32[]{:S(2)}) collective-permute-start(bf16[128,768]{1,0:T(8,128)(2,1)S(1)} %add_convert_fusion.8.refs_0_), channel_id=1, source_target_pairs={{0,16},{4,20},{8,24},{12,28},{16,0},{20,4},{24,8},{28,12},{1,17},{... | collective-permute-start | bytes 589832 | tf_op jit(solution)/shard_map/ppermute | solution.py:353
  520.5 25.7 %collective-permute-start.52 = (bf16[128,768]{1,0:T(8,128)(2,1)S(1)}, bf16[128,768]{1,0:T(8,128)(2,1)S(1)}, u32[]{:S(2)}, u32[]{:S(2)}) collective-permute-start(bf16[128,768]{1,0:T(8,128)(2,1)S(1)} %add_convert_fusion.8.refs_0_), channel_id=1, source_target_pairs={{0,8},{4,12},{8,16},{12,20},{16,24},{20,28},{24,0},{28,4},{1,9},{5... | collective-permute-start | bytes 589832 | tf_op jit(solution)/shard_map/ppermute | solution.py:353
  (224 other events, 2109.6 us)

commit v2 on v0

v2 whole, which is shorter than its diff:
```python
import functools

import jax
import jax.numpy as jnp
from jax import lax
from jax.experimental import pallas as pl
from jax.experimental.pallas import tpu as pltpu
from jax.sharding import PartitionSpec as P

HEAD_DIM = 64
GROUPS = 4
MIN_LENGTH = 544
F32 = jnp.float32
B16 = jnp.bfloat16

epsilon = 1e-05
negative_fill = -1e30
log2_e = 1.4426950408889634
gelu_scale = 0.7978845608028654
gelu_cubic = 0.044715

BASE, TENSOR, Z, X, LENGTH = 0, 1, 2, 3, 4


def nt(left, right):
    return lax.dot_general(
        left, right, (((1,), (1,)), ((), ())), preferred_element_type=F32
    )


def nn(left, right):
    return lax.dot_general(
        left, right, (((1,), (0,)), ((), ())), preferred_element_type=F32
    )


def tn(left, right):
    return lax.dot_general(
        left, right, (((0,), (0,)), ((), ())), preferred_element_type=F32
    )


def tiles(extent, size):
    return [(start, min(size, extent - start)) for start in range(0, extent, size)]


def whole(shape):
    return pl.BlockSpec(shape, lambda *_: (0,) * len(shape))


def once(shape):
    return pl.BlockSpec(
        shape, lambda *_: (0,) * len(shape), pipeline_mode=pl.Buffered(buffer_count=1)
    )


def anywhere():
    return pl.BlockSpec(memory_space=pl.ANY)


def call(kernel, name, scalars, inputs, outs, in_specs=None, out_specs=None, grid=(1,), scratch=(), limit=20, flops=0, aliases={}):
    values = sum(v.size for v in inputs)
    in_specs = in_specs or [once(v.shape) for v in inputs]
    out_specs = out_specs or [whole(shape) for shape, _ in outs]
    return list(
        pl.pallas_call(
            kernel,
            out_shape=[jax.ShapeDtypeStruct(shape, dtype) for shape, dtype in outs],
            grid_spec=pltpu.PrefetchScalarGridSpec(
                num_scalar_prefetch=1,
                grid=grid,
                in_specs=in_specs,
                out_specs=out_specs,
                scratch_shapes=list(scratch),
            ),
            input_output_aliases=aliases,
            compiler_params=pltpu.CompilerParams(
                dimension_semantics=("arbitrary",) * len(grid), vmem_limit_bytes=limit << 20
            ),
            cost_estimate=pl.CostEstimate(
                flops=flops // 16, bytes_accessed=values // 16, transcendentals=0
            ),
            name=name,
        )(scalars, *inputs)
    )


def lane_half(shape, half):
    return (lax.broadcasted_iota(jnp.int32, shape, 1) // HEAD_DIM) == half


def mask_tile(scores, query_start, length):
    key_index = lax.broadcasted_iota(jnp.int32, scores.shape, 0)
    query_index = query_start + lax.broadcasted_iota(jnp.int32, scores.shape, 1)
    allowed = key_index <= query_index
    if scores.shape[0] > MIN_LENGTH:
        allowed = allowed & (key_index < length)
    return jnp.where(allowed, scores, negative_fill)


def place_of(scalars, parts, number, chunk):
    if parts == 1:
        return 0
    return pl.multiple_of(lax.bitwise_xor(scalars[TENSOR], number) * chunk, 16)


def halves_of(refs, number, chunk):
    return refs[number % len(refs)].at[pl.ds(number // len(refs) * chunk, chunk), :]


def attend_kernel(row, chunk, parts, query_tile, scalars, *refs):
    queries, keys, values = (refs[i * parts : (i + 1) * parts] for i in range(3))
    count = 1 if parts == 1 else 2
    outputs = refs[3 * parts : 3 * parts + count]
    lse_ref, q_ref, k_ref, v_ref, vt_ref, ot_ref = refs[3 * parts + count :]
    slots = q_ref.shape[0]
    length = scalars[LENGTH + row]
    for number in range(parts):
        target = pl.ds(place_of(scalars, parts, number, chunk), chunk)
        q_ref[target, :] = queries[number][...]
        k_ref[target, :] = keys[number][...]
        v_ref[target, :] = values[number][...]
    vt_ref[...] = v_ref[...].T
    scale = log2_e / HEAD_DIM**0.5
    for q0, qn in tiles(slots, query_tile):
        extent = q0 + qn
        for half in (0, 1):
            query = q_ref[q0 : q0 + qn, :]
            query = jnp.where(lane_half(query.shape, half), query, jnp.zeros_like(query))
            scores = mask_tile(nt(k_ref[0:extent, :], query), q0, length)
            top = jnp.max(scores, axis=0, keepdims=True)
            weights = jnp.exp2((scores - top) * scale)
            total = jnp.sum(weights, axis=0, keepdims=True)
            lanes = slice(half * HEAD_DIM, half * HEAD_DIM + HEAD_DIM)
            out_t = nn(vt_ref[lanes, 0:extent], weights.astype(B16))
            ot_ref[lanes, q0 : q0 + qn] = out_t * (1.0 / total)
            lse_ref[half, :, q0 : q0 + qn] = top * scale + jnp.log2(total)
    q_ref[...] = ot_ref[...].T.astype(B16)
    for number in range(parts):
        source = pl.ds(place_of(scalars, parts, number, chunk), chunk)
        halves_of(outputs, number, chunk)[...] = q_ref[source, :]


def column(rows, position):
    return pl.BlockSpec((rows, 128), position)


def attend(scalars, row, projected):
    parts = len(projected)
    chunk, width = projected[0].shape
    pairs = width // 384
    slots = chunk * parts
    count = 1 if parts == 1 else 2
    columns = []
    for kind in range(3):
        spot = column(chunk, lambda p, s, kind=kind: (0, kind * pairs + p))
        columns += [spot] * parts
    return call(
        functools.partial(attend_kernel, row, chunk, parts, 512),
        "attend",
        scalars,
        [*projected, *projected, *projected],
        [((slots // count, pairs * 128), B16)] * count + [((2 * pairs, 1, slots), F32)],
        columns,
        [column(slots // count, lambda p, s: (0, p))] * count
        + [pl.BlockSpec((2, 1, slots), lambda p, s: (p, 0, 0))],
        (pairs,),
        [pltpu.VMEM((slots, 128), B16)] * 3
        + [pltpu.VMEM((128, slots), B16), pltpu.VMEM((128, slots), F32)],
        limit=24,
        flops=4 * slots * slots * 128 * pairs,
    )


def attend_back_kernel(row, chunk, parts, query_tile, scalars, *refs):
    queries, keys, values = (refs[i * parts : (i + 1) * parts] for i in range(3))
    count = 1 if parts == 1 else 2
    refs = refs[3 * parts :]
    attended, grads, lse_ref = refs[:count], refs[count : 2 * count], refs[2 * count]
    outputs = refs[2 * count + 1 : 3 * count + 1]
    q_ref, k_ref, v_ref, g_ref, kt_ref, inner_ref, dk_ref, dv_ref, dqt_ref, t_ref = refs[
        3 * count + 1 :
    ]
    slots = q_ref.shape[0]
    half = pl.program_id(0)
    length = scalars[LENGTH + row]

    @pl.when(half == 0)
    def _():
        for number in range(parts):
            target = pl.ds(place_of(scalars, parts, number, chunk), chunk)
            grad = halves_of(grads, number, chunk)[...]
            out = halves_of(attended, number, chunk)[...]
            q_ref[target, :] = queries[number][...]
            k_ref[target, :] = keys[number][...]
            v_ref[target, :] = values[number][...]
            g_ref[target, :] = grad
            t_ref[target, :] = out.astype(F32) * grad.astype(F32)
        kt_ref[...] = k_ref[...].T
        products = t_ref[...].T
        inner_ref[0:1, :] = jnp.sum(products[0:HEAD_DIM], axis=0, keepdims=True)
        inner_ref[1:2, :] = jnp.sum(products[HEAD_DIM:], axis=0, keepdims=True)
        dk_ref[...] = jnp.zeros_like(dk_ref)
        dv_ref[...] = jnp.zeros_like(dv_ref)

    scale = log2_e / HEAD_DIM**0.5
    base = pl.multiple_of(half * HEAD_DIM, HEAD_DIM)
    for q0, qn in tiles(slots, query_tile):
        extent = q0 + qn
        keep = lane_half((qn, 128), half)
        query = q_ref[q0 : q0 + qn, :]
        query = jnp.where(keep, query, jnp.zeros_like(query))
        grad = g_ref[q0 : q0 + qn, :]
        grad = jnp.where(keep, grad, jnp.zeros_like(grad))
        lse = lse_ref[0, :, q0 : q0 + qn]
        inner = jnp.where(
            half == 0, inner_ref[0:1, q0 : q0 + qn], inner_ref[1:2, q0 : q0 + qn]
        )
        scores = mask_tile(nt(k_ref[0:extent, :], query), q0, length)
        probs = jnp.exp2(scores * scale - lse)
        dv_ref[0:extent, :] += nn(probs.astype(B16), grad)
        probs_grad = nt(v_ref[0:extent, :], grad)
        scores_grad = (probs * (probs_grad - inner)).astype(B16)
        dk_ref[0:extent, :] += nn(scores_grad, query)
        dqt_ref[pl.ds(base, HEAD_DIM), q0 : q0 + qn] = nn(
            kt_ref[pl.ds(base, HEAD_DIM), 0:extent], scores_grad
        )

    @pl.when(half == 1)
    def _():
        factor = 1.0 / HEAD_DIM**0.5
        q_ref[...] = (dqt_ref[...].T * factor).astype(B16)
        k_ref[...] = (dk_ref[...] * factor).astype(B16)
        v_ref[...] = dv_ref[...].astype(B16)
        for number in range(parts):
            source = pl.ds(place_of(scalars, parts, number, chunk), chunk)
            target = halves_of(outputs, number, chunk)
            target[:, 0:128] = q_ref[source, :]
            target[:, 128:256] = k_ref[source, :]
            target[:, 256:384] = v_ref[source, :]


def attend_back(scalars, row, projected, attended, grads, lse, pair):
    parts = len(projected)
    chunk, width = projected[0].shape
    pairs = width // 384
    slots = chunk * parts
    count = len(attended)
    rows = slots // count
    columns = []
    for kind in range(3):
        columns += [column(chunk, lambda h, s, kind=kind: (0, kind * pairs + pair))] * parts
    columns += [column(rows, lambda h, s: (0, pair))] * (2 * count)
    columns += [pl.BlockSpec((1, 1, slots), lambda h, s: (2 * pair + h, 0, 0))]
    return call(
        functools.partial(attend_back_kernel, row, chunk, parts, 384),
        "attend_back",
        scalars,
        [*projected, *projected, *projected, *attended, *grads, lse],
        [((rows, 384), B16)] * count,
        columns,
        [whole((rows, 384))] * count,
        (2,),
        [pltpu.VMEM((slots, 128), B16)] * 4
        + [pltpu.VMEM((128, slots), B16), pltpu.VMEM((8, slots), F32)]
        + [pltpu.VMEM((slots, 128), F32)] * 2
        + [pltpu.VMEM((128, slots), F32), pltpu.VMEM((slots, 128), F32)],
        limit=24,
        flops=10 * slots * slots * 128,
    )


def sum_of(terms):
    total = terms[0]
    for term in terms[1:]:
        total = total + term
    return total


def project_kernel(count, scalars, x_ref, *refs):
    for w_ref, out_ref in zip(refs[:count], refs[count:]):
        cols = w_ref.shape[2]
        for kind in range(3):
            columns = slice(kind * cols, kind * cols + cols)
            out_ref[:, columns] = nn(x_ref[...], w_ref[kind]).astype(B16)


def project(scalars, x, ws):
    rows, depth = x.shape
    cols = ws[0].shape[2]
    return call(
        functools.partial(project_kernel, len(ws)),
        "project",
        scalars,
        [x, *ws],
        [((rows, 3 * cols), B16)] * len(ws),
        flops=6 * rows * depth * cols * len(ws),
    )


def out_kernel(count, scalars, *refs):
    xs, ws, outs = refs[:count], refs[count : 2 * count], refs[2 * count :]
    n = outs[0].shape[0]
    for index, out in enumerate(outs):
        rows = slice(index * n, index * n + n)
        total = sum_of([nn(x[rows, :], w[...]) for x, w in zip(xs, ws)])
        out[...] = total.astype(out.dtype)


def partial_shapes(share, width, split):
    return [((share, width), F32)] + ([((share, width), B16)] if split else [])


def out_project(scalars, xs, ws):
    split = len(ws) == 2
    rows, depth = xs[0].shape
    width = ws[0].shape[1]
    return call(
        functools.partial(out_kernel, len(ws)),
        "out_project",
        scalars,
        [*xs, *ws],
        partial_shapes(rows // len(ws), width, split),
        flops=2 * rows * depth * width * len(ws),
    )


def feed_kernel(count, scalars, x_ref, *refs):
    ups, downs, refs = refs[:count], refs[count : 2 * count], refs[2 * count :]
    acts, slopes, out_ref = refs[:count], refs[count : 2 * count], refs[2 * count]
    for start, size in tiles(x_ref.shape[0], 272):
        rows = slice(start, start + size)
        terms = []
        for up, down, act_ref, slope_ref in zip(ups, downs, acts, slopes):
            hidden = nn(x_ref[rows, :], up[...])
            square = hidden * hidden
            bent = jnp.tanh(hidden * (gelu_scale + (gelu_scale * gelu_cubic) * square))
            upper = 0.5 + 0.5 * bent
            act = (hidden * upper).astype(B16)
            act_ref[rows, :] = act
            slope = upper + hidden * (1.0 - bent * bent) * (
                0.5 * gelu_scale + (1.5 * gelu_scale * gelu_cubic) * square
            )
            slope_ref[rows, :] = slope.astype(B16)
            terms.append(nn(act, down[...]))
        out_ref[rows, :] = sum_of(terms).astype(out_ref.dtype)


def feed(scalars, x, ups, downs, dtype):
    rows, depth = x.shape
    units, width = downs[0].shape
    count = len(ups)
    out = call(
        functools.partial(feed_kernel, count),
        "feed",
        scalars,
        [x, *ups, *downs],
        [((rows, units), B16)] * (2 * count) + [((rows, width), dtype)],
        limit=28,
        flops=4 * rows * depth * units * count,
    )
    return out[:count], out[count : 2 * count], out[2 * count]


def feed_back_kernel(count, scalars, x_ref, *refs):
    slopes, ups, downs = (refs[i * count : (i + 1) * count] for i in range(3))
    grads, out_ref = refs[3 * count : 4 * count], refs[4 * count]
    for start, size in tiles(x_ref.shape[0], 272):
        rows = slice(start, start + size)
        terms = []
        for slope, up, down, grad_ref in zip(slopes, ups, downs, grads):
            grad = nt(x_ref[rows, :], down[...]) * slope[rows, :].astype(F32)
            grad = grad.astype(B16)
            grad_ref[rows, :] = grad
            terms.append(nt(grad, up[...]))
        out_ref[rows, :] = sum_of(terms).astype(out_ref.dtype)


def feed_back(scalars, x, slopes, ups, downs, dtype):
    rows, width = x.shape
    depth, units = ups[0].shape
    count = len(ups)
    out = call(
        functools.partial(feed_back_kernel, count),
        "feed_back",
        scalars,
        [x, *slopes, *ups, *downs],
        [((rows, units), B16)] * count + [((rows, depth), dtype)],
        limit=28,
        flops=4 * rows * depth * units * count,
    )
    return out[:count], out[count]


def out_back_kernel(count, scalars, *refs):
    xs, ws, outs = refs[: len(refs) - 2 * count], refs[-2 * count : -count], refs[-count:]
    for w_ref, out_ref in zip(ws, outs):
        for index, x in enumerate(xs):
            n = x.shape[0]
            out_ref[index * n : index * n + n, :] = nt(x[...], w_ref[...]).astype(B16)


def out_back(scalars, xs, ws):
    rows, depth = len(xs) * xs[0].shape[0], xs[0].shape[1]
    cols = ws[0].shape[0]
    return call(
        functools.partial(out_back_kernel, len(ws)),
        "out_back",
        scalars,
        [*xs, *ws],
        [((rows, cols), B16)] * len(ws),
        flops=2 * rows * depth * cols * len(ws),
    )


def project_back_kernel(pairs, count, scalars, *refs):
    sides = [refs[i * pairs : (i + 1) * pairs] for i in range(count)]
    ws, outs = refs[pairs * count : (pairs + 1) * count], refs[(pairs + 1) * count :]
    n = outs[0].shape[0]
    for index, out in enumerate(outs):
        terms = []
        for grads, w_ref in zip(sides, ws):
            for kind in range(3):
                columns = [
                    grad[index * n : index * n + n, kind * 128 : kind * 128 + 128]
                    for grad in grads
                ]
                left = columns[0] if pairs == 1 else jnp.concatenate(columns, axis=1)
                terms.append(nt(left, w_ref[kind]))
        out[...] = sum_of(terms).astype(out.dtype)


def project_back(scalars, sides, ws):
    split = len(ws) == 2
    rows = sides[0][0].shape[0]
    depth, cols = ws[0].shape[1:]
    return call(
        functools.partial(project_back_kernel, len(sides[0]), len(ws)),
        "project_back",
        scalars,
        [v for side in sides for v in side] + list(ws),
        partial_shapes(rows // len(ws), depth, split),
        limit=24,
        flops=6 * rows * depth * cols * len(ws),
    )


def block_of(scalars, index, staged):
    if not staged:
        return index
    z = lax.rem(scalars[Z] + lax.rem(index, 4), 4)
    x = jnp.where(index < 4, scalars[X], 1 - scalars[X])
    return 4 * x + z


def outer_kernel(counts, staged, scalars, *refs):
    products = []
    for left_count, right_count in counts:
        products.append((refs[:left_count], refs[left_count : left_count + right_count]))
        refs = refs[left_count + right_count :]
    outs, refs = refs[: 2 if staged else 1], refs[2 if staged else 1 :]
    buffers = [(refs[2 * i], refs[2 * i + 1]) for i in range(len(products))]
    sems = refs[2 * len(products)]
    step = pl.program_id(0)

    @pl.when(step == 0)
    def _():
        copies = []
        for sources, targets in zip(products, buffers):
            for pieces, target in zip(sources, targets):
                start = 0
                for piece in pieces:
                    rows = piece.shape[0]
                    copies.append(
                        pltpu.make_async_copy(
                            piece, target.at[pl.ds(start, rows), :], sems.at[len(copies)]
                        )
                    )
                    start += rows
        for copy in copies:
            copy.start()
        for copy in copies:
            copy.wait()

    first = 0
    for left_ref, right_ref in buffers:
        if staged:
            spots = [block_of(scalars, 2 * step + i, True) for i in (0, 1)]
            columns = [pl.ds(pl.multiple_of(spot * 128, 128), 128) for spot in spots]
            left = jnp.concatenate([left_ref[:, c] for c in columns], axis=1)
        else:
            left = left_ref[:, pl.ds(pl.multiple_of(step * 256, 256), 256)]
        value = tn(left, right_ref[...]).astype(B16)
        lanes = slice(first, first + value.shape[1])
        if staged:

            @pl.when(step < 2)
            def _(value=value, lanes=lanes):
                outs[0][:, lanes] = value

            @pl.when(step >= 2)
            def _(value=value, lanes=lanes):
                outs[1][:, lanes] = value

        else:
            outs[0][:, lanes] = value
        first += value.shape[1]


def outer_sum(scalars, products, staged):
    inputs, counts, scratch = [], [], []
    height, width = products[0][0][0].shape[1], 0
    flops = 0
    for lefts, rights in products:
        slots = sum(left.shape[0] for left in lefts)
        inputs += [*lefts, *rights]
        counts.append((len(lefts), len(rights)))
        scratch += [pltpu.VMEM((slots, height), B16)]
        scratch += [pltpu.VMEM((slots, rights[0].shape[1]), B16)]
        width += rights[0].shape[1]
        flops += 2 * slots * height * rights[0].shape[1]
    if staged:
        outs = [((height // 2, width), B16)] * 2
        specs = [
            pl.BlockSpec((256, width), lambda i, s: (jnp.minimum(i, 1), 0)),
            pl.BlockSpec((256, width), lambda i, s: (jnp.maximum(i - 2, 0), 0)),
        ]
    else:
        outs = [((height, width), B16)]
        specs = [pl.BlockSpec((256, width), lambda i, s: (i, 0))]
    return call(
        functools.partial(outer_kernel, counts, staged),
        "outer_sum",
        scalars,
        inputs,
        outs,
        [anywhere() for _ in inputs],
        specs,
        (height // 256,),
        scratch + [pltpu.SemaphoreType.DMA((len(inputs),))],
        limit=24,
        flops=flops,
    )


def quarter_kernel(scalars, keep_ref, got_ref, *outs):
    rows = outs[0].shape[0]
    for index, out in enumerate(outs):
        at = slice(index * rows, index * rows + rows)
        out[...] = (keep_ref[at, :].astype(F32) + got_ref[at, :].astype(F32)).astype(B16)


def place_blocks(scalars, quarter, other):
    rows = quarter[0].shape[0]
    result = []
    for half in (0, 1):
        x = scalars[X] if half == 0 else 1 - scalars[X]
        for index in range(4):
            z = lax.rem(scalars[Z] + 4 - index, 4)
            at = slice(index * rows, index * rows + rows)
            value = quarter[index][...] if half == 0 else other[at, :]
            result.append((value, 4 * x + z))
    return result


def place_kernel(scalars, *refs):
    quarter, other, out_ref, buffer, sems = refs[:4], refs[4], refs[5], refs[6], refs[7]
    rows = quarter[0].shape[0]
    copies = []
    for index, (value, spot) in enumerate(place_blocks(scalars, quarter, other)):
        buffer[index] = value.astype(F32)
        target = out_ref.at[pl.ds(pl.multiple_of(spot * rows, rows), rows), :]
        copy = pltpu.make_async_copy(buffer.at[index], target, sems.at[index])
        copy.start()
        copies.append(copy)
    for copy in copies:
        copy.wait()


def place(scalars, quarter, other):
    rows, width = quarter[0].shape
    (out,) = call(
        place_kernel,
        "place",
        scalars,
        [*quarter, other],
        [((8 * rows, width), F32)],
        out_specs=[anywhere()],
        scratch=[pltpu.VMEM((8, rows, width), F32), pltpu.SemaphoreType.DMA((8,))],
    )
    return out


def place_heads_kernel(pair, has_out, aliased, scalars, *refs):
    quarter, other = refs[:4], refs[4]
    refs = refs[5 + aliased :]
    qkv_ref, refs = refs[0], refs[1:]
    if has_out:
        out_ref, buffer, turned, sems = refs
    else:
        buffer, sems = refs
    rows = quarter[0].shape[0]
    copies = []
    for index, (value, spot) in enumerate(place_blocks(scalars, quarter, other)):
        at = pl.ds(pl.multiple_of(spot * rows, rows), rows)
        for kind in range(3):
            buffer[kind, index] = value[:, kind * 128 : kind * 128 + 128].astype(F32)
            copies.append(
                pltpu.make_async_copy(
                    buffer.at[kind, index],
                    qkv_ref.at[kind, at, pl.ds(pair * 128, 128)],
                    sems.at[len(copies)],
                )
            )
            copies[-1].start()
        if has_out:
            turned[index] = value[:, 384:].astype(F32).T
            copies.append(
                pltpu.make_async_copy(turned.at[index], out_ref.at[:, at], sems.at[len(copies)])
            )
            copies[-1].start()
    for copy in copies:
        copy.wait()


def place_heads(scalars, quarter, other, pair, pairs, into):
    rows, width = quarter[0].shape
    has_out = width > 384
    inputs = [*quarter, other] + ([] if into is None else [into])
    in_specs = [whole(v.shape) for v in [*quarter, other]]
    in_specs += [] if into is None else [anywhere()]
    outs = [((3, 8 * rows, pairs * 128), F32)]
    scratch = [pltpu.VMEM((3, 8, rows, 128), F32)]
    if has_out:
        outs.append(((width - 384, 8 * rows), F32))
        scratch.append(pltpu.VMEM((8, width - 384, rows), F32))
    return call(
        functools.partial(place_heads_kernel, pair, has_out, int(into is not None)),
        "place_heads",
        scalars,
        inputs,
        outs,
        in_specs,
        [anywhere() for _ in outs],
        scratch=scratch + [pltpu.SemaphoreType.DMA((32,))],
        aliases={} if into is None else {6: 0},
    )


class DpSum:
    swap = [(i, i ^ 1) for i in range(8)]

    def __init__(self, scalars, order, keep, send):
        self.scalars, self.order, self.keep = scalars, order, keep
        self.got = lax.ppermute(send, "dp", self.swap)

    def shifted(self, value, steps):
        size = 8
        pairs = [(d, (d + 2 * steps) % size) for d in range(size)]
        return lax.ppermute(value, "dp", pairs)

    def scatter(self):
        (got,) = self.order.enter(self.got)
        rows, width = self.keep.shape
        self.own, *sent = call(
            quarter_kernel,
            "quarter",
            self.scalars,
            [self.keep, got],
            [((rows // 4, width), B16)] * 4,
        )
        self.order.leave(*sent)
        self.got = [self.shifted(v, s) for v, s in zip(sent, (1, 2, 3))]

    def collect(self):
        got = self.order.enter(*self.got)
        total = self.own.astype(F32)
        for piece in got:
            total = total + piece.astype(F32)
        total = total.astype(B16)
        self.order.leave(total)
        self.quarter = [total] + [self.shifted(total, s) for s in (1, 2, 3)]

    def spread(self):
        quarter = self.order.enter(*self.quarter)
        half = jnp.concatenate(quarter, axis=0)
        self.order.leave(half)
        self.other = lax.ppermute(half, "dp", self.swap)


class Order:
    def __init__(self):
        self.last = ()

    def enter(self, *values):
        return lax.optimization_barrier(tuple(values) + self.last)[: len(values)]

    def leave(self, *values):
        self.last = tuple(values)


def normalize(values):
    center = values - jnp.mean(values, axis=-1, keepdims=True)
    inverse = lax.rsqrt(jnp.mean(center * center, axis=-1, keepdims=True) + epsilon)
    return center * inverse, inverse


def values_back(grad, gain, vhat, inverse):
    scaled = grad * gain
    mean_scaled = jnp.mean(scaled, axis=-1, keepdims=True)
    mean_product = jnp.mean(scaled * vhat, axis=-1, keepdims=True)
    return (scaled - mean_scaled - vhat * mean_product) * inverse


def added(refs, rows):
    total = refs[0][rows, :].astype(F32)
    for ref in refs[1:]:
        total = total + ref[rows, :].astype(F32)
    return total


def fold(values):
    return jnp.sum(values.reshape(-1, 8, values.shape[-1]), axis=0)


def over_slots(share, width, sums, body):
    tile = 16 if share % 16 == 0 else 8
    totals = [jnp.zeros((8, width), F32)] * sums
    for start in range(0, share, tile):
        terms = body(pl.ds(start, tile), start, tile)
        totals = [total + fold(term) for total, term in zip(totals, terms)]
    return totals


def valid_rows(scalars, row, start, tile):
    slot = scalars[BASE] + start + lax.broadcasted_iota(jnp.int32, (tile, 1), 0)
    return (slot < scalars[LENGTH + row]).astype(F32)


def keep_sums(ref, totals):
    for index, total in enumerate(totals):
        ref[index : index + 1, :] = jnp.sum(total, axis=0, keepdims=True)


def first_kernel(scalars, x_ref, gains, biases, *outs):
    share, width = outs[0].shape
    for row, out in enumerate(outs):

        def body(rows, start, tile, row=row, out=out):
            vhat, _ = normalize(x_ref[row, rows, :].astype(F32))
            out[rows, :] = (vhat * gains[0:1, :] + biases[0:1, :]).astype(B16)
            return []

        over_slots(share, width, 0, body)


def middle_kernel(row, count, scalars, *refs):
    addends = refs[:count]
    x_ref, gains, biases, sum_ref, middle_ref, normed_ref, stat_ref = refs[count:]
    share, width = sum_ref.shape

    def body(rows, start, tile):
        attn_sum = added(addends, rows)
        sum_ref[rows, :] = attn_sum
        vhat, _ = normalize(attn_sum)
        branch = vhat * gains[1:2, :] + biases[1:2, :]
        middle = x_ref[0, rows, :].astype(F32) + branch
        middle_ref[rows, :] = middle
        vhat, _ = normalize(middle)
        normed_ref[rows, :] = (vhat * gains[2:3, :] + biases[2:3, :]).astype(B16)
        return [branch * branch * valid_rows(scalars, row, start, tile)]

    keep_sums(stat_ref, over_slots(share, width, 1, body))


def last_kernel(row, count, scalars, *refs):
    addends = refs[:count]
    middle_ref, cot_ref, gains, biases, out_ref, grad_ref, stat_ref = refs[count:]
    share, width = out_ref.shape

    def body(rows, start, tile):
        vhat, inverse = normalize(added(addends, rows))
        branch = vhat * gains[3:4, :] + biases[3:4, :]
        result = middle_ref[rows, :] + branch
        out_ref[rows, :] = result.astype(B16)
        valid = valid_rows(scalars, row, start, tile)
        out_grad = cot_ref[0, rows, :].astype(F32) * valid
        grad_ref[rows, :] = values_back(out_grad, gains[3:4, :], vhat, inverse).astype(B16)
        return [
            result * result * valid,
            branch * branch * valid,
            out_grad * vhat,
            out_grad,
        ]

    keep_sums(stat_ref, over_slots(share, width, 4, body))


def middle_back_kernel(row, count, scalars, *refs):
    addends = refs[:count]
    sum_ref, middle_ref, cot_ref, gains, carry_ref, grad_ref, stat_ref = refs[count:]
    share, width = sum_ref.shape

    def body(rows, start, tile):
        normed_grad = added(addends, rows)
        mhat, inverse = normalize(middle_ref[rows, :])
        out_grad = cot_ref[0, rows, :].astype(F32) * valid_rows(scalars, row, start, tile)
        carry = out_grad + values_back(normed_grad, gains[2:3, :], mhat, inverse)
        carry_ref[rows, :] = carry
        ahat, inverse = normalize(sum_ref[rows, :])
        grad_ref[rows, :] = values_back(carry, gains[1:2, :], ahat, inverse).astype(B16)
        return [normed_grad * mhat, normed_grad, carry * ahat, carry]

    keep_sums(stat_ref, over_slots(share, width, 4, body))


def first_back_kernel(row, count, scalars, *refs):
    addends = refs[:count]
    x_ref, carry_ref, gains, out_ref, stat_ref = refs[count:]
    share, width = out_ref.shape

    def body(rows, start, tile):
        grad = added(addends, rows)
        vhat, inverse = normalize(x_ref[0, rows, :].astype(F32))
        back = values_back(grad, gains[0:1, :], vhat, inverse)
        out_ref[rows, :] = (carry_ref[rows, :] + back).astype(B16)
        return [grad * vhat, grad]

    keep_sums(stat_ref, over_slots(share, width, 2, body))


def small_kernel(row_count, share, scalars, *refs):
    firsts, middles, lasts, backs = (
        refs[i * row_count : (i + 1) * row_count] for i in range(4)
    )
    out_ref = refs[4 * row_count]
    width = out_ref.shape[1]
    spots = ((firsts, 0), (backs, 2), (backs, 0), (lasts, 2))
    spots += ((firsts, 1), (backs, 3), (backs, 1), (lasts, 3))
    for index, (source, line) in enumerate(spots):
        total = source[0][line : line + 1, :]
        for ref in source[1:]:
            total = total + ref[line : line + 1, :]
        out_ref[index : index + 1, :] = total
    lane = lax.broadcasted_iota(jnp.int32, (1, width), 1)
    totals = [jnp.zeros((1, width), F32)] * GROUPS
    for row in range(row_count):
        count = jnp.clip(scalars[LENGTH + row] - scalars[BASE], 0, share).astype(F32)
        values = jnp.where(lane == 3, count, 0.0)
        sources = (lasts[row][0:1, :], middles[row][0:1, :], lasts[row][1:2, :])
        for index, source in enumerate(sources):
            values = jnp.where(lane == index, jnp.sum(source, axis=1, keepdims=True), values)
        group = scalars[LENGTH + row_count + row]
        for index in range(GROUPS):
            totals[index] = totals[index] + jnp.where(group == index, values, 0.0)
    for index, total in enumerate(totals):
        out_ref[8 + index : 9 + index, :] = total
    out_ref[12:16, :] = jnp.zeros((4, width), F32)


def swap_core(value):
    return lax.ppermute(value, "tensor", [(0, 1), (1, 0), (2, 3), (3, 2)])


def swap_chip(value):
    return lax.ppermute(value, "tensor", [(0, 2), (2, 0), (1, 3), (3, 1)])


class Row:
    def __init__(self, index, order, split, scalars, tokens, cotangent, gains, biases, pairs):
        self.index, self.order, self.split, self.scalars = index, order, split, scalars
        self.tokens, self.cotangent = tokens, cotangent
        self.gains, self.biases = gains, biases
        self.shape = tokens.shape[1:]
        self.projected, self.act, self.slope, self.hidden_grad = [], [], [], []
        self.projected_grad = [None] * pairs

    def gather(self, own):
        if self.split:
            return [own, swap_chip(own)]
        return [lax.all_gather(own, "tensor", axis=0, tiled=True)]

    def reduce(self, own, far):
        if self.split:
            return [own, swap_chip(far)]
        return [lax.psum_scatter(own, "tensor", scatter_dimension=0, tiled=True)]

    def both(self, pieces):
        return [*pieces, *[swap_core(v) for v in pieces]] if self.split else list(pieces)

    def mixed(self, pieces):
        first = [piece[0] for piece in pieces]
        return first + [swap_core(piece[1]) for piece in pieces] if self.split else first

    def over_row(self, kernel, name, inputs, outs):
        addends = self.order.enter(*self.addends)
        inputs = [*addends, *inputs]
        row = pl.BlockSpec((1, *self.shape), lambda i, s: (self.index, 0, 0))
        specs = [row if v.ndim == 3 else whole(v.shape) for v in inputs]
        return call(
            functools.partial(kernel, self.index, len(addends)),
            name,
            self.scalars,
            inputs,
            outs,
            specs,
        )

    def project(self, part, ws):
        (x,) = self.order.enter(self.attn_in[part])
        own, *other = project(self.scalars, x, ws)
        self.order.leave(own, *other)
        self.projected += [own, *[swap_core(v) for v in other]]

    def attend(self):
        projected = self.order.enter(*self.projected)
        *self.attended, self.lse = attend(self.scalars, self.index, projected)
        self.order.leave(*self.attended)
        self.heads = [self.attended[0]] + [swap_core(v) for v in self.attended[1:]]

    def out_project(self, ws):
        xs = self.order.enter(*self.heads)
        own, *far = out_project(self.scalars, xs, ws)
        self.order.leave(own, *far)
        self.addends = self.reduce(own, *(far or [None]))

    def middle(self):
        self.attn_sum, self.mid, normed, self.stat_middle = self.over_row(
            middle_kernel,
            "middle",
            [self.tokens, self.gains, self.biases],
            [(self.shape, F32)] * 2 + [(self.shape, B16), ((1, self.shape[1]), F32)],
        )
        self.order.leave(normed)
        self.ffn_in = self.gather(normed)

    def feed(self, part, ups, downs):
        (x,) = self.order.enter(self.ffn_in[part])
        act, slope, out = feed(self.scalars, x, ups, downs, B16 if part else F32)
        self.order.leave(out)
        self.act.append(act)
        self.slope.append(slope)
        if part == 0:
            self.own = out
        if part == len(self.ffn_in) - 1:
            self.addends = self.reduce(self.own, out)

    def last(self):
        self.output, grad, self.stat_last = self.over_row(
            last_kernel,
            "last",
            [self.mid, self.cotangent, self.gains, self.biases],
            [(self.shape, B16)] * 2 + [((4, self.shape[1]), F32)],
        )
        self.order.leave(grad)
        self.ffn_grad = self.gather(grad)

    def feed_back(self, part, ups, downs):
        (x,) = self.order.enter(self.ffn_grad[part])
        grad, out = feed_back(
            self.scalars, x, self.slope[part], ups, downs, B16 if part else F32
        )
        self.order.leave(out)
        self.hidden_grad.append(grad)
        if part == 0:
            self.own = out
        if part == len(self.ffn_grad) - 1:
            self.addends = self.reduce(self.own, out)

    def middle_back(self):
        self.carry, grad, self.stat_back = self.over_row(
            middle_back_kernel,
            "middle_back",
            [self.attn_sum, self.mid, self.cotangent, self.gains],
            [(self.shape, F32), (self.shape, B16), ((4, self.shape[1]), F32)],
        )
        self.order.leave(grad)
        self.attn_grad = self.gather(grad)

    def out_back(self, ws):
        xs = self.order.enter(*self.attn_grad)
        own, *other = out_back(self.scalars, xs, ws)
        self.order.leave(own, *other)
        self.attended_grad = [own] + [swap_core(v) for v in other]

    def attend_back(self, pair):
        grads = self.order.enter(*self.attended_grad)
        out = attend_back(
            self.scalars, self.index, self.projected, self.attended, grads, self.lse, pair
        )
        self.projected_grad[pair] = out
        self.order.leave(*out)

    def project_back(self, ws):
        sides = [[grad[0] for grad in self.projected_grad]]
        if self.split:
            sides.append([swap_core(grad[1]) for grad in self.projected_grad])
        flat = self.order.enter(*[v for side in sides for v in side])
        pairs = len(self.projected_grad)
        sides = [flat[i * pairs : (i + 1) * pairs] for i in range(len(sides))]
        own, *far = project_back(self.scalars, sides, ws)
        self.order.leave(own, *far)
        self.addends = self.reduce(own, *(far or [None]))

    def first_back(self):
        self.input_grad, self.stat_first = self.over_row(
            first_back_kernel,
            "first_back",
            [self.tokens, self.carry, self.gains],
            [(self.shape, B16), ((2, self.shape[1]), F32)],
        )
        self.order.leave(self.input_grad)


def doubling(values, axis, step):
    size = lax.axis_size(axis)
    return values + lax.ppermute(values, axis, [(i, i ^ step) for i in range(size)])


def per_device(tokens, cotangent, lengths, groups, w_qkv, w_out, w_up, w_down, gains, biases):
    row_count, share, width = tokens.shape
    t_size, d_size = lax.axis_size("tensor"), lax.axis_size("dp")
    pairs = w_qkv.shape[2] // 128
    split = t_size == 4 and share % 16 == 0
    staged = d_size == 8
    t, d = lax.axis_index("tensor"), lax.axis_index("dp")
    both = lambda w: [w, swap_core(w)] if split else [w]
    qkvs = [w.transpose(1, 0, 2) for w in both(w_qkv)]
    outs, ups, downs = both(w_out), both(w_up), both(w_down)
    parts = range(2 if split else 1)
    spots = jnp.stack([t * share, t, d // 2, d % 2]).astype(jnp.int32)
    scalars = jnp.concatenate([spots, lengths, groups])
    order = Order()
    rows = [
        Row(r, order, split, scalars, tokens, cotangent, gains, biases, pairs)
        for r in range(row_count)
    ]
    normed = call(
        first_kernel,
        "first",
        scalars,
        [tokens, gains, biases],
        [((share, width), B16)] * row_count,
    )
    order.leave(*normed)
    for row, own in zip(rows, normed):
        row.attn_in = row.gather(own)

    def outer(*products):
        flat = [v for lefts, rights in products for v in (*lefts, *rights)]
        values = list(order.enter(*flat))
        again = []
        for lefts, rights in products:
            taken, values = values[: len(lefts) + len(rights)], values[len(lefts) + len(rights) :]
            again.append((taken[: len(lefts)], taken[len(lefts) :]))
        return again

    def both_cores(name):
        return [v for row in rows for v in row.both(getattr(row, name))]

    def own_columns(name):
        return [v for row in rows for v in row.mixed(getattr(row, name))]

    def listed(values):
        return [v for value in values for v in value]

    def summed(products, manual=True):
        products = outer(*products)
        out = outer_sum(scalars, products, staged and manual)
        order.leave(*out)
        if staged and manual:
            return DpSum(scalars, order, *out)
        return out[0] if staged is False else lax.psum(out[0], "dp")

    lead, *others = rows
    lead.project(0, qkvs)
    for row in others:
        row.project(0, qkvs)
    if split:
        lead.project(1, qkvs)
    lead.attend()
    if split:
        for row in others:
            row.project(1, qkvs)
    lead.out_project(outs)
    for row in others:
        row.attend()
    lead.middle()
    for row in others:
        row.out_project(outs)
    lead.feed(0, ups, downs)
    if split:
        lead.feed(1, ups, downs)
    for row in others:
        row.middle()
        row.feed(0, ups, downs)
    lead.last()
    lead.feed_back(0, ups, downs)
    if split:
        for row in others:
            row.feed(1, ups, downs)
    if split:
        lead.feed_back(1, ups, downs)
    for row in others:
        row.last()
        row.feed_back(0, ups, downs)
    lead.middle_back()
    if split:
        for row in others:
            row.feed_back(1, ups, downs)
    grad_down = summed([(own_columns("act"), both_cores("ffn_grad"))], manual=False)
    lead.out_back(outs)
    for row in others:
        row.middle_back()
    up = summed([(both_cores("ffn_in"), own_columns("hidden_grad"))])
    lead.attend_back(0)
    for row in others:
        row.out_back(outs)
    if staged:
        up.scatter()
    for row in others:
        row.attend_back(0)

    attn_in = both_cores("attn_in")

    def qkv_product(pair):
        return (attn_in, listed(row.projected_grad[pair] for row in rows))

    attended = listed(row.attended for row in rows)
    heads = [summed([qkv_product(0), (both_cores("attn_grad"), attended)])]
    if staged:
        up.collect()
    for pair in range(1, pairs):
        lead.attend_back(pair)
        if staged:
            heads[0].scatter()
        if pair == pairs - 1:
            lead.project_back(qkvs)
        if staged:
            up.spread()
        for row in others:
            row.attend_back(pair)
        heads.append(summed([qkv_product(pair)]))
    if pairs == 1:
        lead.project_back(qkvs)
    for row in others:
        row.project_back(qkvs)
    if staged:
        heads[0].collect()
    lead.first_back()
    if staged:
        (grad_down,) = order.enter(grad_down)
        grad_down = grad_down.astype(F32)
        order.leave(grad_down)
        for total in heads[1:]:
            total.scatter()
        heads[0].spread()
        (got,) = order.enter(up.other)
        grad_up = place(scalars, up.quarter, got)
        order.leave(grad_up)
    for row in others:
        row.first_back()
    if staged:
        for total in heads[1:]:
            total.collect()
    stats = [row.stat_first for row in rows] + [row.stat_middle for row in rows]
    stats += [row.stat_last for row in rows] + [row.stat_back for row in rows]
    (small,) = call(
        functools.partial(small_kernel, row_count, share),
        "small",
        scalars,
        list(order.enter(*stats)),
        [((16, width), F32)],
    )
    order.leave(small)
    steps = [("tensor", 1 << i) for i in range(t_size.bit_length() - 1)]
    steps += [("dp", 1 << i) for i in range(d_size.bit_length() - 1)]
    powers = t_size & (t_size - 1) == 0 and d_size & (d_size - 1) == 0
    if powers:
        for axis, step in steps[:2]:
            small = doubling(small, axis, step)
        steps = steps[2:]
    if staged:
        (got,) = order.enter(heads[0].other)
        grad_qkv, grad_out = place_heads(scalars, heads[0].quarter, got, 0, pairs, None)
        order.leave(grad_out)
        for total in heads[1:]:
            total.spread()
    if powers:
        for axis, step in steps:
            small = doubling(small, axis, step)
    else:
        small = lax.psum(small, ("dp", "tensor"))
    if staged:
        for pair in range(1, pairs):
            (grad_qkv,) = place_heads(
                scalars, heads[pair].quarter, heads[pair].other, pair, pairs, grad_qkv
            )
        grad_qkv = grad_qkv.transpose(1, 0, 2)
    else:
        grad_down, grad_up, *blocks = [
            v.astype(F32) for v in lax.psum((grad_down, up, *heads), "dp")
        ]
        grad_out = blocks[0][:, 384:].T
        blocks = [grad[:, :384].reshape(width, 3, 128) for grad in blocks]
        grad_qkv = jnp.concatenate(blocks, axis=2)
    sums = small[8 : 8 + GROUPS]
    group_rms = jnp.sqrt(sums[:, :3] / (sums[:, 3:4] * width))
    return (
        jnp.stack([row.output for row in rows]),
        jnp.stack([row.input_grad for row in rows]),
        grad_qkv,
        grad_out,
        grad_up,
        grad_down.astype(F32),
        small[:4],
        small[4:8],
        group_rms,
    )


def solution(mesh):
    placed = (
        P("dp", "tensor", None),
        P("dp", "tensor", None),
        P("dp"),
        P("dp"),
        P(None, None, "tensor"),
        P("tensor", None),
        P(None, "tensor"),
        P("tensor", None),
        P(),
        P(),
    )
    return jax.shard_map(
        per_device,
        mesh=mesh,
        in_specs=placed,
        out_specs=(
            P("dp", "tensor", None),
            P("dp", "tensor", None),
            P(None, None, "tensor"),
            P("tensor", None),
            P(None, "tensor"),
            P("tensor", None),
            P(),
            P(),
            P(),
        ),
        check_vma=False,
    )
```

time: 1240 us -> 486 us (0.39)
  waiting for transfers between devices: 769 us -> 194 us
  matrix products: 183 us -> 0 us
  Pallas kernels: 0 us -> 154 us
  other arithmetic: 108 us -> 8.85 us
  starting transfers between devices: 0.76 us -> 68.2 us
  local copies, waits for them, and re-layouts: 94.3 us -> 40 us
  blocking collectives: 42.8 us -> 0 us
  loops' own time: 22.4 us -> 0 us
    psum x1, waiting for transfers between devices: 356 us -> 24.4 us  [summed(): return out[0] if staged is False else lax.psum(out[0], 'dp')]
    reduce_scatter x4 -> x0, waiting for transfers between devices: 269 us -> none  [the longest x1 75.2 us: per_device(): lax.psum_scatter(matmul_back(hidden_grad16, w_up), 'tensor', scatter_dime...]
    dot_general x42 -> x0, matrix products: 183 us -> none  [the longest x8 36.4 us: masked_scores(): jnp.einsum('qhd,khd->hqk', query_block, key_row, preferred_element_type=j...]
    ppermute x0 -> x85, waiting for transfers between devices: none -> 169 us  [the longest x16 104 us: swap_chip(): return lax.ppermute(value, 'tensor', [(0, 2), (2, 0), (1, 3), (3, 1)])]
    pallas_call x0 -> x44, Pallas kernels: none -> 154 us  [call(): pl.pallas_call(kernel, out_shape=[jax.ShapeDtypeStruct(shape, dtype) for...]
    all_gather x4 -> x0, waiting for transfers between devices: 144 us -> none  [the longest x1 36.1 us: per_device(): attn_full = lax.all_gather(attn_in16, 'tensor', axis=1, tiled=True)]
    ppermute x0 -> x85, starting transfers between devices: none -> 68.2 us  [the longest x18 29 us: shifted(): return lax.ppermute(value, 'dp', pairs)]
    convert_element_type x11 -> x4, other arithmetic: 53.1 us -> 5.73 us  [the longest x1 4.14 us: per_device(): grad_down = grad_down.astype(F32)]
  transfers between devices with their start and end apart: 9 -> 86, of which waited for: 9 -> 33; matrix products, arithmetic and copies ran while one was open for 3% -> 3% of each run, Pallas kernels for 0% -> 32%
where the time goes in v2:
time: 486 us; the launch traced here: 481 us
  waiting for transfers between devices  194 us (40%)
  Pallas kernels  154 us (32%)
  starting transfers between devices  68.2 us (14%)
  local copies, waits for them, and re-layouts  40 us (8%)
  between operations  16.1 us (3%)
  other arithmetic  8.85 us (2%)
    pallas_call x44, Pallas kernels, call(): pl.pallas_call(kernel, out_shape=[jax.ShapeDtypeStruct(shape, dtype) for...  154 us
    ppermute x16, waiting for transfers between devices, swap_chip(): return lax.ppermute(value, 'tensor', [(0, 2), (2, 0), (1, 3), (3, 1)])  104 us
    unnamed x310, local copies, waits for them, and re-layouts  37.9 us
    ppermute x18, starting transfers between devices, shifted(): return lax.ppermute(value, 'dp', pairs)  29 us
    ppermute x18, waiting for transfers between devices, shifted(): return lax.ppermute(value, 'dp', pairs)  25.9 us
    psum x1, waiting for transfers between devices, summed(): return out[0] if staged is False else lax.psum(out[0], 'dp')  24.4 us
    ppermute x3, waiting for transfers between devices, __init__(): self.got = lax.ppermute(send, 'dp', self.swap)  22.7 us
    ppermute x16, starting transfers between devices, swap_chip(): return lax.ppermute(value, 'tensor', [(0, 2), (2, 0), (1, 3), (3, 1)])  22.4 us
  transfers between devices with their start and end apart: 86, of which 33 were waited for; matrix products, arithmetic and copies ran while one was open for 3% of the time, Pallas kernels for 32%

profile of v2, /device:TPU:0, one launch (start us, length us, event | category | flops | bytes accessed | tf_op | source)
XLA Modules:
  0.0 481.2 jit_solution(18056899560251462181)
XLA Ops:
  23.2 6.2 %collective-permute-done.2.x_ref.refs_1_ = bf16[272,1024]{1,0:T(8,128)(2,1)S(1)} collective-permute-done((bf16[272,1024]{1,0:T(8,128)(2,1)}, bf16[272,1024]{1,0:T(8,128)(2,1)S(1)}, u32[]{:S(2)}, u32[]{:S(2)}) %collective-permute-start.2) | collective-permute-done | bytes 557088 | tf_op jit(solution)/shard_map/ppermute | solution.py:866
  33.4 8.3 %attend.2 = (bf16[544,256]{1,0:T(8,128)(2,1)S(1)}, bf16[544,256]{1,0:T(8,128)(2,1)S(1)}, f32[4,1,1088]{2,1,0:T(1,128)S(1)}) custom-call(s32[8]{0:T(128)S(1)} %concatenate.12.scalars, bf16[272,768]{1,0:T(8,128)(2,1)S(1)} %get-tuple-element.295.refs_0_.refs_4_.refs_8_, bf16[272,768]{1,0:T(8,128)(2,1)S(1)} %collective-permute-done.1.refs_1_.refs_5_.refs_9_, ...), custom_call_target="tpu_custom_call" | custom-call | flops 75759616 | bytes 156672 | tf_op jit(solution)/shard_map/attend/pallas_call | solution.py:66
  42.3 4.1 collective-permute-done.5.x_ref.refs_5_
  53.6 8.0 %attend.3 = (bf16[544,256]{1,0:T(8,128)(2,1)S(1)}, bf16[544,256]{1,0:T(8,128)(2,1)S(1)}, f32[4,1,1088]{2,1,0:T(1,128)S(1)}) custom-call(s32[8]{0:T(128)S(1)} %concatenate.12.scalars, bf16[272,768]{1,0:T(8,128)(2,1)S(1)} %get-tuple-element.308.refs_0_.refs_4_.refs_8_, bf16[272,768]{1,0:T(8,128)(2,1)S(1)} %collective-permute-done.8.refs_1_.refs_5_.refs_9_, ...), custom_call_target="tpu_custom_call" | custom-call | flops 75759616 | bytes 156672 | tf_op jit(solution)/shard_map/attend/pallas_call | solution.py:66
  68.2 3.5 feed.4
  71.8 8.6 %collective-permute-done.13.x_ref.refs_1_ = bf16[272,1024]{1,0:T(8,128)(2,1)S(1)} collective-permute-done((bf16[272,1024]{1,0:T(8,128)(2,1)S(1)}, bf16[272,1024]{1,0:T(8,128)(2,1)S(1)}, u32[]{:S(2)}, u32[]{:S(2)}) %collective-permute-start.13) | collective-permute-done | bytes 557088 | tf_op jit(solution)/shard_map/ppermute | solution.py:866
  85.7 6.6 %collective-permute-done.15.refs_1_ = bf16[272,1024]{1,0:T(8,128)(2,1)S(1)} collective-permute-done((bf16[272,1024]{1,0:T(8,128)(2,1)S(1)}, bf16[272,1024]{1,0:T(8,128)(2,1)S(1)}, u32[]{:S(2)}, u32[]{:S(2)}) %collective-permute-start.15) | collective-permute-done | bytes 557088 | tf_op jit(solution)/shard_map/ppermute | solution.py:866
  112.2 4.0 collective-permute-done.16.x_ref.refs_5_
  122.1 6.0 %collective-permute-done.18.x_ref.refs_9_ = bf16[272,1024]{1,0:T(8,128)(2,1)S(1)} collective-permute-done((bf16[272,1024]{1,0:T(8,128)(2,1)S(1)}, bf16[272,1024]{1,0:T(8,128)(2,1)S(1)}, u32[]{:S(2)}, u32[]{:S(2)}) %collective-permute-start.18) | collective-permute-done | bytes 557088 | tf_op jit(solution)/shard_map/ppermute | solution.py:866
  128.1 9.9 %collective-permute-done.17.refs_1_ = bf16[272,1024]{1,0:T(8,128)(2,1)S(1)} collective-permute-done((bf16[272,1024]{1,0:T(8,128)(2,1)S(1)}, bf16[272,1024]{1,0:T(8,128)(2,1)S(1)}, u32[]{:S(2)}, u32[]{:S(2)}) %collective-permute-start.17) | collective-permute-done | bytes 557088 | tf_op jit(solution)/shard_map/ppermute | solution.py:866
  147.0 12.8 %collective-permute-done.19.refs_1_ = bf16[272,1024]{1,0:T(8,128)(2,1)S(1)} collective-permute-done((bf16[272,1024]{1,0:T(8,128)(2,1)S(1)}, bf16[272,1024]{1,0:T(8,128)(2,1)S(1)}, u32[]{:S(2)}, u32[]{:S(2)}) %collective-permute-start.19) | collective-permute-done | bytes 557088 | tf_op jit(solution)/shard_map/ppermute | solution.py:866
  159.9 11.0 %collective-permute-done.27.x_ref.refs_13_ = bf16[272,1024]{1,0:T(8,128)(2,1)S(1)} collective-permute-done((bf16[272,1024]{1,0:T(8,128)(2,1)S(1)}, bf16[272,1024]{1,0:T(8,128)(2,1)S(1)}, u32[]{:S(2)}, u32[]{:S(2)}) %collective-permute-start.27) | collective-permute-done | bytes 557088 | tf_op jit(solution)/shard_map/ppermute | solution.py:866
  184.8 8.1 %collective-permute-done.20.refs_1_.refs_13_ = bf16[272,1024]{1,0:T(8,128)(2,1)S(1)} collective-permute-done((bf16[272,1024]{1,0:T(8,128)(2,1)S(1)}, bf16[272,1024]{1,0:T(8,128)(2,1)S(1)}, u32[]{:S(2)}, u32[]{:S(2)}) %collective-permute-start.20) | collective-permute-done | bytes 557088 | tf_op jit(solution)/shard_map/ppermute | solution.py:866
  193.7 10.7 %collective-permute-done.39.refs_1_ = bf16[272,1024]{1,0:T(8,128)(2,1)S(1)} collective-permute-done((bf16[272,1024]{1,0:T(8,128)(2,1)S(1)}, bf16[272,1024]{1,0:T(8,128)(2,1)S(1)}, u32[]{:S(2)}, u32[]{:S(2)}) %collective-permute-start.39) | collective-permute-done | bytes 557088 | tf_op jit(solution)/shard_map/ppermute | solution.py:866
  205.3 7.8 %outer_sum.4 = bf16[1024,1024]{1,0:T(8,128)(2,1)S(1)} custom-call(s32[8]{0:T(128)S(1)} %concatenate.12.scalars, bf16[272,1024]{1,0:T(8,128)(2,1)S(1)} %get-tuple-element.370.refs_0_, bf16[272,1024]{1,0:T(8,128)(2,1)S(1)} %get-tuple-element.371.refs_1_, bf16[272,1024]{1,0:T(8,128)(2,1)S(1)} %collective-permute-done.21.refs_2_, ...), custom_call_target="tpu_custom_call" | custom-call | flops 285212672 | bytes 278528 | tf_op jit(solution)/shard_map/outer_sum/pallas_call | solution.py:66
  231.5 9.0 %outer_sum.5 = (bf16[512,1024]{1,0:T(8,128)(2,1)S(1)}, bf16[512,1024]{1,0:T(8,128)(2,1)S(1)}) custom-call(s32[8]{0:T(128)S(1)} %concatenate.12.scalars, bf16[272,1024]{1,0:T(8,128)(2,1)S(1)} %copy-done.61, bf16[272,1024]{1,0:T(8,128)(2,1)S(1)} %copy-done.63, bf16[272,1024]{1,0:T(8,128)(2,1)S(1)} %copy-done.115, bf16[272,1024]{1,0:T(8,128)(2,1)S(1)} %copy-done.121, ...), custom_call_target="tpu_custom_call" | custom-call | flops 285212672 | bytes 278528 | tf_op jit(solution)/shard_map/outer_sum/pallas_call | solution.py:66
  245.5 11.9 %collective-permute-done.41.refs_1_.refs_17_ = bf16[272,1024]{1,0:T(8,128)(2,1)S(1)} collective-permute-done((bf16[272,1024]{1,0:T(8,128)(2,1)S(1)}, bf16[272,1024]{1,0:T(8,128)(2,1)S(1)}, u32[]{:S(2)}, u32[]{:S(2)}) %collective-permute-start.41) | collective-permute-done | bytes 557088 | tf_op jit(solution)/shard_map/ppermute | solution.py:866
  257.4 6.7 %attend_back.4 = (bf16[544,384]{1,0:T(8,128)(2,1)S(1)}, bf16[544,384]{1,0:T(8,128)(2,1)S(1)}) custom-call(s32[8]{0:T(128)S(1)} %concatenate.12.scalars, bf16[272,768]{1,0:T(8,128)(2,1)S(1)} %copy-done.17, bf16[272,768]{1,0:T(8,128)(2,1)S(1)} %copy-done.26, bf16[272,768]{1,0:T(8,128)(2,1)S(1)} %copy-done.20, bf16[272,768]{1,0:T(8,128)(2,1)S(1)} %copy-done.23, ...), custom_call_target="tpu_custom_call" | custom-call | flops 94699520 | bytes 191760 | tf_op jit(solution)/shard_map/attend_back/pallas_call | solution.py:66
  273.2 7.1 %attend_back.5 = (bf16[544,384]{1,0:T(8,128)(2,1)S(1)}, bf16[544,384]{1,0:T(8,128)(2,1)S(1)}) custom-call(s32[8]{0:T(128)S(1)} %concatenate.12.scalars, bf16[272,768]{1,0:T(8,128)(2,1)S(1)} %copy-done.5, bf16[272,768]{1,0:T(8,128)(2,1)S(1)} %copy-done.11, bf16[272,768]{1,0:T(8,128)(2,1)S(1)} %copy-done.8, bf16[272,768]{1,0:T(8,128)(2,1)S(1)} %copy-done.14, ...), custom_call_target="tpu_custom_call" | custom-call | flops 94699520 | bytes 191760 | tf_op jit(solution)/shard_map/attend_back/pallas_call | solution.py:66
  280.4 11.4 %outer_sum.6 = (bf16[512,640]{1,0:T(8,128)(2,1)S(1)}, bf16[512,640]{1,0:T(8,128)(2,1)}) custom-call(s32[8]{0:T(128)S(1)} %concatenate.12.scalars, bf16[272,1024]{1,0:T(8,128)(2,1)} %get-tuple-element.491.x_ref.refs_0_, bf16[272,1024]{1,0:T(8,128)(2,1)S(1)} %copy-done.42, bf16[272,1024]{1,0:T(8,128)(2,1)} %collective-permute-done.45.refs_2_, ...), custom_call_target="tpu_custom_call" | custom-call | flops 178257920 | bytes 365568 | tf_op jit(solution)/shard_map/outer_sum/pallas_call | solution.py:66
  300.8 6.7 %attend_back.6 = (bf16[544,384]{1,0:T(8,128)(2,1)S(1)}, bf16[544,384]{1,0:T(8,128)(2,1)S(1)}) custom-call(s32[8]{0:T(128)S(1)} %concatenate.12.scalars, bf16[272,768]{1,0:T(8,128)(2,1)S(1)} %copy-done.18, bf16[272,768]{1,0:T(8,128)(2,1)S(1)} %copy-done.27, bf16[272,768]{1,0:T(8,128)(2,1)S(1)} %copy-done.21, bf16[272,768]{1,0:T(8,128)(2,1)S(1)} %copy-done.24, ...), custom_call_target="tpu_custom_call" | custom-call | flops 94699520 | bytes 191760 | tf_op jit(solution)/shard_map/attend_back/pallas_call | solution.py:66
  310.7 6.2 %collective-permute-done.56.got_ref = bf16[512,640]{1,0:T(8,128)(2,1)} collective-permute-done((bf16[512,640]{1,0:T(8,128)(2,1)}, bf16[512,640]{1,0:T(8,128)(2,1)}, u32[]{:S(2)}, u32[]{:S(2)}) %collective-permute-start.56) | collective-permute-done | bytes 655392 | tf_op jit(solution)/shard_map/ppermute | solution.py:655
  323.0 18.0 %collective-permute-done.62.refs_2_ = bf16[128,1024]{1,0:T(8,128)(2,1)S(1)} collective-permute-done((bf16[128,1024]{1,0:T(8,128)(2,1)S(1)}, bf16[128,1024]{1,0:T(8,128)(2,1)S(1)}, u32[]{:S(2)}, u32[]{:S(2)}) %collective-permute-start.62) | collective-permute-done | bytes 262176 | tf_op jit(solution)/shard_map/ppermute | solution.py:660
  344.1 6.9 %attend_back.7 = (bf16[544,384]{1,0:T(8,128)(2,1)S(1)}, bf16[544,384]{1,0:T(8,128)(2,1)S(1)}) custom-call(s32[8]{0:T(128)S(1)} %concatenate.12.scalars, bf16[272,768]{1,0:T(8,128)(2,1)S(1)} %copy-done.6, bf16[272,768]{1,0:T(8,128)(2,1)S(1)} %copy-done.12, bf16[272,768]{1,0:T(8,128)(2,1)S(1)} %copy-done.9, bf16[272,768]{1,0:T(8,128)(2,1)S(1)} %copy-done.15, ...), custom_call_target="tpu_custom_call" | custom-call | flops 94699520 | bytes 191760 | tf_op jit(solution)/shard_map/attend_back/pallas_call | solution.py:66
  351.1 6.0 %collective-permute-start.58 = (bf16[128,640]{1,0:T(8,128)(2,1)S(1)}, bf16[128,640]{1,0:T(8,128)(2,1)S(1)}, u32[]{:S(2)}, u32[]{:S(2)}) collective-permute-start(bf16[128,640]{1,0:T(8,128)(2,1)S(1)} %get-tuple-element.473), channel_id=1, source_target_pairs={{0,8},{4,12},{8,16},{12,20},{16,24},{20,28},{24,0},{28,4},{1,9},{5... | collective-permute-start | bytes 491528 | tf_op jit(solution)/shard_map/ppermute | solution.py:660
  360.0 4.5 collective-permute-done.58
  365.5 5.7 %outer_sum.7 = (bf16[512,384]{1,0:T(8,128)(2,1)S(1)}, bf16[512,384]{1,0:T(8,128)(2,1)S(1)}) custom-call(s32[8]{0:T(128)S(1)} %concatenate.12.scalars, bf16[272,1024]{1,0:T(8,128)(2,1)} %get-tuple-element.491.x_ref.refs_0_, bf16[272,1024]{1,0:T(8,128)(2,1)S(1)} %copy-done.43, bf16[272,1024]{1,0:T(8,128)(2,1)} %collective-permute-done.45.refs_2_, ...), custom_call_target="tpu_custom_call" | custom-call | flops 106954752 | bytes 191488 | tf_op jit(solution)/shard_map/outer_sum/pallas_call | solution.py:66
  379.7 15.9 %collective-permute-done.71.got_ref = bf16[512,384]{1,0:T(8,128)(2,1)S(1)} collective-permute-done((bf16[512,384]{1,0:T(8,128)(2,1)S(1)}, bf16[512,384]{1,0:T(8,128)(2,1)S(1)}, u32[]{:S(2)}, u32[]{:S(2)}) %collective-permute-start.71) | collective-permute-done | bytes 393248 | tf_op jit(solution)/shard_map/ppermute | solution.py:655
  400.1 24.4 %all-reduce.2.cloned.1.call-done = bf16[1024,1024]{1,0:T(8,128)(2,1)} async-done(((bf16[1024,1024]{1,0:T(8,128)(2,1)}), bf16[1024,1024]{1,0:T(8,128)(2,1)}) %all-reduce.2.cloned.1.call-update) | async-done | bytes 2097168 | tf_op jit(solution)/shard_map/psum | solution.py:1073
  424.5 4.1 convert_element_type.58
  434.6 3.9 place.1
  462.6 4.7 collective-permute-done.84
  (513 shorter events, 196.3 us)
Async XLA Ops:
  7.2 417.3 %all-reduce.2.cloned.1.call-start = ((), (), s32[]{:S(2)}) async-start(), calls=%async_computation | async-start | bytes 4194304 | tf_op jit(solution)/shard_map/psum | solution.py:1073
  15.9 52.2 %collective-permute-start.11 = (bf16[1024,1024]{1,0:T(8,128)(2,1)}, bf16[1024,1024]{1,0:T(8,128)(2,1)S(1)}, u32[]{:S(2)}, u32[]{:S(2)}) collective-permute-start(bf16[1024,1024]{1,0:T(8,128)(2,1)} %refs_2_.27), channel_id=1, source_target_pairs={{0,1},{1,0},{2,3},{3,2},{4,5},{5,4},{6,7},{7,6},{8,9},{9,8},{10,11... | collective-permute-start | bytes 6291464 | tf_op jit(solution)/shard_map/ppermute | solution.py:862
  16.1 52.1 %collective-permute-start.12 = (bf16[1024,1024]{1,0:T(8,128)(2,1)}, bf16[1024,1024]{1,0:T(8,128)(2,1)S(1)}, u32[]{:S(2)}, u32[]{:S(2)}) collective-permute-start(bf16[1024,1024]{1,0:T(8,128)(2,1)} %refs_4_.20), channel_id=1, source_target_pairs={{0,1},{1,0},{2,3},{3,2},{4,5},{5,4},{6,7},{7,6},{8,9},{9,8},{10,11... | collective-permute-start | bytes 6291464 | tf_op jit(solution)/shard_map/ppermute | solution.py:862
  67.8 24.5 %collective-permute-start.15 = (bf16[272,1024]{1,0:T(8,128)(2,1)S(1)}, bf16[272,1024]{1,0:T(8,128)(2,1)S(1)}, u32[]{:S(2)}, u32[]{:S(2)}) collective-permute-start(bf16[272,1024]{1,0:T(8,128)(2,1)S(1)} %get-tuple-element.320), channel_id=1, source_target_pairs={{0,2},{2,0},{1,3},{3,1},{4,6},{6,4},{5,7},{7,5},{8,10},{10,8},{9,1... | collective-permute-start | bytes 1671176 | tf_op jit(solution)/shard_map/ppermute | solution.py:866
  97.1 24.5 %collective-permute-start.21 = (bf16[272,1024]{1,0:T(8,128)(2,1)S(1)}, bf16[272,1024]{1,0:T(8,128)(2,1)S(1)}, u32[]{:S(2)}, u32[]{:S(2)}) collective-permute-start(bf16[272,1024]{1,0:T(8,128)(2,1)S(1)} %get-tuple-element.360), channel_id=1, source_target_pairs={{0,1},{1,0},{2,3},{3,2},{4,5},{5,4},{6,7},{7,6},{8,9},{9,8},{10,11... | collective-permute-start | bytes 1671176 | tf_op jit(solution)/shard_map/ppermute | solution.py:862
  97.1 25.0 %collective-permute-start.31 = (bf16[272,1024]{1,0:T(8,128)(2,1)S(1)}, bf16[272,1024]{1,0:T(8,128)(2,1)S(1)}, u32[]{:S(2)}, u32[]{:S(2)}) collective-permute-start(bf16[272,1024]{1,0:T(8,128)(2,1)S(1)} %get-tuple-element.402.x_ref.refs_0_), channel_id=1, source_target_pairs={{0,1},{1,0},{2,3},{3,2},{4,5},{5,4},{6,7},{7,6},{8,9},{9,8},{10,11... | collective-permute-start | bytes 1671176 | tf_op jit(solution)/shard_map/ppermute | solution.py:862
  145.5 25.4 %collective-permute-start.27 = (bf16[272,1024]{1,0:T(8,128)(2,1)S(1)}, bf16[272,1024]{1,0:T(8,128)(2,1)S(1)}, u32[]{:S(2)}, u32[]{:S(2)}) collective-permute-start(bf16[272,1024]{1,0:T(8,128)(2,1)S(1)} %get-tuple-element.382.x_ref.refs_12_), channel_id=1, source_target_pairs={{0,2},{2,0},{1,3},{3,1},{4,6},{6,4},{5,7},{7,5},{8,10},{10,8},{9,1... | collective-permute-start | bytes 1671176 | tf_op jit(solution)/shard_map/ppermute | solution.py:866
  146.4 31.0 %collective-permute-start.35 = (bf16[272,1024]{1,0:T(8,128)(2,1)S(1)}, bf16[272,1024]{1,0:T(8,128)(2,1)S(1)}, u32[]{:S(2)}, u32[]{:S(2)}) collective-permute-start(bf16[272,1024]{1,0:T(8,128)(2,1)S(1)} %get-tuple-element.392), channel_id=1, source_target_pairs={{0,1},{1,0},{2,3},{3,2},{4,5},{5,4},{6,7},{7,6},{8,9},{9,8},{10,11... | collective-permute-start | bytes 1671176 | tf_op jit(solution)/shard_map/ppermute | solution.py:862
  146.4 36.0 %collective-permute-start.34 = (bf16[272,1024]{1,0:T(8,128)(2,1)S(1)}, bf16[272,1024]{1,0:T(8,128)(2,1)S(1)}, u32[]{:S(2)}, u32[]{:S(2)}) collective-permute-start(bf16[272,1024]{1,0:T(8,128)(2,1)S(1)} %collective-permute-done.16.x_ref.refs_5_), channel_id=1, source_target_pairs={{0,1},{1,0},{2,3},{3,2},{4,5},{5,4},{6,7},{7,6},{8,9},{9,8},{10,11... | collective-permute-start | bytes 1671176 | tf_op jit(solution)/shard_map/ppermute | solution.py:862
  146.9 37.2 %collective-permute-start.28 = (bf16[272,1024]{1,0:T(8,128)(2,1)S(1)}, bf16[272,1024]{1,0:T(8,128)(2,1)S(1)}, u32[]{:S(2)}, u32[]{:S(2)}) collective-permute-start(bf16[272,1024]{1,0:T(8,128)(2,1)S(1)} %get-tuple-element.382.x_ref.refs_12_), channel_id=1, source_target_pairs={{0,1},{1,0},{2,3},{3,2},{4,5},{5,4},{6,7},{7,6},{8,9},{9,8},{10,11... | collective-permute-start | bytes 1671176 | tf_op jit(solution)/shard_map/ppermute | solution.py:862
  159.9 24.3 %collective-permute-start.26 = (bf16[272,1024]{1,0:T(8,128)(2,1)S(1)}, bf16[272,1024]{1,0:T(8,128)(2,1)S(1)}, u32[]{:S(2)}, u32[]{:S(2)}) collective-permute-start(bf16[272,1024]{1,0:T(8,128)(2,1)S(1)} %collective-permute-done.18.x_ref.refs_9_), channel_id=1, source_target_pairs={{0,1},{1,0},{2,3},{3,2},{4,5},{5,4},{6,7},{7,6},{8,9},{9,8},{10,11... | collective-permute-start | bytes 1671176 | tf_op jit(solution)/shard_map/ppermute | solution.py:862
  184.2 44.0 %collective-permute-start.37 = (bf16[272,1024]{1,0:T(8,128)(2,1)}, bf16[272,1024]{1,0:T(8,128)(2,1)}, u32[]{:S(2)}, u32[]{:S(2)}) collective-permute-start(bf16[272,1024]{1,0:T(8,128)(2,1)} %get-tuple-element.396), channel_id=1, source_target_pairs={{0,1},{1,0},{2,3},{3,2},{4,5},{5,4},{6,7},{7,6},{8,9},{9,8},{10,11... | collective-permute-start | bytes 1671176 | tf_op jit(solution)/shard_map/ppermute | solution.py:862
  184.2 44.0 %collective-permute-start.36 = (bf16[272,1024]{1,0:T(8,128)(2,1)}, bf16[272,1024]{1,0:T(8,128)(2,1)}, u32[]{:S(2)}, u32[]{:S(2)}) collective-permute-start(bf16[272,1024]{1,0:T(8,128)(2,1)} %get-tuple-element.393), channel_id=1, source_target_pairs={{0,1},{1,0},{2,3},{3,2},{4,5},{5,4},{6,7},{7,6},{8,9},{9,8},{10,11... | collective-permute-start | bytes 1671176 | tf_op jit(solution)/shard_map/ppermute | solution.py:862
  184.7 43.4 %collective-permute-start.38 = (bf16[272,1024]{1,0:T(8,128)(2,1)}, bf16[272,1024]{1,0:T(8,128)(2,1)}, u32[]{:S(2)}, u32[]{:S(2)}) collective-permute-start(bf16[272,1024]{1,0:T(8,128)(2,1)} %get-tuple-element.397), channel_id=1, source_target_pairs={{0,1},{1,0},{2,3},{3,2},{4,5},{5,4},{6,7},{7,6},{8,9},{9,8},{10,11... | collective-permute-start | bytes 1671176 | tf_op jit(solution)/shard_map/ppermute | solution.py:862
  193.7 48.9 %collective-permute-start.47 = (bf16[272,1024]{1,0:T(8,128)(2,1)}, bf16[272,1024]{1,0:T(8,128)(2,1)}, u32[]{:S(2)}, u32[]{:S(2)}) collective-permute-start(bf16[272,1024]{1,0:T(8,128)(2,1)} %get-tuple-element.495.x_ref.refs_4_), channel_id=1, source_target_pairs={{0,1},{1,0},{2,3},{3,2},{4,5},{5,4},{6,7},{7,6},{8,9},{9,8},{10,11... | collective-permute-start | bytes 1671176 | tf_op jit(solution)/shard_map/ppermute | solution.py:862
  205.3 38.4 %collective-permute-start.45 = (bf16[272,1024]{1,0:T(8,128)(2,1)}, bf16[272,1024]{1,0:T(8,128)(2,1)}, u32[]{:S(2)}, u32[]{:S(2)}) collective-permute-start(bf16[272,1024]{1,0:T(8,128)(2,1)} %get-tuple-element.491.x_ref.refs_0_), channel_id=1, source_target_pairs={{0,1},{1,0},{2,3},{3,2},{4,5},{5,4},{6,7},{7,6},{8,9},{9,8},{10,11... | collective-permute-start | bytes 1671176 | tf_op jit(solution)/shard_map/ppermute | solution.py:862
  240.5 25.6 %collective-permute-start.40 = (bf16[512,1024]{1,0:T(8,128)(2,1)S(1)}, bf16[512,1024]{1,0:T(8,128)(2,1)S(1)}, u32[]{:S(2)}, u32[]{:S(2)}) collective-permute-start(bf16[512,1024]{1,0:T(8,128)(2,1)S(1)} %get-tuple-element.419), channel_id=1, source_target_pairs={{0,4},{4,0},{8,12},{12,8},{16,20},{20,16},{24,28},{28,24},{1,5},{5... | collective-permute-start | bytes 3145736 | tf_op jit(solution)/shard_map/ppermute | solution.py:655
  244.8 24.5 %collective-permute-start.52 = (bf16[272,1024]{1,0:T(8,128)(2,1)S(1)}, bf16[272,1024]{1,0:T(8,128)(2,1)S(1)}, u32[]{:S(2)}, u32[]{:S(2)}) collective-permute-start(bf16[272,1024]{1,0:T(8,128)(2,1)S(1)} %get-tuple-element.455.refs_0_.refs_16_), channel_id=1, source_target_pairs={{0,1},{1,0},{2,3},{3,2},{4,5},{5,4},{6,7},{7,6},{8,9},{9,8},{10,11... | collective-permute-start | bytes 1671176 | tf_op jit(solution)/shard_map/ppermute | solution.py:862
  245.2 35.2 %collective-permute-start.51 = (bf16[272,1024]{1,0:T(8,128)(2,1)S(1)}, bf16[272,1024]{1,0:T(8,128)(2,1)S(1)}, u32[]{:S(2)}, u32[]{:S(2)}) collective-permute-start(bf16[272,1024]{1,0:T(8,128)(2,1)S(1)} %copy-done.77), channel_id=1, source_target_pairs={{0,1},{1,0},{2,3},{3,2},{4,5},{5,4},{6,7},{7,6},{8,9},{9,8},{10,11... | collective-permute-start | bytes 1671176 | tf_op jit(solution)/shard_map/ppermute | solution.py:862
  267.7 26.7 %collective-permute-start.42 = (bf16[128,1024]{1,0:T(8,128)(2,1)}, bf16[128,1024]{1,0:T(8,128)(2,1)}, u32[]{:S(2)}, u32[]{:S(2)}) collective-permute-start(bf16[128,1024]{1,0:T(8,128)(2,1)} %get-tuple-element.431), channel_id=1, source_target_pairs={{0,8},{4,12},{8,16},{12,20},{16,24},{20,28},{24,0},{28,4},{1,9},{5... | collective-permute-start | bytes 786440 | tf_op jit(solution)/shard_map/ppermute | solution.py:660
  269.3 25.1 %collective-permute-start.43 = (bf16[128,1024]{1,0:T(8,128)(2,1)}, bf16[128,1024]{1,0:T(8,128)(2,1)}, u32[]{:S(2)}, u32[]{:S(2)}) collective-permute-start(bf16[128,1024]{1,0:T(8,128)(2,1)} %get-tuple-element.432), channel_id=1, source_target_pairs={{0,16},{4,20},{8,24},{12,28},{16,0},{20,4},{24,8},{28,12},{1,17},{... | collective-permute-start | bytes 786440 | tf_op jit(solution)/shard_map/ppermute | solution.py:660
  292.7 24.2 %collective-permute-start.56 = (bf16[512,640]{1,0:T(8,128)(2,1)}, bf16[512,640]{1,0:T(8,128)(2,1)}, u32[]{:S(2)}, u32[]{:S(2)}) collective-permute-start(bf16[512,640]{1,0:T(8,128)(2,1)} %get-tuple-element.464), channel_id=1, source_target_pairs={{0,4},{4,0},{8,12},{12,8},{16,20},{20,16},{24,28},{28,24},{1,5},{5... | collective-permute-start | bytes 1966088 | tf_op jit(solution)/shard_map/ppermute | solution.py:655
  294.3 24.9 %collective-permute-start.54 = (bf16[544,384]{1,0:T(8,128)(2,1)}, bf16[544,384]{1,0:T(8,128)(2,1)S(1)}, u32[]{:S(2)}, u32[]{:S(2)}) collective-permute-start(bf16[544,384]{1,0:T(8,128)(2,1)} %copy-done.142), channel_id=1, source_target_pairs={{0,1},{1,0},{2,3},{3,2},{4,5},{5,4},{6,7},{7,6},{8,9},{9,8},{10,11... | collective-permute-start | bytes 1253384 | tf_op jit(solution)/shard_map/ppermute | solution.py:862
  309.1 31.9 %collective-permute-start.62 = (bf16[128,1024]{1,0:T(8,128)(2,1)S(1)}, bf16[128,1024]{1,0:T(8,128)(2,1)S(1)}, u32[]{:S(2)}, u32[]{:S(2)}) collective-permute-start(bf16[128,1024]{1,0:T(8,128)(2,1)S(1)} %add_convert_fusion.refs_0_), channel_id=1, source_target_pairs={{0,16},{4,20},{8,24},{12,28},{16,0},{20,4},{24,8},{28,12},{1,17},{... | collective-permute-start | bytes 786440 | tf_op jit(solution)/shard_map/ppermute | solution.py:660
  316.9 24.2 %collective-permute-start.63 = (bf16[128,1024]{1,0:T(8,128)(2,1)S(1)}, bf16[128,1024]{1,0:T(8,128)(2,1)S(1)}, u32[]{:S(2)}, u32[]{:S(2)}) collective-permute-start(bf16[128,1024]{1,0:T(8,128)(2,1)S(1)} %add_convert_fusion.refs_0_), channel_id=1, source_target_pairs={{0,24},{4,28},{8,0},{12,4},{16,8},{20,12},{24,16},{28,20},{1,25},{... | collective-permute-start | bytes 786440 | tf_op jit(solution)/shard_map/ppermute | solution.py:660
  319.2 39.9 %collective-permute-start.64 = (bf16[544,384]{1,0:T(8,128)(2,1)S(1)}, bf16[544,384]{1,0:T(8,128)(2,1)S(1)}, u32[]{:S(2)}, u32[]{:S(2)}) collective-permute-start(bf16[544,384]{1,0:T(8,128)(2,1)S(1)} %copy-done.141), channel_id=1, source_target_pairs={{0,1},{1,0},{2,3},{3,2},{4,5},{5,4},{6,7},{7,6},{8,9},{9,8},{10,11... | collective-permute-start | bytes 1253384 | tf_op jit(solution)/shard_map/ppermute | solution.py:862
  357.1 40.1 %collective-permute-start.57 = (bf16[272,1024]{1,0:T(8,128)(2,1)S(1)}, bf16[272,1024]{1,0:T(8,128)(2,1)S(1)}, u32[]{:S(2)}, u32[]{:S(2)}) collective-permute-start(bf16[272,1024]{1,0:T(8,128)(2,1)S(1)} %get-tuple-element.481), channel_id=1, source_target_pairs={{0,2},{2,0},{1,3},{3,1},{4,6},{6,4},{5,7},{7,5},{8,10},{10,8},{9,1... | collective-permute-start | bytes 1671176 | tf_op jit(solution)/shard_map/ppermute | solution.py:866
  358.3 75.3 %collective-permute-start.67 = (bf16[512,1024]{1,0:T(8,128)(2,1)}, bf16[512,1024]{1,0:T(8,128)(2,1)}, u32[]{:S(2)}, u32[]{:S(2)}) collective-permute-start(bf16[512,1024]{1,0:T(8,128)(2,1)} %constant_dynamic-update-slice_fusion), channel_id=1, source_target_pairs={{0,4},{4,0},{8,12},{12,8},{16,20},{20,16},{24,28},{28,24},{1,5},{5... | collective-permute-start | bytes 3145736 | tf_op jit(solution)/shard_map/ppermute | solution.py:688
  376.9 52.4 %collective-permute-start.68 = (bf16[128,640]{1,0:T(8,128)(2,1)S(1)}, bf16[128,640]{1,0:T(8,128)(2,1)S(1)}, u32[]{:S(2)}, u32[]{:S(2)}) collective-permute-start(bf16[128,640]{1,0:T(8,128)(2,1)S(1)} %add_convert_fusion.1.refs_0_), channel_id=1, source_target_pairs={{0,8},{4,12},{8,16},{12,20},{16,24},{20,28},{24,0},{28,4},{1,9},{5... | collective-permute-start | bytes 491528 | tf_op jit(solution)/shard_map/ppermute | solution.py:660
  378.0 52.2 %collective-permute-start.69 = (bf16[128,640]{1,0:T(8,128)(2,1)S(1)}, bf16[128,640]{1,0:T(8,128)(2,1)S(1)}, u32[]{:S(2)}, u32[]{:S(2)}) collective-permute-start(bf16[128,640]{1,0:T(8,128)(2,1)S(1)} %add_convert_fusion.1.refs_0_), channel_id=1, source_target_pairs={{0,16},{4,20},{8,24},{12,28},{16,0},{20,4},{24,8},{28,12},{1,17},{... | collective-permute-start | bytes 491528 | tf_op jit(solution)/shard_map/ppermute | solution.py:660
  396.4 36.3 %collective-permute-start.70 = (bf16[128,640]{1,0:T(8,128)(2,1)S(1)}, bf16[128,640]{1,0:T(8,128)(2,1)S(1)}, u32[]{:S(2)}, u32[]{:S(2)}) collective-permute-start(bf16[128,640]{1,0:T(8,128)(2,1)S(1)} %add_convert_fusion.1.refs_0_), channel_id=1, source_target_pairs={{0,24},{4,28},{8,0},{12,4},{16,8},{20,12},{24,16},{28,20},{1,25},{... | collective-permute-start | bytes 491528 | tf_op jit(solution)/shard_map/ppermute | solution.py:660
  397.2 41.3 %collective-permute-start.66 = (bf16[272,1024]{1,0:T(8,128)(2,1)}, bf16[272,1024]{1,0:T(8,128)(2,1)}, u32[]{:S(2)}, u32[]{:S(2)}) collective-permute-start(bf16[272,1024]{1,0:T(8,128)(2,1)} %get-tuple-element.510), channel_id=1, source_target_pairs={{0,2},{2,0},{1,3},{3,1},{4,6},{6,4},{5,7},{7,5},{8,10},{10,8},{9,1... | collective-permute-start | bytes 1671176 | tf_op jit(solution)/shard_map/ppermute | solution.py:866
  (206 other events, 2195.7 us)
Sparse Core Ops, SparseCore 0:
  294.4 130.0 all-reduce.1

commit v3 on v2

--- a/solution.py
+++ b/solution.py
@@ -58,7 +58,7 @@
     return pl.BlockSpec(memory_space=pl.ANY)
 
 
-def call(kernel, name, scalars, inputs, outs, in_specs=None, out_specs=None, grid=(1,), scratch=(), limit=20, flops=0, aliases={}):
+def call(kernel, name, scalars, inputs, outs, in_specs=None, out_specs=None, grid=(1,), scratch=(), limit=10, flops=0, aliases={}):
     values = sum(v.size for v in inputs)
     in_specs = in_specs or [once(v.shape) for v in inputs]
     out_specs = out_specs or [whole(shape) for shape, _ in outs]
@@ -167,7 +167,7 @@
         (pairs,),
         [pltpu.VMEM((slots, 128), B16)] * 3
         + [pltpu.VMEM((128, slots), B16), pltpu.VMEM((128, slots), F32)],
-        limit=24,
+        limit=14,
         flops=4 * slots * slots * 128 * pairs,
     )
 
@@ -265,7 +265,7 @@
         + [pltpu.VMEM((128, slots), B16), pltpu.VMEM((8, slots), F32)]
         + [pltpu.VMEM((slots, 128), F32)] * 2
         + [pltpu.VMEM((128, slots), F32), pltpu.VMEM((slots, 128), F32)],
-        limit=24,
+        limit=14,
         flops=10 * slots * slots * 128,
     )
 
@@ -356,7 +356,7 @@
         scalars,
         [x, *ups, *downs],
         [((rows, units), B16)] * (2 * count) + [((rows, width), dtype)],
-        limit=28,
+        limit=18,
         flops=4 * rows * depth * units * count,
     )
     return out[:count], out[count : 2 * count], out[2 * count]
@@ -386,7 +386,7 @@
         scalars,
         [x, *slopes, *ups, *downs],
         [((rows, units), B16)] * count + [((rows, depth), dtype)],
-        limit=28,
+        limit=18,
         flops=4 * rows * depth * units * count,
     )
     return out[:count], out[count]
@@ -440,7 +440,7 @@
         scalars,
         [v for side in sides for v in side] + list(ws),
         partial_shapes(rows // len(ws), depth, split),
-        limit=24,
+        limit=12,
         flops=6 * rows * depth * cols * len(ws),
     )
 
@@ -453,72 +453,53 @@
     return 4 * x + z
 
 
-def outer_kernel(counts, staged, scalars, *refs):
-    products = []
-    for left_count, right_count in counts:
-        products.append((refs[:left_count], refs[left_count : left_count + right_count]))
-        refs = refs[left_count + right_count :]
-    outs, refs = refs[: 2 if staged else 1], refs[2 if staged else 1 :]
-    buffers = [(refs[2 * i], refs[2 * i + 1]) for i in range(len(products))]
-    sems = refs[2 * len(products)]
+def gathered(pieces, target, sems, first):
+    copies, start = [], 0
+    for index, piece in enumerate(pieces):
+        rows = piece.shape[0]
+        spot = target.at[pl.ds(start, rows), :]
+        copies.append(pltpu.make_async_copy(piece, spot, sems.at[first + index]))
+        start += rows
+    return copies
+
+
+def outer_kernel(count, staged, scalars, *refs):
+    lefts, rights = refs[:count], refs[count : 2 * count]
+    outs, (left_ref, right_ref, sems) = refs[2 * count : -3], refs[-3:]
     step = pl.program_id(0)
 
     @pl.when(step == 0)
     def _():
-        copies = []
-        for sources, targets in zip(products, buffers):
-            for pieces, target in zip(sources, targets):
-                start = 0
-                for piece in pieces:
-                    rows = piece.shape[0]
-                    copies.append(
-                        pltpu.make_async_copy(
-                            piece, target.at[pl.ds(start, rows), :], sems.at[len(copies)]
-                        )
-                    )
-                    start += rows
+        copies = gathered(lefts, left_ref, sems, 0) + gathered(rights, right_ref, sems, count)
         for copy in copies:
             copy.start()
         for copy in copies:
             copy.wait()
 
-    first = 0
-    for left_ref, right_ref in buffers:
-        if staged:
-            spots = [block_of(scalars, 2 * step + i, True) for i in (0, 1)]
-            columns = [pl.ds(pl.multiple_of(spot * 128, 128), 128) for spot in spots]
-            left = jnp.concatenate([left_ref[:, c] for c in columns], axis=1)
-        else:
-            left = left_ref[:, pl.ds(pl.multiple_of(step * 256, 256), 256)]
-        value = tn(left, right_ref[...]).astype(B16)
-        lanes = slice(first, first + value.shape[1])
-        if staged:
-
-            @pl.when(step < 2)
-            def _(value=value, lanes=lanes):
-                outs[0][:, lanes] = value
-
-            @pl.when(step >= 2)
-            def _(value=value, lanes=lanes):
-                outs[1][:, lanes] = value
-
-        else:
-            outs[0][:, lanes] = value
-        first += value.shape[1]
-
-
-def outer_sum(scalars, products, staged):
-    inputs, counts, scratch = [], [], []
-    height, width = products[0][0][0].shape[1], 0
-    flops = 0
-    for lefts, rights in products:
-        slots = sum(left.shape[0] for left in lefts)
-        inputs += [*lefts, *rights]
-        counts.append((len(lefts), len(rights)))
-        scratch += [pltpu.VMEM((slots, height), B16)]
-        scratch += [pltpu.VMEM((slots, rights[0].shape[1]), B16)]
-        width += rights[0].shape[1]
-        flops += 2 * slots * height * rights[0].shape[1]
+    if staged:
+        spots = [block_of(scalars, 2 * step + i, True) for i in (0, 1)]
+        columns = [pl.ds(pl.multiple_of(spot * 128, 128), 128) for spot in spots]
+        left = jnp.concatenate([left_ref[:, c] for c in columns], axis=1)
+    else:
+        left = left_ref[:, pl.ds(pl.multiple_of(step * 256, 256), 256)]
+    value = tn(left, right_ref[...]).astype(B16)
+    if staged:
+
+        @pl.when(step < 2)
+        def _():
+            outs[0][...] = value
+
+        @pl.when(step >= 2)
+        def _():
+            outs[1][...] = value
+
+    else:
+        outs[0][...] = value
+
+
+def outer_sum(scalars, lefts, rights, staged):
+    slots = sum(left.shape[0] for left in lefts)
+    height, width = lefts[0].shape[1], rights[0].shape[1]
     if staged:
         outs = [((height // 2, width), B16)] * 2
         specs = [
@@ -528,8 +509,9 @@
     else:
         outs = [((height, width), B16)]
         specs = [pl.BlockSpec((256, width), lambda i, s: (i, 0))]
+    inputs = [*lefts, *rights]
     return call(
-        functools.partial(outer_kernel, counts, staged),
+        functools.partial(outer_kernel, len(lefts), staged),
         "outer_sum",
         scalars,
         inputs,
@@ -537,8 +519,73 @@
         [anywhere() for _ in inputs],
         specs,
         (height // 256,),
-        scratch + [pltpu.SemaphoreType.DMA((len(inputs),))],
-        limit=24,
+        [pltpu.VMEM((slots, height), B16), pltpu.VMEM((slots, width), B16)]
+        + [pltpu.SemaphoreType.DMA((len(inputs),))],
+        limit=18,
+        flops=2 * slots * height * width,
+    )
+
+
+def head_outer_kernel(counts, staged, scalars, *refs):
+    products = []
+    for left_count, right_count in counts:
+        products.append((refs[:left_count], refs[left_count : left_count + right_count]))
+        refs = refs[left_count + right_count :]
+    outs, refs = refs[: 2 if staged else 1], refs[2 if staged else 1 :]
+    buffers = [(refs[2 * i], refs[2 * i + 1]) for i in range(len(products))]
+    total_ref, sems = refs[2 * len(products) :]
+    step = pl.program_id(0)
+
+    @pl.when(step == 0)
+    def _():
+        copies = []
+        for sources, targets in zip(products, buffers):
+            for pieces, target in zip(sources, targets):
+                copies += gathered(pieces, target, sems, len(copies))
+        for copy in copies:
+            copy.start()
+        for copy in copies:
+            copy.wait()
+
+    first = 0
+    for left_ref, right_ref in buffers:
+        right = right_ref[:, pl.ds(pl.multiple_of(step * 256, 256), 256)]
+        height = left_ref.shape[1]
+        total_ref[first : first + height, :] = tn(left_ref[...], right).astype(B16)
+        first += height
+    if staged:
+        rows = total_ref.shape[0] // 8
+        for index in range(8):
+            source = pl.ds(pl.multiple_of(block_of(scalars, index, True) * rows, 16), rows)
+            at = index % 4 * rows
+            outs[index // 4][at : at + rows, :] = total_ref[source, :]
+    else:
+        outs[0][...] = total_ref[...]
+
+
+def head_outer(scalars, products, staged):
+    inputs, counts, scratch = [], [], []
+    height, width, flops = 0, products[0][1][0].shape[1], 0
+    for lefts, rights in products:
+        slots = sum(left.shape[0] for left in lefts)
+        inputs += [*lefts, *rights]
+        counts.append((len(lefts), len(rights)))
+        scratch += [pltpu.VMEM((slots, lefts[0].shape[1]), B16)]
+        scratch += [pltpu.VMEM((slots, width), B16)]
+        height += lefts[0].shape[1]
+        flops += 2 * slots * lefts[0].shape[1] * width
+    parts = 2 if staged else 1
+    return call(
+        functools.partial(head_outer_kernel, counts, staged),
+        "head_outer",
+        scalars,
+        inputs,
+        [((height // parts, width), B16)] * parts,
+        [anywhere() for _ in inputs],
+        [pl.BlockSpec((height // parts, 256), lambda i, s: (0, i))] * parts,
+        (width // 256,),
+        scratch + [pltpu.VMEM((height, 256), B16), pltpu.SemaphoreType.DMA((len(inputs),))],
+        limit=20,
         flops=flops,
     )
 
@@ -595,45 +642,36 @@
     quarter, other = refs[:4], refs[4]
     refs = refs[5 + aliased :]
     qkv_ref, refs = refs[0], refs[1:]
+    out_ref, (rows_ref, buffer, sems) = refs[0] if has_out else None, refs[-3:]
+    rows = quarter[0].shape[0]
+    for value, spot in place_blocks(scalars, quarter, other):
+        rows_ref[pl.ds(pl.multiple_of(spot * rows, 16), rows), :] = value.astype(F32)
+    copies = []
     if has_out:
-        out_ref, buffer, turned, sems = refs
-    else:
-        buffer, sems = refs
-    rows = quarter[0].shape[0]
-    copies = []
-    for index, (value, spot) in enumerate(place_blocks(scalars, quarter, other)):
-        at = pl.ds(pl.multiple_of(spot * rows, rows), rows)
-        for kind in range(3):
-            buffer[kind, index] = value[:, kind * 128 : kind * 128 + 128].astype(F32)
-            copies.append(
-                pltpu.make_async_copy(
-                    buffer.at[kind, index],
-                    qkv_ref.at[kind, at, pl.ds(pair * 128, 128)],
-                    sems.at[len(copies)],
-                )
+        copies.append(
+            pltpu.make_async_copy(
+                rows_ref.at[pl.ds(384, rows_ref.shape[0] - 384), :], out_ref, sems.at[3]
             )
-            copies[-1].start()
-        if has_out:
-            turned[index] = value[:, 384:].astype(F32).T
-            copies.append(
-                pltpu.make_async_copy(turned.at[index], out_ref.at[:, at], sems.at[len(copies)])
-            )
-            copies[-1].start()
+        )
+        copies[-1].start()
+    for kind in range(3):
+        buffer[kind] = rows_ref[kind * 128 : kind * 128 + 128, :].T
+        target = qkv_ref.at[kind, :, pl.ds(pair * 128, 128)]
+        copies.append(pltpu.make_async_copy(buffer.at[kind], target, sems.at[kind]))
+        copies[-1].start()
     for copy in copies:
         copy.wait()
 
 
 def place_heads(scalars, quarter, other, pair, pairs, into):
     rows, width = quarter[0].shape
-    has_out = width > 384
+    total = 8 * rows
+    has_out = total > 384
     inputs = [*quarter, other] + ([] if into is None else [into])
-    in_specs = [whole(v.shape) for v in [*quarter, other]]
+    in_specs = [once(v.shape) for v in [*quarter, other]]
     in_specs += [] if into is None else [anywhere()]
-    outs = [((3, 8 * rows, pairs * 128), F32)]
-    scratch = [pltpu.VMEM((3, 8, rows, 128), F32)]
-    if has_out:
-        outs.append(((width - 384, 8 * rows), F32))
-        scratch.append(pltpu.VMEM((8, width - 384, rows), F32))
+    outs = [((3, width, pairs * 128), F32)]
+    outs += [((total - 384, width), F32)] if has_out else []
     return call(
         functools.partial(place_heads_kernel, pair, has_out, int(into is not None)),
         "place_heads",
@@ -642,7 +680,11 @@
         outs,
         in_specs,
         [anywhere() for _ in outs],
-        scratch=scratch + [pltpu.SemaphoreType.DMA((32,))],
+        scratch=[
+            pltpu.VMEM((total, width), F32),
+            pltpu.VMEM((3, width, 128), F32),
+            pltpu.SemaphoreType.DMA((4,)),
+        ],
         aliases={} if into is None else {6: 0},
     )
 
@@ -653,50 +695,61 @@
     def __init__(self, scalars, order, keep, send):
         self.scalars, self.order, self.keep = scalars, order, keep
         self.got = lax.ppermute(send, "dp", self.swap)
-
-    def shifted(self, value, steps):
-        size = 8
-        pairs = [(d, (d + 2 * steps) % size) for d in range(size)]
-        return lax.ppermute(value, "dp", pairs)
-
-    def scatter(self):
-        (got,) = self.order.enter(self.got)
+        self.steps = self.run()
+
+    def shifted(self, value):
+        return lax.ppermute(value, "dp", [(d, (d + 2) % 8) for d in range(8)])
+
+    def run(self):
+        order = self.order
+        (got,) = order.enter(self.got)
         rows, width = self.keep.shape
-        self.own, *sent = call(
+        blocks = call(
             quarter_kernel,
             "quarter",
             self.scalars,
             [self.keep, got],
             [((rows // 4, width), B16)] * 4,
         )
-        self.order.leave(*sent)
-        self.got = [self.shifted(v, s) for v, s in zip(sent, (1, 2, 3))]
-
-    def collect(self):
-        got = self.order.enter(*self.got)
-        total = self.own.astype(F32)
-        for piece in got:
-            total = total + piece.astype(F32)
-        total = total.astype(B16)
-        self.order.leave(total)
-        self.quarter = [total] + [self.shifted(total, s) for s in (1, 2, 3)]
-
-    def spread(self):
-        quarter = self.order.enter(*self.quarter)
-        half = jnp.concatenate(quarter, axis=0)
-        self.order.leave(half)
+        order.leave(*blocks)
+        got = self.shifted(blocks[3])
+        yield
+        for block in (blocks[2], blocks[1], blocks[0]):
+            (got,) = order.enter(got)
+            total = (block.astype(F32) + got.astype(F32)).astype(B16)
+            order.leave(total)
+            got = self.shifted(total)
+            yield
+        self.quarter = [total]
+        for _ in range(2):
+            (got,) = order.enter(got)
+            order.leave(got)
+            self.quarter.append(got)
+            got = self.shifted(got)
+            yield
+        (got,) = order.enter(got)
+        self.quarter.append(got)
+        half = jnp.concatenate(self.quarter, axis=0)
+        order.leave(half)
         self.other = lax.ppermute(half, "dp", self.swap)
 
 
 class Order:
     def __init__(self):
-        self.last = ()
+        self.last, self.fresh, self.due = (), (), ()
 
     def enter(self, *values):
-        return lax.optimization_barrier(tuple(values) + self.last)[: len(values)]
+        count = len(values)
+        values = lax.optimization_barrier(tuple(values) + self.last + self.due)
+        self.due, self.fresh = self.fresh, ()
+        return values[:count]
 
     def leave(self, *values):
         self.last = tuple(values)
+
+    def soon(self, values):
+        self.fresh = self.fresh + tuple(values)
+        return list(values)
 
 
 def normalize(values):
@@ -872,8 +925,12 @@
         self.tokens, self.cotangent = tokens, cotangent
         self.gains, self.biases = gains, biases
         self.shape = tokens.shape[1:]
-        self.projected, self.act, self.slope, self.hidden_grad = [], [], [], []
+        self.count = 2 if split else 1
+        self.projected, self.slope = [], []
+        self.all = {name: [] for name in ("attn_in", "act", "ffn_in", "ffn_grad")}
+        self.all.update(hidden_grad=[], attn_grad=[])
         self.projected_grad = [None] * pairs
+        self.other_heads = [None] * pairs
 
     def gather(self, own):
         if self.split:
@@ -885,12 +942,12 @@
             return [own, swap_chip(far)]
         return [lax.psum_scatter(own, "tensor", scatter_dimension=0, tiled=True)]
 
-    def both(self, pieces):
-        return [*pieces, *[swap_core(v) for v in pieces]] if self.split else list(pieces)
-
-    def mixed(self, pieces):
-        first = [piece[0] for piece in pieces]
-        return first + [swap_core(piece[1]) for piece in pieces] if self.split else first
+    def keep(self, name, values):
+        own = values[0]
+        pair = [own]
+        if self.split:
+            pair += self.order.soon([swap_core(values[-1])])
+        self.all[name].append(pair)
 
     def over_row(self, kernel, name, inputs, outs):
         addends = self.order.enter(*self.addends)
@@ -911,6 +968,7 @@
         own, *other = project(self.scalars, x, ws)
         self.order.leave(own, *other)
         self.projected += [own, *[swap_core(v) for v in other]]
+        self.keep("attn_in", [x])
 
     def attend(self):
         projected = self.order.enter(*self.projected)
@@ -938,7 +996,8 @@
         (x,) = self.order.enter(self.ffn_in[part])
         act, slope, out = feed(self.scalars, x, ups, downs, B16 if part else F32)
         self.order.leave(out)
-        self.act.append(act)
+        self.keep("act", act)
+        self.keep("ffn_in", [x])
         self.slope.append(slope)
         if part == 0:
             self.own = out
@@ -961,7 +1020,8 @@
             self.scalars, x, self.slope[part], ups, downs, B16 if part else F32
         )
         self.order.leave(out)
-        self.hidden_grad.append(grad)
+        self.keep("hidden_grad", grad)
+        self.keep("ffn_grad", [x])
         if part == 0:
             self.own = out
         if part == len(self.ffn_grad) - 1:
@@ -982,6 +1042,8 @@
         own, *other = out_back(self.scalars, xs, ws)
         self.order.leave(own, *other)
         self.attended_grad = [own] + [swap_core(v) for v in other]
+        for x in xs:
+            self.keep("attn_grad", [x])
 
     def attend_back(self, pair):
         grads = self.order.enter(*self.attended_grad)
@@ -990,11 +1052,13 @@
         )
         self.projected_grad[pair] = out
         self.order.leave(*out)
+        if self.split:
+            self.other_heads[pair : pair + 1] = self.order.soon([swap_core(out[1])])
 
     def project_back(self, ws):
         sides = [[grad[0] for grad in self.projected_grad]]
         if self.split:
-            sides.append([swap_core(grad[1]) for grad in self.projected_grad])
+            sides.append(self.other_heads)
         flat = self.order.enter(*[v for side in sides for v in side])
         pairs = len(self.projected_grad)
         sides = [flat[i * pairs : (i + 1) * pairs] for i in range(len(sides))]
@@ -1046,31 +1110,41 @@
     for row, own in zip(rows, normed):
         row.attn_in = row.gather(own)
 
-    def outer(*products):
-        flat = [v for lefts, rights in products for v in (*lefts, *rights)]
-        values = list(order.enter(*flat))
-        again = []
-        for lefts, rights in products:
-            taken, values = values[: len(lefts) + len(rights)], values[len(lefts) + len(rights) :]
-            again.append((taken[: len(lefts)], taken[len(lefts) :]))
-        return again
-
-    def both_cores(name):
-        return [v for row in rows for v in row.both(getattr(row, name))]
-
-    def own_columns(name):
-        return [v for row in rows for v in row.mixed(getattr(row, name))]
-
     def listed(values):
         return [v for value in values for v in value]
 
-    def summed(products, manual=True):
-        products = outer(*products)
-        out = outer_sum(scalars, products, staged and manual)
+    def kept(name):
+        return [pair[i] for row in rows for i in range(row.count) for pair in row.all[name]]
+
+    def started(out):
         order.leave(*out)
-        if staged and manual:
-            return DpSum(scalars, order, *out)
-        return out[0] if staged is False else lax.psum(out[0], "dp")
+        return DpSum(scalars, order, *out) if staged else out[0]
+
+    def summed(lefts, rights):
+        values = order.enter(*lefts, *rights)
+        count = len(lefts)
+        return started(outer_sum(scalars, values[:count], values[count:], staged))
+
+    def heads_summed(pair, attended):
+        products = [(listed(row.projected_grad[pair] for row in rows), kept("attn_in"))]
+        if attended:
+            products.append((listed(row.attended for row in rows), kept("attn_grad")))
+        values = list(order.enter(*[v for two in products for side in two for v in side]))
+        again = []
+        for two in products:
+            again.append([[values.pop(0) for _ in side] for side in two])
+        return started(head_outer(scalars, again, staged))
+
+    def tick(*totals):
+        if staged:
+            for total in totals:
+                next(total.steps, None)
+
+    def placed(total):
+        (got,) = order.enter(total.other)
+        out = place(scalars, total.quarter, got)
+        order.leave(out)
+        return out
 
     lead, *others = rows
     lead.project(0, qkvs)
@@ -1105,64 +1179,41 @@
         row.last()
         row.feed_back(0, ups, downs)
     lead.middle_back()
-    if split:
-        for row in others:
+    for row in others:
+        if split:
             row.feed_back(1, ups, downs)
-    grad_down = summed([(own_columns("act"), both_cores("ffn_grad"))], manual=False)
+    downs_sum = summed(kept("act"), kept("ffn_grad"))
+    ups_sum = summed(kept("ffn_in"), kept("hidden_grad"))
     lead.out_back(outs)
+    lead.attend_back(0)
     for row in others:
         row.middle_back()
-    up = summed([(both_cores("ffn_in"), own_columns("hidden_grad"))])
-    lead.attend_back(0)
+    tick(downs_sum)
+    for pair in range(1, pairs):
+        lead.attend_back(pair)
+    tick(downs_sum)
     for row in others:
         row.out_back(outs)
-    if staged:
-        up.scatter()
-    for row in others:
         row.attend_back(0)
-
-    attn_in = both_cores("attn_in")
-
-    def qkv_product(pair):
-        return (attn_in, listed(row.projected_grad[pair] for row in rows))
-
-    attended = listed(row.attended for row in rows)
-    heads = [summed([qkv_product(0), (both_cores("attn_grad"), attended)])]
-    if staged:
-        up.collect()
+    tick(downs_sum, ups_sum)
+    heads = [heads_summed(0, True)]
+    tick(downs_sum, ups_sum)
+    lead.project_back(qkvs)
+    tick(ups_sum, downs_sum)
     for pair in range(1, pairs):
-        lead.attend_back(pair)
-        if staged:
-            heads[0].scatter()
-        if pair == pairs - 1:
-            lead.project_back(qkvs)
-        if staged:
-            up.spread()
         for row in others:
             row.attend_back(pair)
-        heads.append(summed([qkv_product(pair)]))
-    if pairs == 1:
-        lead.project_back(qkvs)
+        tick(downs_sum, ups_sum)
+        heads.append(heads_summed(pair, False))
+    tick(heads[0], downs_sum, ups_sum)
     for row in others:
         row.project_back(qkvs)
-    if staged:
-        heads[0].collect()
+    tick(heads[0], ups_sum)
     lead.first_back()
-    if staged:
-        (grad_down,) = order.enter(grad_down)
-        grad_down = grad_down.astype(F32)
-        order.leave(grad_down)
-        for total in heads[1:]:
-            total.scatter()
-        heads[0].spread()
-        (got,) = order.enter(up.other)
-        grad_up = place(scalars, up.quarter, got)
-        order.leave(grad_up)
+    tick(*heads, ups_sum)
     for row in others:
         row.first_back()
-    if staged:
-        for total in heads[1:]:
-            total.collect()
+    tick(*heads)
     stats = [row.stat_first for row in rows] + [row.stat_middle for row in rows]
     stats += [row.stat_last for row in rows] + [row.stat_back for row in rows]
     (small,) = call(
@@ -1177,21 +1228,21 @@
     steps += [("dp", 1 << i) for i in range(d_size.bit_length() - 1)]
     powers = t_size & (t_size - 1) == 0 and d_size & (d_size - 1) == 0
     if powers:
-        for axis, step in steps[:2]:
+        for index, (axis, step) in enumerate(steps):
             small = doubling(small, axis, step)
-        steps = steps[2:]
+            (small,) = order.enter(small)
+            order.leave(small)
+            tick(*heads)
+            if index == 2 and staged:
+                grad_down = placed(downs_sum)
+    else:
+        small = lax.psum(small, ("dp", "tensor"))
     if staged:
+        tick(*heads)
+        grad_up = placed(ups_sum)
         (got,) = order.enter(heads[0].other)
         grad_qkv, grad_out = place_heads(scalars, heads[0].quarter, got, 0, pairs, None)
         order.leave(grad_out)
-        for total in heads[1:]:
-            total.spread()
-    if powers:
-        for axis, step in steps:
-            small = doubling(small, axis, step)
-    else:
-        small = lax.psum(small, ("dp", "tensor"))
-    if staged:
         for pair in range(1, pairs):
             (grad_qkv,) = place_heads(
                 scalars, heads[pair].quarter, heads[pair].other, pair, pairs, grad_qkv
@@ -1199,11 +1250,11 @@
         grad_qkv = grad_qkv.transpose(1, 0, 2)
     else:
         grad_down, grad_up, *blocks = [
-            v.astype(F32) for v in lax.psum((grad_down, up, *heads), "dp")
+            v.astype(F32) for v in lax.psum((downs_sum, ups_sum, *heads), "dp")
         ]
-        grad_out = blocks[0][:, 384:].T
-        blocks = [grad[:, :384].reshape(width, 3, 128) for grad in blocks]
-        grad_qkv = jnp.concatenate(blocks, axis=2)
+        grad_out = blocks[0][384:]
+        blocks = [grad[:384].reshape(3, 128, width) for grad in blocks]
+        grad_qkv = jnp.concatenate(blocks, axis=1).transpose(2, 0, 1)
     sums = small[8 : 8 + GROUPS]
     group_rms = jnp.sqrt(sums[:, :3] / (sums[:, 3:4] * width))
     return (
@@ -1212,7 +1263,7 @@
         grad_qkv,
         grad_out,
         grad_up,
-        grad_down.astype(F32),
+        grad_down,
         small[:4],
         small[4:8],
         group_rms,

time: 486 us -> 396 us (0.81)
  waiting for transfers between devices: 194 us -> 160 us
  local copies, waits for them, and re-layouts: 40 us -> 15.2 us
  between operations: 16.1 us -> 1.87 us
  Pallas kernels: 154 us -> 144 us
  other arithmetic: 8.85 us -> 3.27 us
    ppermute x21 -> x28, waiting for transfers between devices: 29.2 us -> 62.8 us  [the longest x24 49.2 us: shifted(): return lax.ppermute(value, 'dp', [(d, (d + 2) % 8) for d in range(8)])]
    ppermute x16, waiting for transfers between devices: 104 us -> 71.8 us  [swap_chip(): return lax.ppermute(value, 'tensor', [(0, 2), (2, 0), (1, 3), (3, 1)])]
    psum x1 -> x0, waiting for transfers between devices: 24.4 us -> none  [summed(): return out[0] if staged is False else lax.psum(out[0], 'dp')]
    unnamed x310 -> x88, local copies, waits for them, and re-layouts: 37.9 us -> 13.8 us
    ppermute x3 -> x4, waiting for transfers between devices: 22.7 us -> 8.58 us  [__init__(): self.got = lax.ppermute(send, 'dp', self.swap)]
    pallas_call x44 -> x46, Pallas kernels: 154 us -> 144 us  [call(): pl.pallas_call(kernel, out_shape=[jax.ShapeDtypeStruct(shape, dtype) for...]
    ppermute x21 -> x28, starting transfers between devices: 31.7 us -> 24.6 us  [the longest x24 18.9 us: shifted(): return lax.ppermute(value, 'dp', [(d, (d + 2) % 8) for d in range(8)])]
    convert_element_type x4 -> x12, other arithmetic: 5.73 us -> 0.61 us  [run(): total = (block.astype(F32) + got.astype(F32)).astype(B16)]
  transfers between devices with their start and end apart: 86 -> 93, of which waited for: 33 -> 47; matrix products, arithmetic and copies ran while one was open for 3% -> 1% of each run, Pallas kernels for 32% -> 34%
where the time goes in v3:
time: 396 us; the launch traced here: 392 us
  waiting for transfers between devices  160 us (40%)
  Pallas kernels  144 us (36%)
  starting transfers between devices  67.2 us (17%)
  local copies, waits for them, and re-layouts  15.2 us (4%)
    pallas_call x46, Pallas kernels, call(): pl.pallas_call(kernel, out_shape=[jax.ShapeDtypeStruct(shape, dtype) for...  144 us
    ppermute x16, waiting for transfers between devices, swap_chip(): return lax.ppermute(value, 'tensor', [(0, 2), (2, 0), (1, 3), (3, 1)])  71.8 us
    ppermute x24, waiting for transfers between devices, shifted(): return lax.ppermute(value, 'dp', [(d, (d + 2) % 8) for d in range(8)])  49.2 us
    ppermute x16, starting transfers between devices, swap_chip(): return lax.ppermute(value, 'tensor', [(0, 2), (2, 0), (1, 3), (3, 1)])  22.7 us
    ppermute x24, starting transfers between devices, shifted(): return lax.ppermute(value, 'dp', [(d, (d + 2) % 8) for d in range(8)])  18.9 us
    unnamed x88, local copies, waits for them, and re-layouts  13.8 us
    ppermute x4, waiting for transfers between devices, run(): self.other = lax.ppermute(half, 'dp', self.swap)  13.6 us
    ppermute x5, waiting for transfers between devices, doubling(): lax.ppermute(values, axis, [(i, i ^ step) for i in range(size)])  11.4 us
  transfers between devices with their start and end apart: 93, of which 47 were waited for; matrix products, arithmetic and copies ran while one was open for 1% of the time, Pallas kernels for 34%

profile of v3, /device:TPU:0, one launch (start us, length us, event | category | flops | bytes accessed | tf_op | source)
XLA Modules:
  0.0 392.1 jit_solution(6411943327305141292)
XLA Ops:
  13.7 8.2 %collective-permute-done.2.x_ref.refs_5_ = bf16[272,1024]{1,0:T(8,128)(2,1)S(1)} collective-permute-done((bf16[272,1024]{1,0:T(8,128)(2,1)S(1)}, bf16[272,1024]{1,0:T(8,128)(2,1)S(1)}, u32[]{:S(2)}, u32[]{:S(2)}) %collective-permute-start.2) | collective-permute-done | bytes 557088 | tf_op jit(solution)/shard_map/ppermute | solution.py:919
  27.6 8.0 %attend.2 = (bf16[544,256]{1,0:T(8,128)(2,1)S(1)}, bf16[544,256]{1,0:T(8,128)(2,1)S(1)}, f32[4,1,1088]{2,1,0:T(1,128)S(1)}) custom-call(s32[8]{0:T(128)S(1)} %concatenate.15.scalars, bf16[272,768]{1,0:T(8,128)(2,1)S(1)} %get-tuple-element.310.refs_0_.refs_4_.refs_8_, bf16[272,768]{1,0:T(8,128)(2,1)S(1)} %collective-permute-done.1.refs_1_.refs_5_.refs_9_, ...), custom_call_target="tpu_custom_call" | custom-call | flops 75759616 | bytes 156672 | tf_op jit(solution)/shard_map/attend/pallas_call | solution.py:66
  35.6 4.4 %collective-permute-done.7.x_ref.refs_9_ = bf16[272,1024]{1,0:T(8,128)(2,1)S(1)} collective-permute-done((bf16[272,1024]{1,0:T(8,128)(2,1)S(1)}, bf16[272,1024]{1,0:T(8,128)(2,1)S(1)}, u32[]{:S(2)}, u32[]{:S(2)}) %collective-permute-start.7) | collective-permute-done | bytes 557088 | tf_op jit(solution)/shard_map/ppermute | solution.py:919
  48.2 8.0 %attend.3 = (bf16[544,256]{1,0:T(8,128)(2,1)S(1)}, bf16[544,256]{1,0:T(8,128)(2,1)S(1)}, f32[4,1,1088]{2,1,0:T(1,128)S(1)}) custom-call(s32[8]{0:T(128)S(1)} %concatenate.15.scalars, bf16[272,768]{1,0:T(8,128)(2,1)S(1)} %get-tuple-element.323.refs_0_.refs_4_.refs_8_, bf16[272,768]{1,0:T(8,128)(2,1)S(1)} %collective-permute-done.11.refs_1_.refs_5_.refs_9_, ...), custom_call_target="tpu_custom_call" | custom-call | flops 75759616 | bytes 156672 | tf_op jit(solution)/shard_map/attend/pallas_call | solution.py:66
  66.0 3.6 feed.4
  70.2 6.5 %collective-permute-done.17.x_ref.refs_1_ = bf16[272,1024]{1,0:T(8,128)(2,1)S(1)} collective-permute-done((bf16[272,1024]{1,0:T(8,128)(2,1)S(1)}, bf16[272,1024]{1,0:T(8,128)(2,1)S(1)}, u32[]{:S(2)}, u32[]{:S(2)}) %collective-permute-start.17) | collective-permute-done | bytes 557088 | tf_op jit(solution)/shard_map/ppermute | solution.py:919
  76.6 3.5 feed.5
  82.5 6.1 %collective-permute-done.19.refs_1_ = bf16[272,1024]{1,0:T(8,128)(2,1)S(1)} collective-permute-done((bf16[272,1024]{1,0:T(8,128)(2,1)S(1)}, bf16[272,1024]{1,0:T(8,128)(2,1)S(1)}, u32[]{:S(2)}, u32[]{:S(2)}) %collective-permute-start.19) | collective-permute-done | bytes 557088 | tf_op jit(solution)/shard_map/ppermute | solution.py:919
  95.9 4.6 %collective-permute-done.18.refs_1_ = bf16[272,1024]{1,0:T(8,128)(2,1)S(1)} collective-permute-done((bf16[272,1024]{1,0:T(8,128)(2,1)S(1)}, bf16[272,1024]{1,0:T(8,128)(2,1)S(1)}, u32[]{:S(2)}, u32[]{:S(2)}) %collective-permute-start.18) | collective-permute-done | bytes 557088 | tf_op jit(solution)/shard_map/ppermute | solution.py:919
  112.4 3.5 feed.7
  118.5 5.8 %collective-permute-done.28.x_ref.refs_9_ = bf16[272,1024]{1,0:T(8,128)(2,1)S(1)} collective-permute-done((bf16[272,1024]{1,0:T(8,128)(2,1)S(1)}, bf16[272,1024]{1,0:T(8,128)(2,1)S(1)}, u32[]{:S(2)}, u32[]{:S(2)}) %collective-permute-start.28) | collective-permute-done | bytes 557088 | tf_op jit(solution)/shard_map/ppermute | solution.py:919
  128.8 6.0 %collective-permute-done.27.refs_1_ = bf16[272,1024]{1,0:T(8,128)(2,1)S(1)} collective-permute-done((bf16[272,1024]{1,0:T(8,128)(2,1)S(1)}, bf16[272,1024]{1,0:T(8,128)(2,1)S(1)}, u32[]{:S(2)}, u32[]{:S(2)}) %collective-permute-start.27) | collective-permute-done | bytes 557088 | tf_op jit(solution)/shard_map/ppermute | solution.py:919
  144.1 6.3 %collective-permute-done.33.refs_1_ = bf16[272,1024]{1,0:T(8,128)(2,1)S(1)} collective-permute-done((bf16[272,1024]{1,0:T(8,128)(2,1)S(1)}, bf16[272,1024]{1,0:T(8,128)(2,1)S(1)}, u32[]{:S(2)}, u32[]{:S(2)}) %collective-permute-start.33) | collective-permute-done | bytes 557088 | tf_op jit(solution)/shard_map/ppermute | solution.py:919
  152.8 7.1 %collective-permute-done.37.x_ref.refs_13_ = bf16[272,1024]{1,0:T(8,128)(2,1)S(1)} collective-permute-done((bf16[272,1024]{1,0:T(8,128)(2,1)S(1)}, bf16[272,1024]{1,0:T(8,128)(2,1)S(1)}, u32[]{:S(2)}, u32[]{:S(2)}) %collective-permute-start.37) | collective-permute-done | bytes 557088 | tf_op jit(solution)/shard_map/ppermute | solution.py:919
  171.0 8.0 %outer_sum.2 = (bf16[512,1024]{1,0:T(8,128)(2,1)S(1)}, bf16[512,1024]{1,0:T(8,128)(2,1)S(1)}) custom-call(s32[8]{0:T(128)S(1)} %concatenate.15.scalars, bf16[272,1024]{1,0:T(8,128)(2,1)S(1)} %get-tuple-element.393.refs_0_, bf16[272,1024]{1,0:T(8,128)(2,1)S(1)} %get-tuple-element.394.refs_1_, bf16[272,1024]{1,0:T(8,128)(2,1)S(1)} %collective-permute-done.20.refs_2_, ...), custom_call_target="tpu_custom_call" | custom-call | flops 285212672 | bytes 278528 | tf_op jit(solution)/shard_map/outer_sum/pallas_call | solution.py:66
  180.7 8.0 %outer_sum.3 = (bf16[512,1024]{1,0:T(8,128)(2,1)S(1)}, bf16[512,1024]{1,0:T(8,128)(2,1)S(1)}) custom-call(s32[8]{0:T(128)S(1)} %concatenate.15.scalars, bf16[272,1024]{1,0:T(8,128)(2,1)S(1)} %get-tuple-element.411.x_ref.refs_0_, bf16[272,1024]{1,0:T(8,128)(2,1)S(1)} %collective-permute-done.17.x_ref.refs_1_, ...), custom_call_target="tpu_custom_call" | custom-call | flops 285212672 | bytes 278528 | tf_op jit(solution)/shard_map/outer_sum/pallas_call | solution.py:66
  191.6 6.9 %attend_back.4 = (bf16[544,384]{1,0:T(8,128)(2,1)S(1)}, bf16[544,384]{1,0:T(8,128)(2,1)S(1)}) custom-call(s32[8]{0:T(128)S(1)} %concatenate.15.scalars, bf16[272,768]{1,0:T(8,128)(2,1)S(1)} %get-tuple-element.310.refs_0_.refs_4_.refs_8_, bf16[272,768]{1,0:T(8,128)(2,1)S(1)} %collective-permute-done.1.refs_1_.refs_5_.refs_9_, ...), custom_call_target="tpu_custom_call" | custom-call | flops 94699520 | bytes 191760 | tf_op jit(solution)/shard_map/attend_back/pallas_call | solution.py:66
  198.7 6.4 %collective-permute-done.44.refs_1_ = bf16[272,1024]{1,0:T(8,128)(2,1)S(1)} collective-permute-done((bf16[272,1024]{1,0:T(8,128)(2,1)S(1)}, bf16[272,1024]{1,0:T(8,128)(2,1)S(1)}, u32[]{:S(2)}, u32[]{:S(2)}) %collective-permute-start.44) | collective-permute-done | bytes 557088 | tf_op jit(solution)/shard_map/ppermute | solution.py:919
  210.3 6.7 %attend_back.5 = (bf16[544,384]{1,0:T(8,128)(2,1)S(1)}, bf16[544,384]{1,0:T(8,128)(2,1)S(1)}) custom-call(s32[8]{0:T(128)S(1)} %concatenate.15.scalars, bf16[272,768]{1,0:T(8,128)(2,1)S(1)} %get-tuple-element.310.refs_0_.refs_4_.refs_8_, bf16[272,768]{1,0:T(8,128)(2,1)S(1)} %collective-permute-done.1.refs_1_.refs_5_.refs_9_, ...), custom_call_target="tpu_custom_call" | custom-call | flops 94699520 | bytes 191760 | tf_op jit(solution)/shard_map/attend_back/pallas_call | solution.py:66
  225.2 6.7 %attend_back.6 = (bf16[544,384]{1,0:T(8,128)(2,1)S(1)}, bf16[544,384]{1,0:T(8,128)(2,1)S(1)}) custom-call(s32[8]{0:T(128)S(1)} %concatenate.15.scalars, bf16[272,768]{1,0:T(8,128)(2,1)S(1)} %get-tuple-element.323.refs_0_.refs_4_.refs_8_, bf16[272,768]{1,0:T(8,128)(2,1)S(1)} %collective-permute-done.11.refs_1_.refs_5_.refs_9_, ...), custom_call_target="tpu_custom_call" | custom-call | flops 94699520 | bytes 191760 | tf_op jit(solution)/shard_map/attend_back/pallas_call | solution.py:66
  234.2 8.5 %collective-permute-done.49.got_ref = bf16[512,1024]{1,0:T(8,128)(2,1)S(1)} collective-permute-done((bf16[512,1024]{1,0:T(8,128)(2,1)S(1)}, bf16[512,1024]{1,0:T(8,128)(2,1)S(1)}, u32[]{:S(2)}, u32[]{:S(2)}) %collective-permute-start.49) | collective-permute-done | bytes 1048608 | tf_op jit(solution)/shard_map/ppermute | solution.py:697
  245.1 8.0 %head_outer.2 = (bf16[320,1024]{1,0:T(8,128)(2,1)S(1)}, bf16[320,1024]{1,0:T(8,128)(2,1)S(1)}) custom-call(s32[8]{0:T(128)S(1)} %concatenate.15.scalars, bf16[544,384]{1,0:T(8,128)(2,1)S(1)} %get-tuple-element.495.refs_0_, bf16[544,384]{1,0:T(8,128)(2,1)S(1)} %get-tuple-element.468.refs_1_, bf16[544,384]{1,0:T(8,128)(2,1)S(1)} %get-tuple-element.530.refs_2_.refs_0_, ...), custom_call_target="tpu_custom_call" | custom-call | flops 178257920 | bytes 365568 | tf_op jit(solution)/shard_map/head_outer/pallas_call | solution.py:66
  257.6 6.8 %collective-permute-done.60 = bf16[128,1024]{1,0:T(8,128)(2,1)S(1)} collective-permute-done((bf16[128,1024]{1,0:T(8,128)(2,1)S(1)}, bf16[128,1024]{1,0:T(8,128)(2,1)S(1)}, u32[]{:S(2)}, u32[]{:S(2)}) %collective-permute-start.60) | collective-permute-done | bytes 262176 | tf_op jit(solution)/shard_map/ppermute | solution.py:701
  264.5 3.9 collective-permute-done.62.refs_1_
  268.4 6.7 %attend_back.7 = (bf16[544,384]{1,0:T(8,128)(2,1)S(1)}, bf16[544,384]{1,0:T(8,128)(2,1)S(1)}) custom-call(s32[8]{0:T(128)S(1)} %concatenate.15.scalars, bf16[272,768]{1,0:T(8,128)(2,1)S(1)} %get-tuple-element.323.refs_0_.refs_4_.refs_8_, bf16[272,768]{1,0:T(8,128)(2,1)S(1)} %collective-permute-done.11.refs_1_.refs_5_.refs_9_, ...), custom_call_target="tpu_custom_call" | custom-call | flops 94699520 | bytes 191760 | tf_op jit(solution)/shard_map/attend_back/pallas_call | solution.py:66
  275.8 10.9 %collective-permute-done.63.refs_2_ = bf16[128,1024]{1,0:T(8,128)(2,1)S(1)} collective-permute-done((bf16[128,1024]{1,0:T(8,128)(2,1)S(1)}, bf16[128,1024]{1,0:T(8,128)(2,1)S(1)}, u32[]{:S(2)}, u32[]{:S(2)}) %collective-permute-start.63) | collective-permute-done | bytes 262176 | tf_op jit(solution)/shard_map/ppermute | solution.py:701
  286.7 5.6 %collective-permute-done.61 = bf16[128,1024]{1,0:T(8,128)(2,1)S(1)} collective-permute-done((bf16[128,1024]{1,0:T(8,128)(2,1)S(1)}, bf16[128,1024]{1,0:T(8,128)(2,1)S(1)}, u32[]{:S(2)}, u32[]{:S(2)}) %collective-permute-start.61) | collective-permute-done | bytes 262176 | tf_op jit(solution)/shard_map/ppermute | solution.py:701
  292.5 5.3 %head_outer.3 = (bf16[192,1024]{1,0:T(8,128)(2,1)S(1)}, bf16[192,1024]{1,0:T(8,128)(2,1)S(1)}) custom-call(s32[8]{0:T(128)S(1)} %concatenate.15.scalars, bf16[544,384]{1,0:T(8,128)(2,1)S(1)} %get-tuple-element.509.refs_1_.refs_0_, bf16[544,384]{1,0:T(8,128)(2,1)S(1)} %get-tuple-element.510.refs_1_, bf16[544,384]{1,0:T(8,128)(2,1)S(1)} %get-tuple-element.531.refs_2_.refs_1_, ...), custom_call_target="tpu_custom_call" | custom-call | flops 106954752 | bytes 191488 | tf_op jit(solution)/shard_map/head_outer/pallas_call | solution.py:66
  309.7 4.2 %collective-permute-done.68.refs_2_ = bf16[128,1024]{1,0:T(8,128)(2,1)S(1)} collective-permute-done((bf16[128,1024]{1,0:T(8,128)(2,1)S(1)}, bf16[128,1024]{1,0:T(8,128)(2,1)S(1)}, u32[]{:S(2)}, u32[]{:S(2)}) %collective-permute-start.68) | collective-permute-done | bytes 262176 | tf_op jit(solution)/shard_map/ppermute | solution.py:701
  337.5 4.0 %collective-permute-done.84 = f32[16,1024]{1,0:T(8,128)S(1)} collective-permute-done((f32[16,1024]{1,0:T(8,128)S(1)}, f32[16,1024]{1,0:T(8,128)S(1)}, u32[]{:S(2)}, u32[]{:S(2)}) %collective-permute-start.84) | collective-permute-done | bytes 65568 | tf_op jit(solution)/shard_map/ppermute | solution.py:1081
  363.6 4.1 %collective-permute-done.88.refs_3_ = bf16[48,1024]{1,0:T(8,128)(2,1)S(1)} collective-permute-done((bf16[48,1024]{1,0:T(8,128)(2,1)S(1)}, bf16[48,1024]{1,0:T(8,128)(2,1)S(1)}, u32[]{:S(2)}, u32[]{:S(2)}) %collective-permute-start.88) | collective-permute-done | bytes 98336 | tf_op jit(solution)/shard_map/ppermute | solution.py:701
  374.1 11.4 %collective-permute-done.91.refs_4_ = bf16[320,1024]{1,0:T(8,128)(2,1)S(1)} collective-permute-done((bf16[320,1024]{1,0:T(8,128)(2,1)S(1)}, bf16[320,1024]{1,0:T(8,128)(2,1)S(1)}, u32[]{:S(2)}, u32[]{:S(2)}) %collective-permute-start.91) | collective-permute-done | bytes 655392 | tf_op jit(solution)/shard_map/ppermute | solution.py:734
  (314 shorter events, 186.6 us)
Async XLA Ops:
  6.1 15.8 %collective-permute-start.2 = (bf16[272,1024]{1,0:T(8,128)(2,1)S(1)}, bf16[272,1024]{1,0:T(8,128)(2,1)S(1)}, u32[]{:S(2)}, u32[]{:S(2)}) collective-permute-start(bf16[272,1024]{1,0:T(8,128)(2,1)S(1)} %get-tuple-element.513.x_ref.refs_4_), channel_id=1, source_target_pairs={{0,2},{2,0},{1,3},{3,1},{4,6},{6,4},{5,7},{7,5},{8,10},{10,8},{9,1... | collective-permute-start | bytes 1671176 | tf_op jit(solution)/shard_map/ppermute | solution.py:919
  24.2 41.9 %collective-permute-start.15 = (bf16[1024,1024]{1,0:T(8,128)(2,1)S(1)}, bf16[1024,1024]{1,0:T(8,128)(2,1)S(1)}, u32[]{:S(2)}, u32[]{:S(2)}) collective-permute-start(bf16[1024,1024]{1,0:T(8,128)(2,1)S(1)} %copy-done), channel_id=1, source_target_pairs={{0,1},{1,0},{2,3},{3,2},{4,5},{5,4},{6,7},{7,6},{8,9},{9,8},{10,11... | collective-permute-start | bytes 6291464 | tf_op jit(solution)/shard_map/ppermute | solution.py:915
  24.6 41.4 %collective-permute-start.16 = (bf16[1024,1024]{1,0:T(8,128)(2,1)S(1)}, bf16[1024,1024]{1,0:T(8,128)(2,1)S(1)}, u32[]{:S(2)}, u32[]{:S(2)}) collective-permute-start(bf16[1024,1024]{1,0:T(8,128)(2,1)S(1)} %copy-done.1), channel_id=1, source_target_pairs={{0,1},{1,0},{2,3},{3,2},{4,5},{5,4},{6,7},{7,6},{8,9},{9,8},{10,11... | collective-permute-start | bytes 6291464 | tf_op jit(solution)/shard_map/ppermute | solution.py:915
  27.1 16.2 %collective-permute-start.9 = (bf16[256,1024]{1,0:T(8,128)(2,1)S(1)}, bf16[256,1024]{1,0:T(8,128)(2,1)S(1)}, u32[]{:S(2)}, u32[]{:S(2)}) collective-permute-start(bf16[256,1024]{1,0:T(8,128)(2,1)S(1)} %copy-done.7), channel_id=1, source_target_pairs={{0,1},{1,0},{2,3},{3,2},{4,5},{5,4},{6,7},{7,6},{8,9},{9,8},{10,11... | collective-permute-start | bytes 1572872 | tf_op jit(solution)/shard_map/ppermute | solution.py:915
  61.0 15.6 %collective-permute-start.17 = (bf16[272,1024]{1,0:T(8,128)(2,1)S(1)}, bf16[272,1024]{1,0:T(8,128)(2,1)S(1)}, u32[]{:S(2)}, u32[]{:S(2)}) collective-permute-start(bf16[272,1024]{1,0:T(8,128)(2,1)S(1)} %get-tuple-element.411.x_ref.refs_0_), channel_id=1, source_target_pairs={{0,2},{2,0},{1,3},{3,1},{4,6},{6,4},{5,7},{7,5},{8,10},{10,8},{9,1... | collective-permute-start | bytes 1671176 | tf_op jit(solution)/shard_map/ppermute | solution.py:919
  65.7 22.9 %collective-permute-start.19 = (bf16[272,1024]{1,0:T(8,128)(2,1)S(1)}, bf16[272,1024]{1,0:T(8,128)(2,1)S(1)}, u32[]{:S(2)}, u32[]{:S(2)}) collective-permute-start(bf16[272,1024]{1,0:T(8,128)(2,1)S(1)} %get-tuple-element.335), channel_id=1, source_target_pairs={{0,2},{2,0},{1,3},{3,1},{4,6},{6,4},{5,7},{7,5},{8,10},{10,8},{9,1... | collective-permute-start | bytes 1671176 | tf_op jit(solution)/shard_map/ppermute | solution.py:919
  66.0 16.5 %collective-permute-start.21 = (bf16[272,1024]{1,0:T(8,128)(2,1)S(1)}, bf16[272,1024]{1,0:T(8,128)(2,1)S(1)}, u32[]{:S(2)}, u32[]{:S(2)}) collective-permute-start(bf16[272,1024]{1,0:T(8,128)(2,1)S(1)} %get-tuple-element.411.x_ref.refs_0_), channel_id=1, source_target_pairs={{0,1},{1,0},{2,3},{3,2},{4,5},{5,4},{6,7},{7,6},{8,9},{9,8},{10,11... | collective-permute-start | bytes 1671176 | tf_op jit(solution)/shard_map/ppermute | solution.py:915
  80.8 19.7 %collective-permute-start.18 = (bf16[272,1024]{1,0:T(8,128)(2,1)S(1)}, bf16[272,1024]{1,0:T(8,128)(2,1)S(1)}, u32[]{:S(2)}, u32[]{:S(2)}) collective-permute-start(bf16[272,1024]{1,0:T(8,128)(2,1)S(1)} %get-tuple-element.339), channel_id=1, source_target_pairs={{0,2},{2,0},{1,3},{3,1},{4,6},{6,4},{5,7},{7,5},{8,10},{10,8},{9,1... | collective-permute-start | bytes 1671176 | tf_op jit(solution)/shard_map/ppermute | solution.py:919
  94.2 18.3 %collective-permute-start.24 = (bf16[272,1024]{1,0:T(8,128)(2,1)S(1)}, bf16[272,1024]{1,0:T(8,128)(2,1)S(1)}, u32[]{:S(2)}, u32[]{:S(2)}) collective-permute-start(bf16[272,1024]{1,0:T(8,128)(2,1)S(1)} %get-tuple-element.415.x_ref.refs_4_), channel_id=1, source_target_pairs={{0,2},{2,0},{1,3},{3,1},{4,6},{6,4},{5,7},{7,5},{8,10},{10,8},{9,1... | collective-permute-start | bytes 1671176 | tf_op jit(solution)/shard_map/ppermute | solution.py:919
  102.8 21.6 %collective-permute-start.28 = (bf16[272,1024]{1,0:T(8,128)(2,1)S(1)}, bf16[272,1024]{1,0:T(8,128)(2,1)S(1)}, u32[]{:S(2)}, u32[]{:S(2)}) collective-permute-start(bf16[272,1024]{1,0:T(8,128)(2,1)S(1)} %get-tuple-element.401.x_ref.refs_8_), channel_id=1, source_target_pairs={{0,2},{2,0},{1,3},{3,1},{4,6},{6,4},{5,7},{7,5},{8,10},{10,8},{9,1... | collective-permute-start | bytes 1671176 | tf_op jit(solution)/shard_map/ppermute | solution.py:919
  108.5 15.9 %collective-permute-start.29 = (bf16[272,1024]{1,0:T(8,128)(2,1)S(1)}, bf16[272,1024]{1,0:T(8,128)(2,1)S(1)}, u32[]{:S(2)}, u32[]{:S(2)}) collective-permute-start(bf16[272,1024]{1,0:T(8,128)(2,1)S(1)} %get-tuple-element.359), channel_id=1, source_target_pairs={{0,1},{1,0},{2,3},{3,2},{4,5},{5,4},{6,7},{7,6},{8,9},{9,8},{10,11... | collective-permute-start | bytes 1671176 | tf_op jit(solution)/shard_map/ppermute | solution.py:915
  108.5 15.9 %collective-permute-start.30 = (bf16[272,1024]{1,0:T(8,128)(2,1)S(1)}, bf16[272,1024]{1,0:T(8,128)(2,1)S(1)}, u32[]{:S(2)}, u32[]{:S(2)}) collective-permute-start(bf16[272,1024]{1,0:T(8,128)(2,1)S(1)} %get-tuple-element.401.x_ref.refs_8_), channel_id=1, source_target_pairs={{0,1},{1,0},{2,3},{3,2},{4,5},{5,4},{6,7},{7,6},{8,9},{9,8},{10,11... | collective-permute-start | bytes 1671176 | tf_op jit(solution)/shard_map/ppermute | solution.py:915
  112.4 25.0 %collective-permute-start.32 = (bf16[272,1024]{1,0:T(8,128)(2,1)S(1)}, bf16[272,1024]{1,0:T(8,128)(2,1)S(1)}, u32[]{:S(2)}, u32[]{:S(2)}) collective-permute-start(bf16[272,1024]{1,0:T(8,128)(2,1)S(1)} %collective-permute-done.24.x_ref.refs_5_), channel_id=1, source_target_pairs={{0,1},{1,0},{2,3},{3,2},{4,5},{5,4},{6,7},{7,6},{8,9},{9,8},{10,11... | collective-permute-start | bytes 1671176 | tf_op jit(solution)/shard_map/ppermute | solution.py:915
  116.8 18.0 %collective-permute-start.27 = (bf16[272,1024]{1,0:T(8,128)(2,1)S(1)}, bf16[272,1024]{1,0:T(8,128)(2,1)S(1)}, u32[]{:S(2)}, u32[]{:S(2)}) collective-permute-start(bf16[272,1024]{1,0:T(8,128)(2,1)S(1)} %get-tuple-element.358), channel_id=1, source_target_pairs={{0,2},{2,0},{1,3},{3,1},{4,6},{6,4},{5,7},{7,5},{8,10},{10,8},{9,1... | collective-permute-start | bytes 1671176 | tf_op jit(solution)/shard_map/ppermute | solution.py:919
  134.8 15.6 %collective-permute-start.33 = (bf16[272,1024]{1,0:T(8,128)(2,1)S(1)}, bf16[272,1024]{1,0:T(8,128)(2,1)S(1)}, u32[]{:S(2)}, u32[]{:S(2)}) collective-permute-start(bf16[272,1024]{1,0:T(8,128)(2,1)S(1)} %get-tuple-element.363), channel_id=1, source_target_pairs={{0,2},{2,0},{1,3},{3,1},{4,6},{6,4},{5,7},{7,5},{8,10},{10,8},{9,1... | collective-permute-start | bytes 1671176 | tf_op jit(solution)/shard_map/ppermute | solution.py:919
  140.1 19.9 %collective-permute-start.37 = (bf16[272,1024]{1,0:T(8,128)(2,1)S(1)}, bf16[272,1024]{1,0:T(8,128)(2,1)S(1)}, u32[]{:S(2)}, u32[]{:S(2)}) collective-permute-start(bf16[272,1024]{1,0:T(8,128)(2,1)S(1)} %get-tuple-element.405.x_ref.refs_12_), channel_id=1, source_target_pairs={{0,2},{2,0},{1,3},{3,1},{4,6},{6,4},{5,7},{7,5},{8,10},{10,8},{9,1... | collective-permute-start | bytes 1671176 | tf_op jit(solution)/shard_map/ppermute | solution.py:919
  143.6 16.4 %collective-permute-start.38 = (bf16[272,1024]{1,0:T(8,128)(2,1)S(1)}, bf16[272,1024]{1,0:T(8,128)(2,1)S(1)}, u32[]{:S(2)}, u32[]{:S(2)}) collective-permute-start(bf16[272,1024]{1,0:T(8,128)(2,1)S(1)} %get-tuple-element.382), channel_id=1, source_target_pairs={{0,1},{1,0},{2,3},{3,2},{4,5},{5,4},{6,7},{7,6},{8,9},{9,8},{10,11... | collective-permute-start | bytes 1671176 | tf_op jit(solution)/shard_map/ppermute | solution.py:915
  143.6 17.1 %collective-permute-start.39 = (bf16[272,1024]{1,0:T(8,128)(2,1)S(1)}, bf16[272,1024]{1,0:T(8,128)(2,1)S(1)}, u32[]{:S(2)}, u32[]{:S(2)}) collective-permute-start(bf16[272,1024]{1,0:T(8,128)(2,1)S(1)} %get-tuple-element.405.x_ref.refs_12_), channel_id=1, source_target_pairs={{0,1},{1,0},{2,3},{3,2},{4,5},{5,4},{6,7},{7,6},{8,9},{9,8},{10,11... | collective-permute-start | bytes 1671176 | tf_op jit(solution)/shard_map/ppermute | solution.py:915
  164.7 15.9 %collective-permute-start.40 = (bf16[272,1024]{1,0:T(8,128)(2,1)S(1)}, bf16[272,1024]{1,0:T(8,128)(2,1)S(1)}, u32[]{:S(2)}, u32[]{:S(2)}) collective-permute-start(bf16[272,1024]{1,0:T(8,128)(2,1)S(1)} %get-tuple-element.387), channel_id=1, source_target_pairs={{0,1},{1,0},{2,3},{3,2},{4,5},{5,4},{6,7},{7,6},{8,9},{9,8},{10,11... | collective-permute-start | bytes 1671176 | tf_op jit(solution)/shard_map/ppermute | solution.py:915
  165.2 23.5 %collective-permute-start.36 = (bf16[272,1024]{1,0:T(8,128)(2,1)S(1)}, bf16[272,1024]{1,0:T(8,128)(2,1)S(1)}, u32[]{:S(2)}, u32[]{:S(2)}) collective-permute-start(bf16[272,1024]{1,0:T(8,128)(2,1)S(1)} %get-tuple-element.483.refs_0_.refs_16_), channel_id=1, source_target_pairs={{0,2},{2,0},{1,3},{3,1},{4,6},{6,4},{5,7},{7,5},{8,10},{10,8},{9,1... | collective-permute-start | bytes 1671176 | tf_op jit(solution)/shard_map/ppermute | solution.py:919
  179.0 28.9 %collective-permute-start.43 = (bf16[512,1024]{1,0:T(8,128)(2,1)S(1)}, bf16[512,1024]{1,0:T(8,128)(2,1)S(1)}, u32[]{:S(2)}, u32[]{:S(2)}) collective-permute-start(bf16[512,1024]{1,0:T(8,128)(2,1)S(1)} %get-tuple-element.410), channel_id=1, source_target_pairs={{0,4},{4,0},{8,12},{12,8},{16,20},{20,16},{24,28},{28,24},{1,5},{5... | collective-permute-start | bytes 3145736 | tf_op jit(solution)/shard_map/ppermute | solution.py:697
  217.1 25.6 %collective-permute-start.49 = (bf16[512,1024]{1,0:T(8,128)(2,1)S(1)}, bf16[512,1024]{1,0:T(8,128)(2,1)S(1)}, u32[]{:S(2)}, u32[]{:S(2)}) collective-permute-start(bf16[512,1024]{1,0:T(8,128)(2,1)S(1)} %get-tuple-element.428), channel_id=1, source_target_pairs={{0,4},{4,0},{8,12},{12,8},{16,20},{20,16},{24,28},{28,24},{1,5},{5... | collective-permute-start | bytes 3145736 | tf_op jit(solution)/shard_map/ppermute | solution.py:697
  234.2 18.9 %collective-permute-start.58 = (bf16[128,1024]{1,0:T(8,128)(2,1)S(1)}, bf16[128,1024]{1,0:T(8,128)(2,1)S(1)}, u32[]{:S(2)}, u32[]{:S(2)}) collective-permute-start(bf16[128,1024]{1,0:T(8,128)(2,1)S(1)} %add_convert_fusion.4), channel_id=1, source_target_pairs={{0,8},{4,12},{8,16},{12,20},{16,24},{20,28},{24,0},{28,4},{1,9},{5... | collective-permute-start | bytes 786440 | tf_op jit(solution)/shard_map/ppermute | solution.py:701
  275.1 17.3 %collective-permute-start.64 = (bf16[544,384]{1,0:T(8,128)(2,1)S(1)}, bf16[544,384]{1,0:T(8,128)(2,1)S(1)}, u32[]{:S(2)}, u32[]{:S(2)}) collective-permute-start(bf16[544,384]{1,0:T(8,128)(2,1)S(1)} %get-tuple-element.512.refs_3_), channel_id=1, source_target_pairs={{0,1},{1,0},{2,3},{3,2},{4,5},{5,4},{6,7},{7,6},{8,9},{9,8},{10,11... | collective-permute-start | bytes 1253384 | tf_op jit(solution)/shard_map/ppermute | solution.py:915
  275.1 22.7 %collective-permute-start.67 = (bf16[320,1024]{1,0:T(8,128)(2,1)S(1)}, bf16[320,1024]{1,0:T(8,128)(2,1)S(1)}, u32[]{:S(2)}, u32[]{:S(2)}) collective-permute-start(bf16[320,1024]{1,0:T(8,128)(2,1)S(1)} %get-tuple-element.492), channel_id=1, source_target_pairs={{0,4},{4,0},{8,12},{12,8},{16,20},{20,16},{24,28},{28,24},{1,5},{5... | collective-permute-start | bytes 1966088 | tf_op jit(solution)/shard_map/ppermute | solution.py:697
  275.8 16.6 %collective-permute-start.61 = (bf16[128,1024]{1,0:T(8,128)(2,1)S(1)}, bf16[128,1024]{1,0:T(8,128)(2,1)S(1)}, u32[]{:S(2)}, u32[]{:S(2)}) collective-permute-start(bf16[128,1024]{1,0:T(8,128)(2,1)S(1)} %add_convert_fusion.1), channel_id=1, source_target_pairs={{0,8},{4,12},{8,16},{12,20},{16,24},{20,28},{24,0},{28,4},{1,9},{5... | collective-permute-start | bytes 786440 | tf_op jit(solution)/shard_map/ppermute | solution.py:701
  298.6 15.6 %collective-permute-start.59 = (bf16[272,1024]{1,0:T(8,128)(2,1)S(1)}, bf16[272,1024]{1,0:T(8,128)(2,1)S(1)}, u32[]{:S(2)}, u32[]{:S(2)}) collective-permute-start(bf16[272,1024]{1,0:T(8,128)(2,1)S(1)} %get-tuple-element.500), channel_id=1, source_target_pairs={{0,2},{2,0},{1,3},{3,1},{4,6},{6,4},{5,7},{7,5},{8,10},{10,8},{9,1... | collective-permute-start | bytes 1671176 | tf_op jit(solution)/shard_map/ppermute | solution.py:919
  307.7 16.4 %collective-permute-start.70 = (bf16[272,1024]{1,0:T(8,128)(2,1)S(1)}, bf16[272,1024]{1,0:T(8,128)(2,1)S(1)}, u32[]{:S(2)}, u32[]{:S(2)}) collective-permute-start(bf16[272,1024]{1,0:T(8,128)(2,1)S(1)} %get-tuple-element.535), channel_id=1, source_target_pairs={{0,2},{2,0},{1,3},{3,1},{4,6},{6,4},{5,7},{7,5},{8,10},{10,8},{9,1... | collective-permute-start | bytes 1671176 | tf_op jit(solution)/shard_map/ppermute | solution.py:919
  317.3 35.9 %collective-permute-start.87 = (bf16[512,1024]{1,0:T(8,128)(2,1)S(1)}, bf16[512,1024]{1,0:T(8,128)(2,1)S(1)}, u32[]{:S(2)}, u32[]{:S(2)}) collective-permute-start(bf16[512,1024]{1,0:T(8,128)(2,1)S(1)} %pad_maximum_fusion.2), channel_id=1, source_target_pairs={{0,4},{4,0},{8,12},{12,8},{16,20},{20,16},{24,28},{28,24},{1,5},{5... | collective-permute-start | bytes 3145736 | tf_op jit(solution)/shard_map/ppermute | solution.py:734
  345.4 26.1 %collective-permute-start.92 = (bf16[512,1024]{1,0:T(8,128)(2,1)S(1)}, bf16[512,1024]{1,0:T(8,128)(2,1)S(1)}, u32[]{:S(2)}, u32[]{:S(2)}) collective-permute-start(bf16[512,1024]{1,0:T(8,128)(2,1)S(1)} %pad_maximum_fusion.3), channel_id=1, source_target_pairs={{0,4},{4,0},{8,12},{12,8},{16,20},{20,16},{24,28},{28,24},{1,5},{5... | collective-permute-start | bytes 3145736 | tf_op jit(solution)/shard_map/ppermute | solution.py:734
  359.1 26.4 %collective-permute-start.91 = (bf16[320,1024]{1,0:T(8,128)(2,1)S(1)}, bf16[320,1024]{1,0:T(8,128)(2,1)S(1)}, u32[]{:S(2)}, u32[]{:S(2)}) collective-permute-start(bf16[320,1024]{1,0:T(8,128)(2,1)S(1)} %pad_maximum_fusion.4), channel_id=1, source_target_pairs={{0,4},{4,0},{8,12},{12,8},{16,20},{20,16},{24,28},{28,24},{1,5},{5... | collective-permute-start | bytes 1966088 | tf_op jit(solution)/shard_map/ppermute | solution.py:734
  367.7 22.1 %collective-permute-start.90 = (bf16[192,1024]{1,0:T(8,128)(2,1)S(1)}, bf16[192,1024]{1,0:T(8,128)(2,1)S(1)}, u32[]{:S(2)}, u32[]{:S(2)}) collective-permute-start(bf16[192,1024]{1,0:T(8,128)(2,1)S(1)} %pad_maximum_fusion.5), channel_id=1, source_target_pairs={{0,4},{4,0},{8,12},{12,8},{16,20},{20,16},{24,28},{28,24},{1,5},{5... | collective-permute-start | bytes 1179656 | tf_op jit(solution)/shard_map/ppermute | solution.py:734
  (105 other events, 765.6 us)

commit v4 on v3

--- a/solution.py
+++ b/solution.py
@@ -20,6 +20,54 @@
 gelu_cubic = 0.044715
 
 BASE, TENSOR, Z, X, LENGTH = 0, 1, 2, 3, 4
+
+
+STAGES = (
+    "FB1",
+    "OB0",
+    "WD",
+    "WU",
+    "MB1",
+    "AB00",
+    "AB01",
+    "D",
+    "OB1",
+    "AB10",
+    "D",
+    "HP",
+    "U",
+    "PB0",
+    "D",
+    "AB11",
+    "U",
+    "HQ",
+    "D",
+    "PB1",
+    "P",
+    "Q",
+    "U",
+    "D",
+    "P",
+    "U",
+    "FL0",
+    "P",
+    "Q",
+    "U",
+    "FL1",
+    "PD",
+    "Q",
+    "P",
+    "SM",
+    "S",
+    "P",
+    "Q",
+    "S",
+    "Q",
+    "S",
+    "S",
+    "S",
+    "PU",
+)
 
 
 def nt(left, right):
@@ -445,10 +493,14 @@
     )
 
 
+def turned(index):
+    return 2 * lax.rem(index, 2) + index // 2
+
+
 def block_of(scalars, index, staged):
     if not staged:
         return index
-    z = lax.rem(scalars[Z] + lax.rem(index, 4), 4)
+    z = lax.bitwise_xor(scalars[Z], turned(lax.rem(index, 4)))
     x = jnp.where(index < 4, scalars[X], 1 - scalars[X])
     return 4 * x + z
 
@@ -590,31 +642,34 @@
     )
 
 
-def quarter_kernel(scalars, keep_ref, got_ref, *outs):
+def halve_kernel(scalars, keep_ref, got_ref, *outs):
     rows = outs[0].shape[0]
     for index, out in enumerate(outs):
         at = slice(index * rows, index * rows + rows)
         out[...] = (keep_ref[at, :].astype(F32) + got_ref[at, :].astype(F32)).astype(B16)
 
 
-def place_blocks(scalars, quarter, other):
-    rows = quarter[0].shape[0]
+def halves_sum(scalars, keep, got):
+    rows, width = keep.shape
+    return call(halve_kernel, "halve", scalars, [keep, got], [((rows // 2, width), B16)] * 2)
+
+
+def place_blocks(scalars, pieces):
     result = []
-    for half in (0, 1):
+    for half, piece in enumerate(pieces):
         x = scalars[X] if half == 0 else 1 - scalars[X]
+        rows = piece.shape[0] // 4
         for index in range(4):
-            z = lax.rem(scalars[Z] + 4 - index, 4)
-            at = slice(index * rows, index * rows + rows)
-            value = quarter[index][...] if half == 0 else other[at, :]
-            result.append((value, 4 * x + z))
+            z = lax.bitwise_xor(scalars[Z], 2 * (index % 2) + index // 2)
+            result.append((piece[index * rows : index * rows + rows, :], 4 * x + z))
     return result
 
 
 def place_kernel(scalars, *refs):
-    quarter, other, out_ref, buffer, sems = refs[:4], refs[4], refs[5], refs[6], refs[7]
-    rows = quarter[0].shape[0]
+    pieces, (out_ref, buffer, sems) = refs[:2], refs[2:]
+    rows = buffer.shape[1]
     copies = []
-    for index, (value, spot) in enumerate(place_blocks(scalars, quarter, other)):
+    for index, (value, spot) in enumerate(place_blocks(scalars, pieces)):
         buffer[index] = value.astype(F32)
         target = out_ref.at[pl.ds(pl.multiple_of(spot * rows, rows), rows), :]
         copy = pltpu.make_async_copy(buffer.at[index], target, sems.at[index])
@@ -624,13 +679,13 @@
         copy.wait()
 
 
-def place(scalars, quarter, other):
-    rows, width = quarter[0].shape
+def place(scalars, pieces):
+    rows, width = pieces[0].shape[0] // 4, pieces[0].shape[1]
     (out,) = call(
         place_kernel,
         "place",
         scalars,
-        [*quarter, other],
+        pieces,
         [((8 * rows, width), F32)],
         out_specs=[anywhere()],
         scratch=[pltpu.VMEM((8, rows, width), F32), pltpu.SemaphoreType.DMA((8,))],
@@ -639,12 +694,11 @@
 
 
 def place_heads_kernel(pair, has_out, aliased, scalars, *refs):
-    quarter, other = refs[:4], refs[4]
-    refs = refs[5 + aliased :]
+    pieces, refs = refs[:2], refs[2 + aliased :]
     qkv_ref, refs = refs[0], refs[1:]
     out_ref, (rows_ref, buffer, sems) = refs[0] if has_out else None, refs[-3:]
-    rows = quarter[0].shape[0]
-    for value, spot in place_blocks(scalars, quarter, other):
+    for value, spot in place_blocks(scalars, pieces):
+        rows = value.shape[0]
         rows_ref[pl.ds(pl.multiple_of(spot * rows, 16), rows), :] = value.astype(F32)
     copies = []
     if has_out:
@@ -663,12 +717,11 @@
         copy.wait()
 
 
-def place_heads(scalars, quarter, other, pair, pairs, into):
-    rows, width = quarter[0].shape
-    total = 8 * rows
+def place_heads(scalars, pieces, pair, pairs, into):
+    total, width = 2 * pieces[0].shape[0], pieces[0].shape[1]
     has_out = total > 384
-    inputs = [*quarter, other] + ([] if into is None else [into])
-    in_specs = [once(v.shape) for v in [*quarter, other]]
+    inputs = list(pieces) + ([] if into is None else [into])
+    in_specs = [once(v.shape) for v in pieces]
     in_specs += [] if into is None else [anywhere()]
     outs = [((3, width, pairs * 128), F32)]
     outs += [((total - 384, width), F32)] if has_out else []
@@ -685,53 +738,45 @@
             pltpu.VMEM((3, width, 128), F32),
             pltpu.SemaphoreType.DMA((4,)),
         ],
-        aliases={} if into is None else {6: 0},
+        aliases={} if into is None else {3: 0},
     )
 
 
 class DpSum:
-    swap = [(i, i ^ 1) for i in range(8)]
-
     def __init__(self, scalars, order, keep, send):
         self.scalars, self.order, self.keep = scalars, order, keep
-        self.got = lax.ppermute(send, "dp", self.swap)
+        self.got = self.exchanged(send, 1)
         self.steps = self.run()
 
-    def shifted(self, value):
-        return lax.ppermute(value, "dp", [(d, (d + 2) % 8) for d in range(8)])
+    def exchanged(self, value, bit):
+        return lax.ppermute(value, "dp", [(i, i ^ bit) for i in range(8)])
+
+    def entered(self):
+        (got,) = self.order.enter(self.got)
+        return got
 
     def run(self):
-        order = self.order
-        (got,) = order.enter(self.got)
-        rows, width = self.keep.shape
-        blocks = call(
-            quarter_kernel,
-            "quarter",
-            self.scalars,
-            [self.keep, got],
-            [((rows // 4, width), B16)] * 4,
-        )
-        order.leave(*blocks)
-        got = self.shifted(blocks[3])
+        keep, send = halves_sum(self.scalars, self.keep, self.entered())
+        self.order.leave(keep, send)
+        self.got = self.exchanged(send, 2)
         yield
-        for block in (blocks[2], blocks[1], blocks[0]):
-            (got,) = order.enter(got)
-            total = (block.astype(F32) + got.astype(F32)).astype(B16)
-            order.leave(total)
-            got = self.shifted(total)
+        keep, send = halves_sum(self.scalars, keep, self.entered())
+        self.order.leave(keep, send)
+        self.got = self.exchanged(send, 4)
+        yield
+        total = (keep.astype(F32) + self.entered().astype(F32)).astype(B16)
+        self.order.leave(total)
+        for bit in (4, 2):
+            self.got = self.exchanged(total, bit)
             yield
-        self.quarter = [total]
-        for _ in range(2):
-            (got,) = order.enter(got)
-            order.leave(got)
-            self.quarter.append(got)
-            got = self.shifted(got)
-            yield
-        (got,) = order.enter(got)
-        self.quarter.append(got)
-        half = jnp.concatenate(self.quarter, axis=0)
-        order.leave(half)
-        self.other = lax.ppermute(half, "dp", self.swap)
+            total = jnp.concatenate([total, self.entered()], axis=0)
+            self.order.leave(total)
+        self.total = total
+        self.got = self.exchanged(total, 1)
+        yield
+
+    def pieces(self):
+        return [self.total, self.entered()]
 
 
 class Order:
@@ -1141,8 +1186,7 @@
                 next(total.steps, None)
 
     def placed(total):
-        (got,) = order.enter(total.other)
-        out = place(scalars, total.quarter, got)
+        out = place(scalars, total.pieces())
         order.leave(out)
         return out
 
@@ -1179,84 +1223,93 @@
         row.last()
         row.feed_back(0, ups, downs)
     lead.middle_back()
-    for row in others:
-        if split:
-            row.feed_back(1, ups, downs)
-    downs_sum = summed(kept("act"), kept("ffn_grad"))
-    ups_sum = summed(kept("ffn_in"), kept("hidden_grad"))
-    lead.out_back(outs)
-    lead.attend_back(0)
-    for row in others:
-        row.middle_back()
-    tick(downs_sum)
-    for pair in range(1, pairs):
-        lead.attend_back(pair)
-    tick(downs_sum)
-    for row in others:
-        row.out_back(outs)
-        row.attend_back(0)
-    tick(downs_sum, ups_sum)
-    heads = [heads_summed(0, True)]
-    tick(downs_sum, ups_sum)
-    lead.project_back(qkvs)
-    tick(ups_sum, downs_sum)
-    for pair in range(1, pairs):
-        for row in others:
+    other = others[0]
+
+    def attend_back(row, pair):
+        if pair < pairs:
             row.attend_back(pair)
-        tick(downs_sum, ups_sum)
-        heads.append(heads_summed(pair, False))
-    tick(heads[0], downs_sum, ups_sum)
-    for row in others:
-        row.project_back(qkvs)
-    tick(heads[0], ups_sum)
-    lead.first_back()
-    tick(*heads, ups_sum)
-    for row in others:
-        row.first_back()
-    tick(*heads)
-    stats = [row.stat_first for row in rows] + [row.stat_middle for row in rows]
-    stats += [row.stat_last for row in rows] + [row.stat_back for row in rows]
-    (small,) = call(
-        functools.partial(small_kernel, row_count, share),
-        "small",
-        scalars,
-        list(order.enter(*stats)),
-        [((16, width), F32)],
-    )
-    order.leave(small)
-    steps = [("tensor", 1 << i) for i in range(t_size.bit_length() - 1)]
-    steps += [("dp", 1 << i) for i in range(d_size.bit_length() - 1)]
+
+    def head_sum(pair):
+        if pair < pairs:
+            sums["Q" if pair else "P"] = heads_summed(pair, pair == 0)
+
+    def small_sums():
+        stats = [row.stat_first for row in rows] + [row.stat_middle for row in rows]
+        stats += [row.stat_last for row in rows] + [row.stat_back for row in rows]
+        (values,) = call(
+            functools.partial(small_kernel, row_count, share),
+            "small",
+            scalars,
+            list(order.enter(*stats)),
+            [((16, width), F32)],
+        )
+        order.leave(values)
+        sums["S"] = values
+
     powers = t_size & (t_size - 1) == 0 and d_size & (d_size - 1) == 0
-    if powers:
-        for index, (axis, step) in enumerate(steps):
-            small = doubling(small, axis, step)
-            (small,) = order.enter(small)
-            order.leave(small)
-            tick(*heads)
-            if index == 2 and staged:
-                grad_down = placed(downs_sum)
-    else:
-        small = lax.psum(small, ("dp", "tensor"))
+    hops = [("tensor", 1 << k) for k in range(t_size.bit_length() - 1)]
+    hops += [("dp", 1 << k) for k in range(1, d_size.bit_length() - 1)] + [("dp", 1)]
+
+    def hop():
+        axis, step = hops.pop(0)
+        values = doubling(sums["S"], axis, step)
+        if hops:
+            (values,) = order.enter(values)
+            order.leave(values)
+        sums["S"] = values
+
+    sums, placed_sums = {}, {}
+    stages = {
+        "FB1": lambda: other.feed_back(1, ups, downs) if split else None,
+        "OB0": lambda: lead.out_back(outs),
+        "OB1": lambda: other.out_back(outs),
+        "WD": lambda: sums.update(D=summed(kept("act"), kept("ffn_grad"))),
+        "WU": lambda: sums.update(U=summed(kept("ffn_in"), kept("hidden_grad"))),
+        "MB1": other.middle_back,
+        "AB00": lambda: attend_back(lead, 0),
+        "AB01": lambda: attend_back(lead, 1),
+        "AB10": lambda: attend_back(other, 0),
+        "AB11": lambda: attend_back(other, 1),
+        "HP": lambda: head_sum(0),
+        "HQ": lambda: head_sum(1),
+        "PB0": lambda: lead.project_back(qkvs),
+        "PB1": lambda: other.project_back(qkvs),
+        "FL0": lead.first_back,
+        "FL1": other.first_back,
+        "SM": small_sums,
+    }
+    for stage in STAGES:
+        if stage in stages:
+            stages[stage]()
+        elif stage == "S":
+            if powers and hops:
+                hop()
+        elif staged and stage in ("PD", "PU"):
+            placed_sums[stage] = placed(sums[stage[1]])
+        elif staged and stage in sums:
+            tick(sums[stage])
+    while powers and hops:
+        hop()
+    small = sums["S"] if powers else lax.psum(sums["S"], ("dp", "tensor"))
+    heads = [sums[name] for name in ("P", "Q") if name in sums]
     if staged:
-        tick(*heads)
-        grad_up = placed(ups_sum)
-        (got,) = order.enter(heads[0].other)
-        grad_qkv, grad_out = place_heads(scalars, heads[0].quarter, got, 0, pairs, None)
+        grad_down, grad_up = placed_sums["PD"], placed_sums["PU"]
+        pieces = heads[0].pieces()
+        grad_qkv, grad_out = place_heads(scalars, pieces, 0, pairs, None)
         order.leave(grad_out)
         for pair in range(1, pairs):
-            (grad_qkv,) = place_heads(
-                scalars, heads[pair].quarter, heads[pair].other, pair, pairs, grad_qkv
-            )
+            pieces = heads[pair].pieces()
+            (grad_qkv,) = place_heads(scalars, pieces, pair, pairs, grad_qkv)
         grad_qkv = grad_qkv.transpose(1, 0, 2)
     else:
         grad_down, grad_up, *blocks = [
-            v.astype(F32) for v in lax.psum((downs_sum, ups_sum, *heads), "dp")
+            v.astype(F32) for v in lax.psum((sums["D"], sums["U"], *heads), "dp")
         ]
         grad_out = blocks[0][384:]
         blocks = [grad[:384].reshape(3, 128, width) for grad in blocks]
         grad_qkv = jnp.concatenate(blocks, axis=1).transpose(2, 0, 1)
-    sums = small[8 : 8 + GROUPS]
-    group_rms = jnp.sqrt(sums[:, :3] / (sums[:, 3:4] * width))
+    group = small[8 : 8 + GROUPS]
+    group_rms = jnp.sqrt(group[:, :3] / (group[:, 3:4] * width))
     return (
         jnp.stack([row.output for row in rows]),
         jnp.stack([row.input_grad for row in rows]),

time: 396 us -> 382 us (0.965)
  waiting for transfers between devices: 160 us -> 143 us
    ppermute x32 -> x24, waiting for transfers between devices: 71.4 us -> 52.4 us  [exchanged(): return lax.ppermute(value, 'dp', [(i, i ^ bit) for i in range(8)])]
    ppermute x5, waiting for transfers between devices: 11.4 us -> 18.8 us  [doubling(): lax.ppermute(values, axis, [(i, i ^ step) for i in range(size)])]
    ppermute x16, waiting for transfers between devices: 71.8 us -> 64.5 us  [swap_chip(): return lax.ppermute(value, 'tensor', [(0, 2), (2, 0), (1, 3), (3, 1)])]
    pallas_call x46 -> x50, Pallas kernels: 144 us -> 147 us  [call(): pl.pallas_call(kernel, out_shape=[jax.ShapeDtypeStruct(shape, dtype) for...]
    unnamed x88 -> x100, local copies, waits for them, and re-layouts: 13.8 us -> 12.4 us
    ppermute x32 -> x24, starting transfers between devices: 29 us -> 29.7 us  [exchanged(): return lax.ppermute(value, 'dp', [(i, i ^ bit) for i in range(8)])]
  transfers between devices with their start and end apart: 93 -> 85, of which waited for: 47 -> 35; matrix products, arithmetic and copies ran while one was open for 1% -> 1% of each run, Pallas kernels for 34% -> 38%
where the time goes in v4:
time: 382 us; the launch traced here: 378 us
  Pallas kernels  147 us (38%)
  waiting for transfers between devices  143 us (37%)
  starting transfers between devices  69.9 us (18%)
  local copies, waits for them, and re-layouts  13.7 us (4%)
    pallas_call x50, Pallas kernels, call(): pl.pallas_call(kernel, out_shape=[jax.ShapeDtypeStruct(shape, dtype) for...  147 us
    ppermute x16, waiting for transfers between devices, swap_chip(): return lax.ppermute(value, 'tensor', [(0, 2), (2, 0), (1, 3), (3, 1)])  64.5 us
    ppermute x24, waiting for transfers between devices, exchanged(): return lax.ppermute(value, 'dp', [(i, i ^ bit) for i in range(8)])  52.4 us
    ppermute x24, starting transfers between devices, exchanged(): return lax.ppermute(value, 'dp', [(i, i ^ bit) for i in range(8)])  29.7 us
    ppermute x16, starting transfers between devices, swap_chip(): return lax.ppermute(value, 'tensor', [(0, 2), (2, 0), (1, 3), (3, 1)])  25 us
    ppermute x5, waiting for transfers between devices, doubling(): lax.ppermute(values, axis, [(i, i ^ step) for i in range(size)])  18.8 us
    unnamed x100, local copies, waits for them, and re-layouts  12.4 us
    ppermute x40, starting transfers between devices, swap_core(): return lax.ppermute(value, 'tensor', [(0, 1), (1, 0), (2, 3), (3, 2)])  8.82 us
  transfers between devices with their start and end apart: 85, of which 35 were waited for; matrix products, arithmetic and copies ran while one was open for 1% of the time, Pallas kernels for 38%

profile of v4, /device:TPU:0, one launch (start us, length us, event | category | flops | bytes accessed | tf_op | source)
XLA Modules:
  0.0 378.3 jit_solution(6701561582026897982)
XLA Ops:
  13.7 8.2 %collective-permute-done.2.x_ref.refs_5_ = bf16[272,1024]{1,0:T(8,128)(2,1)S(1)} collective-permute-done((bf16[272,1024]{1,0:T(8,128)(2,1)S(1)}, bf16[272,1024]{1,0:T(8,128)(2,1)S(1)}, u32[]{:S(2)}, u32[]{:S(2)}) %collective-permute-start.2) | collective-permute-done | bytes 557088 | tf_op jit(solution)/shard_map/ppermute | solution.py:964
  27.6 8.0 %attend.2 = (bf16[544,256]{1,0:T(8,128)(2,1)S(1)}, bf16[544,256]{1,0:T(8,128)(2,1)S(1)}, f32[4,1,1088]{2,1,0:T(1,128)S(1)}) custom-call(s32[8]{0:T(128)S(1)} %concatenate.31.scalars, bf16[272,768]{1,0:T(8,128)(2,1)S(1)} %get-tuple-element.302.refs_0_.refs_4_.refs_8_, bf16[272,768]{1,0:T(8,128)(2,1)S(1)} %collective-permute-done.1.refs_1_.refs_5_.refs_9_, ...), custom_call_target="tpu_custom_call" | custom-call | flops 75759616 | bytes 156672 | tf_op jit(solution)/shard_map/attend/pallas_call | solution.py:114
  35.6 4.4 %collective-permute-done.7.x_ref.refs_9_ = bf16[272,1024]{1,0:T(8,128)(2,1)S(1)} collective-permute-done((bf16[272,1024]{1,0:T(8,128)(2,1)S(1)}, bf16[272,1024]{1,0:T(8,128)(2,1)S(1)}, u32[]{:S(2)}, u32[]{:S(2)}) %collective-permute-start.7) | collective-permute-done | bytes 557088 | tf_op jit(solution)/shard_map/ppermute | solution.py:964
  48.2 8.0 %attend.3 = (bf16[544,256]{1,0:T(8,128)(2,1)S(1)}, bf16[544,256]{1,0:T(8,128)(2,1)S(1)}, f32[4,1,1088]{2,1,0:T(1,128)S(1)}) custom-call(s32[8]{0:T(128)S(1)} %concatenate.31.scalars, bf16[272,768]{1,0:T(8,128)(2,1)S(1)} %get-tuple-element.315.refs_0_.refs_4_.refs_8_, bf16[272,768]{1,0:T(8,128)(2,1)S(1)} %collective-permute-done.11.refs_1_.refs_5_.refs_9_, ...), custom_call_target="tpu_custom_call" | custom-call | flops 75759616 | bytes 156672 | tf_op jit(solution)/shard_map/attend/pallas_call | solution.py:114
  66.0 3.6 feed.4
  70.9 5.7 %collective-permute-done.17.x_ref.refs_1_ = bf16[272,1024]{1,0:T(8,128)(2,1)S(1)} collective-permute-done((bf16[272,1024]{1,0:T(8,128)(2,1)S(1)}, bf16[272,1024]{1,0:T(8,128)(2,1)S(1)}, u32[]{:S(2)}, u32[]{:S(2)}) %collective-permute-start.17) | collective-permute-done | bytes 557088 | tf_op jit(solution)/shard_map/ppermute | solution.py:964
  76.6 3.5 feed.5
  83.3 5.3 %collective-permute-done.19.refs_1_ = bf16[272,1024]{1,0:T(8,128)(2,1)S(1)} collective-permute-done((bf16[272,1024]{1,0:T(8,128)(2,1)S(1)}, bf16[272,1024]{1,0:T(8,128)(2,1)S(1)}, u32[]{:S(2)}, u32[]{:S(2)}) %collective-permute-start.19) | collective-permute-done | bytes 557088 | tf_op jit(solution)/shard_map/ppermute | solution.py:964
  90.9 3.5 feed.6
  96.7 3.6 collective-permute-done.18.refs_1_
  112.3 3.5 feed.7
  117.7 6.6 %collective-permute-done.28.x_ref.refs_9_ = bf16[272,1024]{1,0:T(8,128)(2,1)S(1)} collective-permute-done((bf16[272,1024]{1,0:T(8,128)(2,1)S(1)}, bf16[272,1024]{1,0:T(8,128)(2,1)S(1)}, u32[]{:S(2)}, u32[]{:S(2)}) %collective-permute-start.28) | collective-permute-done | bytes 557088 | tf_op jit(solution)/shard_map/ppermute | solution.py:964
  128.0 6.9 %collective-permute-done.27.refs_1_ = bf16[272,1024]{1,0:T(8,128)(2,1)S(1)} collective-permute-done((bf16[272,1024]{1,0:T(8,128)(2,1)S(1)}, bf16[272,1024]{1,0:T(8,128)(2,1)S(1)}, u32[]{:S(2)}, u32[]{:S(2)}) %collective-permute-start.27) | collective-permute-done | bytes 557088 | tf_op jit(solution)/shard_map/ppermute | solution.py:964
  144.2 6.2 %collective-permute-done.33.refs_1_ = bf16[272,1024]{1,0:T(8,128)(2,1)S(1)} collective-permute-done((bf16[272,1024]{1,0:T(8,128)(2,1)S(1)}, bf16[272,1024]{1,0:T(8,128)(2,1)S(1)}, u32[]{:S(2)}, u32[]{:S(2)}) %collective-permute-start.33) | collective-permute-done | bytes 557088 | tf_op jit(solution)/shard_map/ppermute | solution.py:964
  154.7 7.7 %collective-permute-done.37.x_ref.refs_13_ = bf16[272,1024]{1,0:T(8,128)(2,1)S(1)} collective-permute-done((bf16[272,1024]{1,0:T(8,128)(2,1)S(1)}, bf16[272,1024]{1,0:T(8,128)(2,1)S(1)}, u32[]{:S(2)}, u32[]{:S(2)}) %collective-permute-start.37) | collective-permute-done | bytes 557088 | tf_op jit(solution)/shard_map/ppermute | solution.py:964
  168.4 3.6 collective-permute-done.36.refs_1_.refs_17_
  175.9 8.0 %outer_sum.2 = (bf16[512,1024]{1,0:T(8,128)(2,1)S(1)}, bf16[512,1024]{1,0:T(8,128)(2,1)S(1)}) custom-call(s32[8]{0:T(128)S(1)} %concatenate.31.scalars, bf16[272,1024]{1,0:T(8,128)(2,1)S(1)} %copy-done.11, bf16[272,1024]{1,0:T(8,128)(2,1)S(1)} %copy-done.15, bf16[272,1024]{1,0:T(8,128)(2,1)S(1)} %copy-done.13, bf16[272,1024]{1,0:T(8,128)(2,1)S(1)} %copy-done.17, ...), custom_call_target="tpu_custom_call" | custom-call | flops 285212672 | bytes 278528 | tf_op jit(solution)/shard_map/outer_sum/pallas_call | solution.py:114
  185.6 8.0 %outer_sum.3 = (bf16[512,1024]{1,0:T(8,128)(2,1)S(1)}, bf16[512,1024]{1,0:T(8,128)(2,1)S(1)}) custom-call(s32[8]{0:T(128)S(1)} %concatenate.31.scalars, bf16[272,1024]{1,0:T(8,128)(2,1)S(1)} %get-tuple-element.407.x_ref.refs_0_, bf16[272,1024]{1,0:T(8,128)(2,1)S(1)} %collective-permute-done.17.x_ref.refs_1_, ...), custom_call_target="tpu_custom_call" | custom-call | flops 285212672 | bytes 278528 | tf_op jit(solution)/shard_map/outer_sum/pallas_call | solution.py:114
  196.4 6.9 %attend_back.4 = (bf16[544,384]{1,0:T(8,128)(2,1)S(1)}, bf16[544,384]{1,0:T(8,128)(2,1)S(1)}) custom-call(s32[8]{0:T(128)S(1)} %concatenate.31.scalars, bf16[272,768]{1,0:T(8,128)(2,1)S(1)} %get-tuple-element.302.refs_0_.refs_4_.refs_8_, bf16[272,768]{1,0:T(8,128)(2,1)S(1)} %collective-permute-done.1.refs_1_.refs_5_.refs_9_, ...), custom_call_target="tpu_custom_call" | custom-call | flops 94699520 | bytes 191760 | tf_op jit(solution)/shard_map/attend_back/pallas_call | solution.py:114
  203.6 6.7 %attend_back.5 = (bf16[544,384]{1,0:T(8,128)(2,1)S(1)}, bf16[544,384]{1,0:T(8,128)(2,1)S(1)}) custom-call(s32[8]{0:T(128)S(1)} %concatenate.31.scalars, bf16[272,768]{1,0:T(8,128)(2,1)S(1)} %get-tuple-element.302.refs_0_.refs_4_.refs_8_, bf16[272,768]{1,0:T(8,128)(2,1)S(1)} %collective-permute-done.1.refs_1_.refs_5_.refs_9_, ...), custom_call_target="tpu_custom_call" | custom-call | flops 94699520 | bytes 191760 | tf_op jit(solution)/shard_map/attend_back/pallas_call | solution.py:114
  217.2 6.7 %attend_back.6 = (bf16[544,384]{1,0:T(8,128)(2,1)S(1)}, bf16[544,384]{1,0:T(8,128)(2,1)S(1)}) custom-call(s32[8]{0:T(128)S(1)} %concatenate.31.scalars, bf16[272,768]{1,0:T(8,128)(2,1)S(1)} %get-tuple-element.315.refs_0_.refs_4_.refs_8_, bf16[272,768]{1,0:T(8,128)(2,1)S(1)} %collective-permute-done.11.refs_1_.refs_5_.refs_9_, ...), custom_call_target="tpu_custom_call" | custom-call | flops 94699520 | bytes 191760 | tf_op jit(solution)/shard_map/attend_back/pallas_call | solution.py:114
  230.1 8.0 %head_outer.2 = (bf16[320,1024]{1,0:T(8,128)(2,1)S(1)}, bf16[320,1024]{1,0:T(8,128)(2,1)S(1)}) custom-call(s32[8]{0:T(128)S(1)} %concatenate.31.scalars, bf16[544,384]{1,0:T(8,128)(2,1)S(1)} %get-tuple-element.482.refs_0_, bf16[544,384]{1,0:T(8,128)(2,1)S(1)} %get-tuple-element.454.refs_1_, bf16[544,384]{1,0:T(8,128)(2,1)S(1)} %get-tuple-element.511.refs_2_.refs_0_, ...), custom_call_target="tpu_custom_call" | custom-call | flops 178257920 | bytes 365568 | tf_op jit(solution)/shard_map/head_outer/pallas_call | solution.py:114
  243.1 6.7 %attend_back.7 = (bf16[544,384]{1,0:T(8,128)(2,1)S(1)}, bf16[544,384]{1,0:T(8,128)(2,1)S(1)}) custom-call(s32[8]{0:T(128)S(1)} %concatenate.31.scalars, bf16[272,768]{1,0:T(8,128)(2,1)S(1)} %get-tuple-element.315.refs_0_.refs_4_.refs_8_, bf16[272,768]{1,0:T(8,128)(2,1)S(1)} %collective-permute-done.11.refs_1_.refs_5_.refs_9_, ...), custom_call_target="tpu_custom_call" | custom-call | flops 94699520 | bytes 191760 | tf_op jit(solution)/shard_map/attend_back/pallas_call | solution.py:114
  253.6 5.5 %head_outer.3 = (bf16[192,1024]{1,0:T(8,128)(2,1)S(1)}, bf16[192,1024]{1,0:T(8,128)(2,1)S(1)}) custom-call(s32[8]{0:T(128)S(1)} %concatenate.31.scalars, bf16[544,384]{1,0:T(8,128)(2,1)S(1)} %get-tuple-element.496.refs_1_.refs_0_, bf16[544,384]{1,0:T(8,128)(2,1)S(1)} %get-tuple-element.497.refs_1_, bf16[544,384]{1,0:T(8,128)(2,1)S(1)} %get-tuple-element.512.refs_2_.refs_1_, ...), custom_call_target="tpu_custom_call" | custom-call | flops 106954752 | bytes 191488 | tf_op jit(solution)/shard_map/head_outer/pallas_call | solution.py:114
  260.1 4.9 %collective-permute-done.63 = bf16[128,1024]{1,0:T(8,128)(2,1)S(1)} collective-permute-done((bf16[128,1024]{1,0:T(8,128)(2,1)S(1)}, bf16[128,1024]{1,0:T(8,128)(2,1)S(1)}, u32[]{:S(2)}, u32[]{:S(2)}) %collective-permute-start.63) | collective-permute-done | bytes 262176 | tf_op jit(solution)/shard_map/ppermute | solution.py:752
  271.2 4.4 %collective-permute-done.61.got_ref = bf16[192,1024]{1,0:T(8,128)(2,1)S(1)} collective-permute-done((bf16[192,1024]{1,0:T(8,128)(2,1)S(1)}, bf16[192,1024]{1,0:T(8,128)(2,1)S(1)}, u32[]{:S(2)}, u32[]{:S(2)}) %collective-permute-start.61) | collective-permute-done | bytes 393248 | tf_op jit(solution)/shard_map/ppermute | solution.py:752
  276.3 6.7 %collective-permute-done.59 = bf16[128,1024]{1,0:T(8,128)(2,1)S(1)} collective-permute-done((bf16[128,1024]{1,0:T(8,128)(2,1)S(1)}, bf16[128,1024]{1,0:T(8,128)(2,1)S(1)}, u32[]{:S(2)}, u32[]{:S(2)}) %collective-permute-start.59) | collective-permute-done | bytes 262176 | tf_op jit(solution)/shard_map/ppermute | solution.py:752
  289.4 7.4 %collective-permute-done.65.got_ref = bf16[160,1024]{1,0:T(8,128)(2,1)S(1)} collective-permute-done((bf16[160,1024]{1,0:T(8,128)(2,1)S(1)}, bf16[160,1024]{1,0:T(8,128)(2,1)S(1)}, u32[]{:S(2)}, u32[]{:S(2)}) %collective-permute-start.65) | collective-permute-done | bytes 327712 | tf_op jit(solution)/shard_map/ppermute | solution.py:752
  303.6 10.2 %collective-permute-done.70 = bf16[80,1024]{1,0:T(8,128)(2,1)S(1)} collective-permute-done((bf16[80,1024]{1,0:T(8,128)(2,1)S(1)}, bf16[80,1024]{1,0:T(8,128)(2,1)S(1)}, u32[]{:S(2)}, u32[]{:S(2)}) %collective-permute-start.70) | collective-permute-done | bytes 163872 | tf_op jit(solution)/shard_map/ppermute | solution.py:752
  317.3 3.8 %collective-permute-done.69.got_ref = bf16[96,1024]{1,0:T(8,128)(2,1)S(1)} collective-permute-done((bf16[96,1024]{1,0:T(8,128)(2,1)S(1)}, bf16[96,1024]{1,0:T(8,128)(2,1)S(1)}, u32[]{:S(2)}, u32[]{:S(2)}) %collective-permute-start.69) | collective-permute-done | bytes 196640 | tf_op jit(solution)/shard_map/ppermute | solution.py:752
  332.1 6.7 %collective-permute-done.75 = bf16[160,1024]{1,0:T(8,128)(2,1)S(1)} collective-permute-done((bf16[160,1024]{1,0:T(8,128)(2,1)S(1)}, bf16[160,1024]{1,0:T(8,128)(2,1)S(1)}, u32[]{:S(2)}, u32[]{:S(2)}) %collective-permute-start.75) | collective-permute-done | bytes 327712 | tf_op jit(solution)/shard_map/ppermute | solution.py:752
  359.7 10.4 %collective-permute-done.84 = f32[16,1024]{1,0:T(8,128)S(1)} collective-permute-done((f32[16,1024]{1,0:T(8,128)S(1)}, f32[16,1024]{1,0:T(8,128)S(1)}, u32[]{:S(2)}, u32[]{:S(2)}) %collective-permute-start.84) | collective-permute-done | bytes 65568 | tf_op jit(solution)/shard_map/ppermute | solution.py:1126
  (310 shorter events, 176.8 us)
Async XLA Ops:
  6.1 15.8 %collective-permute-start.2 = (bf16[272,1024]{1,0:T(8,128)(2,1)S(1)}, bf16[272,1024]{1,0:T(8,128)(2,1)S(1)}, u32[]{:S(2)}, u32[]{:S(2)}) collective-permute-start(bf16[272,1024]{1,0:T(8,128)(2,1)S(1)} %get-tuple-element.500.x_ref.refs_4_), channel_id=1, source_target_pairs={{0,2},{2,0},{1,3},{3,1},{4,6},{6,4},{5,7},{7,5},{8,10},{10,8},{9,1... | collective-permute-start | bytes 1671176 | tf_op jit(solution)/shard_map/ppermute | solution.py:964
  24.2 41.9 %collective-permute-start.15 = (bf16[1024,1024]{1,0:T(8,128)(2,1)S(1)}, bf16[1024,1024]{1,0:T(8,128)(2,1)S(1)}, u32[]{:S(2)}, u32[]{:S(2)}) collective-permute-start(bf16[1024,1024]{1,0:T(8,128)(2,1)S(1)} %copy-done), channel_id=1, source_target_pairs={{0,1},{1,0},{2,3},{3,2},{4,5},{5,4},{6,7},{7,6},{8,9},{9,8},{10,11... | collective-permute-start | bytes 6291464 | tf_op jit(solution)/shard_map/ppermute | solution.py:960
  24.6 41.5 %collective-permute-start.16 = (bf16[1024,1024]{1,0:T(8,128)(2,1)S(1)}, bf16[1024,1024]{1,0:T(8,128)(2,1)S(1)}, u32[]{:S(2)}, u32[]{:S(2)}) collective-permute-start(bf16[1024,1024]{1,0:T(8,128)(2,1)S(1)} %copy-done.1), channel_id=1, source_target_pairs={{0,1},{1,0},{2,3},{3,2},{4,5},{5,4},{6,7},{7,6},{8,9},{9,8},{10,11... | collective-permute-start | bytes 6291464 | tf_op jit(solution)/shard_map/ppermute | solution.py:960
  27.1 16.2 %collective-permute-start.9 = (bf16[256,1024]{1,0:T(8,128)(2,1)S(1)}, bf16[256,1024]{1,0:T(8,128)(2,1)S(1)}, u32[]{:S(2)}, u32[]{:S(2)}) collective-permute-start(bf16[256,1024]{1,0:T(8,128)(2,1)S(1)} %copy-done.7), channel_id=1, source_target_pairs={{0,1},{1,0},{2,3},{3,2},{4,5},{5,4},{6,7},{7,6},{8,9},{9,8},{10,11... | collective-permute-start | bytes 1572872 | tf_op jit(solution)/shard_map/ppermute | solution.py:960
  65.7 22.9 %collective-permute-start.19 = (bf16[272,1024]{1,0:T(8,128)(2,1)S(1)}, bf16[272,1024]{1,0:T(8,128)(2,1)S(1)}, u32[]{:S(2)}, u32[]{:S(2)}) collective-permute-start(bf16[272,1024]{1,0:T(8,128)(2,1)S(1)} %get-tuple-element.327), channel_id=1, source_target_pairs={{0,2},{2,0},{1,3},{3,1},{4,6},{6,4},{5,7},{7,5},{8,10},{10,8},{9,1... | collective-permute-start | bytes 1671176 | tf_op jit(solution)/shard_map/ppermute | solution.py:964
  66.0 17.2 %collective-permute-start.21 = (bf16[272,1024]{1,0:T(8,128)(2,1)S(1)}, bf16[272,1024]{1,0:T(8,128)(2,1)S(1)}, u32[]{:S(2)}, u32[]{:S(2)}) collective-permute-start(bf16[272,1024]{1,0:T(8,128)(2,1)S(1)} %get-tuple-element.407.x_ref.refs_0_), channel_id=1, source_target_pairs={{0,1},{1,0},{2,3},{3,2},{4,5},{5,4},{6,7},{7,6},{8,9},{9,8},{10,11... | collective-permute-start | bytes 1671176 | tf_op jit(solution)/shard_map/ppermute | solution.py:960
  81.5 18.8 %collective-permute-start.18 = (bf16[272,1024]{1,0:T(8,128)(2,1)S(1)}, bf16[272,1024]{1,0:T(8,128)(2,1)S(1)}, u32[]{:S(2)}, u32[]{:S(2)}) collective-permute-start(bf16[272,1024]{1,0:T(8,128)(2,1)S(1)} %get-tuple-element.331), channel_id=1, source_target_pairs={{0,2},{2,0},{1,3},{3,1},{4,6},{6,4},{5,7},{7,5},{8,10},{10,8},{9,1... | collective-permute-start | bytes 1671176 | tf_op jit(solution)/shard_map/ppermute | solution.py:964
  95.0 17.3 %collective-permute-start.24 = (bf16[272,1024]{1,0:T(8,128)(2,1)S(1)}, bf16[272,1024]{1,0:T(8,128)(2,1)S(1)}, u32[]{:S(2)}, u32[]{:S(2)}) collective-permute-start(bf16[272,1024]{1,0:T(8,128)(2,1)S(1)} %get-tuple-element.411.x_ref.refs_4_), channel_id=1, source_target_pairs={{0,2},{2,0},{1,3},{3,1},{4,6},{6,4},{5,7},{7,5},{8,10},{10,8},{9,1... | collective-permute-start | bytes 1671176 | tf_op jit(solution)/shard_map/ppermute | solution.py:964
  102.6 21.6 %collective-permute-start.28 = (bf16[272,1024]{1,0:T(8,128)(2,1)S(1)}, bf16[272,1024]{1,0:T(8,128)(2,1)S(1)}, u32[]{:S(2)}, u32[]{:S(2)}) collective-permute-start(bf16[272,1024]{1,0:T(8,128)(2,1)S(1)} %get-tuple-element.397.x_ref.refs_8_), channel_id=1, source_target_pairs={{0,2},{2,0},{1,3},{3,1},{4,6},{6,4},{5,7},{7,5},{8,10},{10,8},{9,1... | collective-permute-start | bytes 1671176 | tf_op jit(solution)/shard_map/ppermute | solution.py:964
  115.9 19.0 %collective-permute-start.27 = (bf16[272,1024]{1,0:T(8,128)(2,1)S(1)}, bf16[272,1024]{1,0:T(8,128)(2,1)S(1)}, u32[]{:S(2)}, u32[]{:S(2)}) collective-permute-start(bf16[272,1024]{1,0:T(8,128)(2,1)S(1)} %get-tuple-element.350), channel_id=1, source_target_pairs={{0,2},{2,0},{1,3},{3,1},{4,6},{6,4},{5,7},{7,5},{8,10},{10,8},{9,1... | collective-permute-start | bytes 1671176 | tf_op jit(solution)/shard_map/ppermute | solution.py:964
  117.7 19.0 %collective-permute-start.32 = (bf16[272,1024]{1,0:T(8,128)(2,1)S(1)}, bf16[272,1024]{1,0:T(8,128)(2,1)S(1)}, u32[]{:S(2)}, u32[]{:S(2)}) collective-permute-start(bf16[272,1024]{1,0:T(8,128)(2,1)S(1)} %collective-permute-done.24.x_ref.refs_5_), channel_id=1, source_target_pairs={{0,1},{1,0},{2,3},{3,2},{4,5},{5,4},{6,7},{7,6},{8,9},{9,8},{10,11... | collective-permute-start | bytes 1671176 | tf_op jit(solution)/shard_map/ppermute | solution.py:960
  138.5 23.8 %collective-permute-start.37 = (bf16[272,1024]{1,0:T(8,128)(2,1)S(1)}, bf16[272,1024]{1,0:T(8,128)(2,1)S(1)}, u32[]{:S(2)}, u32[]{:S(2)}) collective-permute-start(bf16[272,1024]{1,0:T(8,128)(2,1)S(1)} %get-tuple-element.401.x_ref.refs_12_), channel_id=1, source_target_pairs={{0,2},{2,0},{1,3},{3,1},{4,6},{6,4},{5,7},{7,5},{8,10},{10,8},{9,1... | collective-permute-start | bytes 1671176 | tf_op jit(solution)/shard_map/ppermute | solution.py:964
  143.6 18.7 %collective-permute-start.38 = (bf16[272,1024]{1,0:T(8,128)(2,1)S(1)}, bf16[272,1024]{1,0:T(8,128)(2,1)S(1)}, u32[]{:S(2)}, u32[]{:S(2)}) collective-permute-start(bf16[272,1024]{1,0:T(8,128)(2,1)S(1)} %get-tuple-element.371), channel_id=1, source_target_pairs={{0,1},{1,0},{2,3},{3,2},{4,5},{5,4},{6,7},{7,6},{8,9},{9,8},{10,11... | collective-permute-start | bytes 1671176 | tf_op jit(solution)/shard_map/ppermute | solution.py:960
  143.7 19.5 %collective-permute-start.39 = (bf16[272,1024]{1,0:T(8,128)(2,1)S(1)}, bf16[272,1024]{1,0:T(8,128)(2,1)S(1)}, u32[]{:S(2)}, u32[]{:S(2)}) collective-permute-start(bf16[272,1024]{1,0:T(8,128)(2,1)S(1)} %get-tuple-element.401.x_ref.refs_12_), channel_id=1, source_target_pairs={{0,1},{1,0},{2,3},{3,2},{4,5},{5,4},{6,7},{7,6},{8,9},{9,8},{10,11... | collective-permute-start | bytes 1671176 | tf_op jit(solution)/shard_map/ppermute | solution.py:960
  152.9 19.2 %collective-permute-start.36 = (bf16[272,1024]{1,0:T(8,128)(2,1)S(1)}, bf16[272,1024]{1,0:T(8,128)(2,1)S(1)}, u32[]{:S(2)}, u32[]{:S(2)}) collective-permute-start(bf16[272,1024]{1,0:T(8,128)(2,1)S(1)} %get-tuple-element.469.refs_0_.refs_16_), channel_id=1, source_target_pairs={{0,2},{2,0},{1,3},{3,1},{4,6},{6,4},{5,7},{7,5},{8,10},{10,8},{9,1... | collective-permute-start | bytes 1671176 | tf_op jit(solution)/shard_map/ppermute | solution.py:964
  172.6 21.0 %collective-permute-start.41 = (bf16[272,1024]{1,0:T(8,128)(2,1)S(1)}, bf16[272,1024]{1,0:T(8,128)(2,1)S(1)}, u32[]{:S(2)}, u32[]{:S(2)}) collective-permute-start(bf16[272,1024]{1,0:T(8,128)(2,1)S(1)} %get-tuple-element.375), channel_id=1, source_target_pairs={{0,2},{2,0},{1,3},{3,1},{4,6},{6,4},{5,7},{7,5},{8,10},{10,8},{9,1... | collective-permute-start | bytes 1671176 | tf_op jit(solution)/shard_map/ppermute | solution.py:964
  183.9 27.1 %collective-permute-start.50 = (bf16[512,1024]{1,0:T(8,128)(2,1)S(1)}, bf16[512,1024]{1,0:T(8,128)(2,1)S(1)}, u32[]{:S(2)}, u32[]{:S(2)}) collective-permute-start(bf16[512,1024]{1,0:T(8,128)(2,1)S(1)} %get-tuple-element.406), channel_id=1, source_target_pairs={{0,4},{4,0},{8,12},{12,8},{16,20},{20,16},{24,28},{28,24},{1,5},{5... | collective-permute-start | bytes 3145736 | tf_op jit(solution)/shard_map/ppermute | solution.py:752
  195.8 16.3 %collective-permute-start.49 = (bf16[272,1024]{1,0:T(8,128)(2,1)S(1)}, bf16[272,1024]{1,0:T(8,128)(2,1)S(1)}, u32[]{:S(2)}, u32[]{:S(2)}) collective-permute-start(bf16[272,1024]{1,0:T(8,128)(2,1)S(1)} %get-tuple-element.473.refs_0_.refs_20_), channel_id=1, source_target_pairs={{0,2},{2,0},{1,3},{3,1},{4,6},{6,4},{5,7},{7,5},{8,10},{10,8},{9,1... | collective-permute-start | bytes 1671176 | tf_op jit(solution)/shard_map/ppermute | solution.py:964
  210.6 27.5 %collective-permute-start.48 = (bf16[512,1024]{1,0:T(8,128)(2,1)S(1)}, bf16[512,1024]{1,0:T(8,128)(2,1)S(1)}, u32[]{:S(2)}, u32[]{:S(2)}) collective-permute-start(bf16[512,1024]{1,0:T(8,128)(2,1)S(1)} %get-tuple-element.424), channel_id=1, source_target_pairs={{0,4},{4,0},{8,12},{12,8},{16,20},{20,16},{24,28},{28,24},{1,5},{5... | collective-permute-start | bytes 3145736 | tf_op jit(solution)/shard_map/ppermute | solution.py:752
  250.4 19.3 %collective-permute-start.62 = (bf16[320,1024]{1,0:T(8,128)(2,1)S(1)}, bf16[320,1024]{1,0:T(8,128)(2,1)S(1)}, u32[]{:S(2)}, u32[]{:S(2)}) collective-permute-start(bf16[320,1024]{1,0:T(8,128)(2,1)S(1)} %get-tuple-element.478), channel_id=1, source_target_pairs={{0,4},{4,0},{8,12},{12,8},{16,20},{20,16},{24,28},{28,24},{1,5},{5... | collective-permute-start | bytes 1966088 | tf_op jit(solution)/shard_map/ppermute | solution.py:752
  259.1 16.5 %collective-permute-start.61 = (bf16[192,1024]{1,0:T(8,128)(2,1)S(1)}, bf16[192,1024]{1,0:T(8,128)(2,1)S(1)}, u32[]{:S(2)}, u32[]{:S(2)}) collective-permute-start(bf16[192,1024]{1,0:T(8,128)(2,1)S(1)} %get-tuple-element.509), channel_id=1, source_target_pairs={{0,4},{4,0},{8,12},{12,8},{16,20},{20,16},{24,28},{28,24},{1,5},{5... | collective-permute-start | bytes 1179656 | tf_op jit(solution)/shard_map/ppermute | solution.py:752
  265.0 21.5 %collective-permute-start.66 = (bf16[256,1024]{1,0:T(8,128)(2,1)S(1)}, bf16[256,1024]{1,0:T(8,128)(2,1)S(1)}, u32[]{:S(2)}, u32[]{:S(2)}) collective-permute-start(bf16[256,1024]{1,0:T(8,128)(2,1)S(1)} %pad_maximum_fusion.5), channel_id=1, source_target_pairs={{0,8},{4,12},{8,0},{12,4},{16,24},{20,28},{24,16},{28,20},{1,9},{5... | collective-permute-start | bytes 1572872 | tf_op jit(solution)/shard_map/ppermute | solution.py:752
  265.1 17.9 %collective-permute-start.59 = (bf16[128,1024]{1,0:T(8,128)(2,1)S(1)}, bf16[128,1024]{1,0:T(8,128)(2,1)S(1)}, u32[]{:S(2)}, u32[]{:S(2)}) collective-permute-start(bf16[128,1024]{1,0:T(8,128)(2,1)S(1)} %get-tuple-element.495), channel_id=1, source_target_pairs={{0,16},{4,20},{8,24},{12,28},{16,0},{20,4},{24,8},{28,12},{1,17},{... | collective-permute-start | bytes 786440 | tf_op jit(solution)/shard_map/ppermute | solution.py:752
  270.4 26.4 %collective-permute-start.65 = (bf16[160,1024]{1,0:T(8,128)(2,1)S(1)}, bf16[160,1024]{1,0:T(8,128)(2,1)S(1)}, u32[]{:S(2)}, u32[]{:S(2)}) collective-permute-start(bf16[160,1024]{1,0:T(8,128)(2,1)S(1)} %get-tuple-element.519), channel_id=1, source_target_pairs={{0,8},{4,12},{8,0},{12,4},{16,24},{20,28},{24,16},{28,20},{1,9},{5... | collective-permute-start | bytes 983048 | tf_op jit(solution)/shard_map/ppermute | solution.py:752
  286.6 36.8 %collective-permute-start.72 = (bf16[512,1024]{1,0:T(8,128)(2,1)S(1)}, bf16[512,1024]{1,0:T(8,128)(2,1)S(1)}, u32[]{:S(2)}, u32[]{:S(2)}) collective-permute-start(bf16[512,1024]{1,0:T(8,128)(2,1)S(1)} %pad_maximum_fusion.2.refs_0_), channel_id=1, source_target_pairs={{0,4},{4,0},{8,12},{12,8},{16,20},{20,16},{24,28},{28,24},{1,5},{5... | collective-permute-start | bytes 3145736 | tf_op jit(solution)/shard_map/ppermute | solution.py:752
  297.7 24.1 %collective-permute-start.68 = (bf16[256,1024]{1,0:T(8,128)(2,1)S(1)}, bf16[256,1024]{1,0:T(8,128)(2,1)S(1)}, u32[]{:S(2)}, u32[]{:S(2)}) collective-permute-start(bf16[256,1024]{1,0:T(8,128)(2,1)S(1)} %pad_maximum_fusion.6), channel_id=1, source_target_pairs={{0,8},{4,12},{8,0},{12,4},{16,24},{20,28},{24,16},{28,20},{1,9},{5... | collective-permute-start | bytes 1572872 | tf_op jit(solution)/shard_map/ppermute | solution.py:752
  297.9 24.0 %collective-permute-start.67 = (bf16[272,1024]{1,0:T(8,128)(2,1)S(1)}, bf16[272,1024]{1,0:T(8,128)(2,1)S(1)}, u32[]{:S(2)}, u32[]{:S(2)}) collective-permute-start(bf16[272,1024]{1,0:T(8,128)(2,1)S(1)} %get-tuple-element.516), channel_id=1, source_target_pairs={{0,2},{2,0},{1,3},{3,1},{4,6},{6,4},{5,7},{7,5},{8,10},{10,8},{9,1... | collective-permute-start | bytes 1671176 | tf_op jit(solution)/shard_map/ppermute | solution.py:964
  302.0 19.2 %collective-permute-start.69 = (bf16[96,1024]{1,0:T(8,128)(2,1)S(1)}, bf16[96,1024]{1,0:T(8,128)(2,1)S(1)}, u32[]{:S(2)}, u32[]{:S(2)}) collective-permute-start(bf16[96,1024]{1,0:T(8,128)(2,1)S(1)} %get-tuple-element.522), channel_id=1, source_target_pairs={{0,8},{4,12},{8,0},{12,4},{16,24},{20,28},{24,16},{28,20},{1,9},{5... | collective-permute-start | bytes 589832 | tf_op jit(solution)/shard_map/ppermute | solution.py:752
  328.5 28.5 %collective-permute-start.81 = (bf16[512,1024]{1,0:T(8,128)(2,1)S(1)}, bf16[512,1024]{1,0:T(8,128)(2,1)S(1)}, u32[]{:S(2)}, u32[]{:S(2)}) collective-permute-start(bf16[512,1024]{1,0:T(8,128)(2,1)S(1)} %pad_maximum_fusion.3.refs_0_), channel_id=1, source_target_pairs={{0,4},{4,0},{8,12},{12,8},{16,20},{20,16},{24,28},{28,24},{1,5},{5... | collective-permute-start | bytes 3145736 | tf_op jit(solution)/shard_map/ppermute | solution.py:752
  350.4 21.2 %collective-permute-start.80 = (bf16[320,1024]{1,0:T(8,128)(2,1)S(1)}, bf16[320,1024]{1,0:T(8,128)(2,1)S(1)}, u32[]{:S(2)}, u32[]{:S(2)}) collective-permute-start(bf16[320,1024]{1,0:T(8,128)(2,1)S(1)} %pad_maximum_fusion.4.refs_0_), channel_id=1, source_target_pairs={{0,4},{4,0},{8,12},{12,8},{16,20},{20,16},{24,28},{28,24},{1,5},{5... | collective-permute-start | bytes 1966088 | tf_op jit(solution)/shard_map/ppermute | solution.py:752
  353.4 16.7 %collective-permute-start.84 = (f32[16,1024]{1,0:T(8,128)S(1)}, f32[16,1024]{1,0:T(8,128)S(1)}, u32[]{:S(2)}, u32[]{:S(2)}) collective-permute-start(f32[16,1024]{1,0:T(8,128)S(1)} %add.40), channel_id=1, source_target_pairs={{0,4},{4,0},{8,12},{12,8},{16,20},{20,16},{24,28},{28,24},{1,5},{5... | collective-permute-start | bytes 196616 | tf_op jit(solution)/shard_map/ppermute | solution.py:1126
  356.0 20.1 %collective-permute-start.79 = (bf16[192,1024]{1,0:T(8,128)(2,1)S(1)}, bf16[192,1024]{1,0:T(8,128)(2,1)S(1)}, u32[]{:S(2)}, u32[]{:S(2)}) collective-permute-start(bf16[192,1024]{1,0:T(8,128)(2,1)S(1)} %pad_maximum_fusion.7.refs_0_), channel_id=1, source_target_pairs={{0,4},{4,0},{8,12},{12,8},{16,20},{20,16},{24,28},{28,24},{1,5},{5... | collective-permute-start | bytes 1179656 | tf_op jit(solution)/shard_map/ppermute | solution.py:752
  (103 other events, 833.8 us)

commit v5 on v4

--- a/solution.py
+++ b/solution.py
@@ -493,16 +493,12 @@
     )
 
 
-def turned(index):
-    return 2 * lax.rem(index, 2) + index // 2
-
-
-def block_of(scalars, index, staged):
-    if not staged:
+def block_of(scalars, index, bits):
+    if not bits:
         return index
-    z = lax.bitwise_xor(scalars[Z], turned(lax.rem(index, 4)))
-    x = jnp.where(index < 4, scalars[X], 1 - scalars[X])
-    return 4 * x + z
+    flips = [(index // 4) * bits[0], (index // 2 % 2) * bits[1], (index % 2) * bits[2]]
+    owner = lax.bitwise_xor(2 * scalars[Z] + scalars[X], sum(flips))
+    return 4 * lax.rem(owner, 2) + owner // 2
 
 
 def gathered(pieces, target, sems, first):
@@ -529,7 +525,7 @@
             copy.wait()
 
     if staged:
-        spots = [block_of(scalars, 2 * step + i, True) for i in (0, 1)]
+        spots = [block_of(scalars, 2 * step + i, (1, 2, 4)) for i in (0, 1)]
         columns = [pl.ds(pl.multiple_of(spot * 128, 128), 128) for spot in spots]
         left = jnp.concatenate([left_ref[:, c] for c in columns], axis=1)
     else:
@@ -578,7 +574,8 @@
     )
 
 
-def head_outer_kernel(counts, staged, scalars, *refs):
+def head_outer_kernel(counts, bits, scalars, *refs):
+    staged = bits is not None
     products = []
     for left_count, right_count in counts:
         products.append((refs[:left_count], refs[left_count : left_count + right_count]))
@@ -608,14 +605,14 @@
     if staged:
         rows = total_ref.shape[0] // 8
         for index in range(8):
-            source = pl.ds(pl.multiple_of(block_of(scalars, index, True) * rows, 16), rows)
+            source = pl.ds(pl.multiple_of(block_of(scalars, index, bits) * rows, 16), rows)
             at = index % 4 * rows
             outs[index // 4][at : at + rows, :] = total_ref[source, :]
     else:
         outs[0][...] = total_ref[...]
 
 
-def head_outer(scalars, products, staged):
+def head_outer(scalars, products, bits):
     inputs, counts, scratch = [], [], []
     height, width, flops = 0, products[0][1][0].shape[1], 0
     for lefts, rights in products:
@@ -626,9 +623,9 @@
         scratch += [pltpu.VMEM((slots, width), B16)]
         height += lefts[0].shape[1]
         flops += 2 * slots * lefts[0].shape[1] * width
-    parts = 2 if staged else 1
+    parts = 1 if bits is None else 2
     return call(
-        functools.partial(head_outer_kernel, counts, staged),
+        functools.partial(head_outer_kernel, counts, bits),
         "head_outer",
         scalars,
         inputs,
@@ -654,14 +651,13 @@
     return call(halve_kernel, "halve", scalars, [keep, got], [((rows // 2, width), B16)] * 2)
 
 
-def place_blocks(scalars, pieces):
+def place_blocks(scalars, pieces, bits):
     result = []
     for half, piece in enumerate(pieces):
-        x = scalars[X] if half == 0 else 1 - scalars[X]
         rows = piece.shape[0] // 4
         for index in range(4):
-            z = lax.bitwise_xor(scalars[Z], 2 * (index % 2) + index // 2)
-            result.append((piece[index * rows : index * rows + rows, :], 4 * x + z))
+            value = piece[index * rows : index * rows + rows, :]
+            result.append((value, block_of(scalars, 4 * half + index, bits)))
     return result
 
 
@@ -669,7 +665,7 @@
     pieces, (out_ref, buffer, sems) = refs[:2], refs[2:]
     rows = buffer.shape[1]
     copies = []
-    for index, (value, spot) in enumerate(place_blocks(scalars, pieces)):
+    for index, (value, spot) in enumerate(place_blocks(scalars, pieces, (1, 2, 4))):
         buffer[index] = value.astype(F32)
         target = out_ref.at[pl.ds(pl.multiple_of(spot * rows, rows), rows), :]
         copy = pltpu.make_async_copy(buffer.at[index], target, sems.at[index])
@@ -693,11 +689,11 @@
     return out
 
 
-def place_heads_kernel(pair, has_out, aliased, scalars, *refs):
+def place_heads_kernel(pair, bits, has_out, aliased, scalars, *refs):
     pieces, refs = refs[:2], refs[2 + aliased :]
     qkv_ref, refs = refs[0], refs[1:]
     out_ref, (rows_ref, buffer, sems) = refs[0] if has_out else None, refs[-3:]
-    for value, spot in place_blocks(scalars, pieces):
+    for value, spot in place_blocks(scalars, pieces, bits):
         rows = value.shape[0]
         rows_ref[pl.ds(pl.multiple_of(spot * rows, 16), rows), :] = value.astype(F32)
     copies = []
@@ -717,7 +713,7 @@
         copy.wait()
 
 
-def place_heads(scalars, pieces, pair, pairs, into):
+def place_heads(scalars, pieces, pair, pairs, into, bits):
     total, width = 2 * pieces[0].shape[0], pieces[0].shape[1]
     has_out = total > 384
     inputs = list(pieces) + ([] if into is None else [into])
@@ -726,7 +722,7 @@
     outs = [((3, width, pairs * 128), F32)]
     outs += [((total - 384, width), F32)] if has_out else []
     return call(
-        functools.partial(place_heads_kernel, pair, has_out, int(into is not None)),
+        functools.partial(place_heads_kernel, pair, bits, has_out, int(into is not None)),
         "place_heads",
         scalars,
         inputs,
@@ -743,9 +739,9 @@
 
 
 class DpSum:
-    def __init__(self, scalars, order, keep, send):
-        self.scalars, self.order, self.keep = scalars, order, keep
-        self.got = self.exchanged(send, 1)
+    def __init__(self, scalars, order, bits, keep, send):
+        self.scalars, self.order, self.bits, self.keep = scalars, order, bits, keep
+        self.got = self.exchanged(send, bits[0])
         self.steps = self.run()
 
     def exchanged(self, value, bit):
@@ -758,21 +754,21 @@
     def run(self):
         keep, send = halves_sum(self.scalars, self.keep, self.entered())
         self.order.leave(keep, send)
-        self.got = self.exchanged(send, 2)
+        self.got = self.exchanged(send, self.bits[1])
         yield
         keep, send = halves_sum(self.scalars, keep, self.entered())
         self.order.leave(keep, send)
-        self.got = self.exchanged(send, 4)
+        self.got = self.exchanged(send, self.bits[2])
         yield
         total = (keep.astype(F32) + self.entered().astype(F32)).astype(B16)
         self.order.leave(total)
-        for bit in (4, 2):
+        for bit in self.bits[:0:-1]:
             self.got = self.exchanged(total, bit)
             yield
             total = jnp.concatenate([total, self.entered()], axis=0)
             self.order.leave(total)
         self.total = total
-        self.got = self.exchanged(total, 1)
+        self.got = self.exchanged(total, self.bits[0])
         yield
 
     def pieces(self):
@@ -1147,7 +1143,7 @@
     normed = call(
         first_kernel,
         "first",
-        scalars,
+        lengths,
         [tokens, gains, biases],
         [((share, width), B16)] * row_count,
     )
@@ -1161,14 +1157,17 @@
     def kept(name):
         return [pair[i] for row in rows for i in range(row.count) for pair in row.all[name]]
 
-    def started(out):
+    head_bits = [(2, 1, 4), (1, 2, 4)][:pairs] if staged else [None] * pairs
+
+    def started(out, bits):
         order.leave(*out)
-        return DpSum(scalars, order, *out) if staged else out[0]
+        return DpSum(scalars, order, bits, *out) if staged else out[0]
 
     def summed(lefts, rights):
         values = order.enter(*lefts, *rights)
         count = len(lefts)
-        return started(outer_sum(scalars, values[:count], values[count:], staged))
+        out = outer_sum(scalars, values[:count], values[count:], staged)
+        return started(out, (1, 2, 4))
 
     def heads_summed(pair, attended):
         products = [(listed(row.projected_grad[pair] for row in rows), kept("attn_in"))]
@@ -1178,7 +1177,7 @@
         again = []
         for two in products:
             again.append([[values.pop(0) for _ in side] for side in two])
-        return started(head_outer(scalars, again, staged))
+        return started(head_outer(scalars, again, head_bits[pair]), head_bits[pair])
 
     def tick(*totals):
         if staged:
@@ -1203,9 +1202,9 @@
     lead.out_project(outs)
     for row in others:
         row.attend()
-    lead.middle()
     for row in others:
         row.out_project(outs)
+    lead.middle()
     lead.feed(0, ups, downs)
     if split:
         lead.feed(1, ups, downs)
@@ -1295,11 +1294,13 @@
     if staged:
         grad_down, grad_up = placed_sums["PD"], placed_sums["PU"]
         pieces = heads[0].pieces()
-        grad_qkv, grad_out = place_heads(scalars, pieces, 0, pairs, None)
+        grad_qkv, grad_out = place_heads(scalars, pieces, 0, pairs, None, head_bits[0])
         order.leave(grad_out)
         for pair in range(1, pairs):
             pieces = heads[pair].pieces()
-            (grad_qkv,) = place_heads(scalars, pieces, pair, pairs, grad_qkv)
+            (grad_qkv,) = place_heads(
+                scalars, pieces, pair, pairs, grad_qkv, head_bits[pair]
+            )
         grad_qkv = grad_qkv.transpose(1, 0, 2)
     else:
         grad_down, grad_up, *blocks = [

time: 382 us -> 378 us (0.990)
  waiting for transfers between devices: 143 us -> 139 us
  local copies, waits for them, and re-layouts: 13.7 us -> 9.72 us
    ppermute x5, waiting for transfers between devices: 18.8 us -> 8.72 us  [doubling(): lax.ppermute(values, axis, [(i, i ^ step) for i in range(size)])]
    ppermute x16, waiting for transfers between devices: 64.5 us -> 69.6 us  [swap_chip(): return lax.ppermute(value, 'tensor', [(0, 2), (2, 0), (1, 3), (3, 1)])]
    ppermute x24, waiting for transfers between devices: 52.4 us -> 56.6 us  [exchanged(): return lax.ppermute(value, 'dp', [(i, i ^ bit) for i in range(8)])]
    unnamed x100 -> x82, local copies, waits for them, and re-layouts: 12.4 us -> 8.35 us
  transfers between devices with their start and end apart: 85 -> 85, of which waited for: 35 -> 32; matrix products, arithmetic and copies ran while one was open for 1% -> 1% of each run, Pallas kernels for 38% -> 39%
where the time goes in v5:
time: 378 us; the launch traced here: 374 us
  Pallas kernels  148 us (39%)
  waiting for transfers between devices  139 us (37%)
  starting transfers between devices  72.7 us (19%)
  local copies, waits for them, and re-layouts  9.72 us (3%)
    pallas_call x50, Pallas kernels, call(): pl.pallas_call(kernel, out_shape=[jax.ShapeDtypeStruct(shape, dtype) for...  148 us
    ppermute x16, waiting for transfers between devices, swap_chip(): return lax.ppermute(value, 'tensor', [(0, 2), (2, 0), (1, 3), (3, 1)])  69.6 us
    ppermute x24, waiting for transfers between devices, exchanged(): return lax.ppermute(value, 'dp', [(i, i ^ bit) for i in range(8)])  56.6 us
    ppermute x24, starting transfers between devices, exchanged(): return lax.ppermute(value, 'dp', [(i, i ^ bit) for i in range(8)])  32.7 us
    ppermute x16, starting transfers between devices, swap_chip(): return lax.ppermute(value, 'tensor', [(0, 2), (2, 0), (1, 3), (3, 1)])  25.1 us
    ppermute x40, starting transfers between devices, swap_core(): return lax.ppermute(value, 'tensor', [(0, 1), (1, 0), (2, 3), (3, 2)])  9.45 us
    ppermute x5, waiting for transfers between devices, doubling(): lax.ppermute(values, axis, [(i, i ^ step) for i in range(size)])  8.72 us
    unnamed x82, local copies, waits for them, and re-layouts  8.35 us
  transfers between devices with their start and end apart: 85, of which 32 were waited for; matrix products, arithmetic and copies ran while one was open for 1% of the time, Pallas kernels for 39%

profile of v5, /device:TPU:0, one launch (start us, length us, event | category | flops | bytes accessed | tf_op | source)
XLA Modules:
  0.0 374.1 jit_solution(8709387920249172715)
XLA Ops:
  14.3 7.5 %collective-permute-done.2.x_ref.refs_5_ = bf16[272,1024]{1,0:T(8,128)(2,1)S(1)} collective-permute-done((bf16[272,1024]{1,0:T(8,128)(2,1)S(1)}, bf16[272,1024]{1,0:T(8,128)(2,1)S(1)}, u32[]{:S(2)}, u32[]{:S(2)}) %collective-permute-start.2) | collective-permute-done | bytes 557088 | tf_op jit(solution)/shard_map/ppermute | solution.py:960
  27.5 8.0 %attend.2 = (bf16[544,256]{1,0:T(8,128)(2,1)S(1)}, bf16[544,256]{1,0:T(8,128)(2,1)S(1)}, f32[4,1,1088]{2,1,0:T(1,128)S(1)}) custom-call(s32[8]{0:T(128)S(1)} %concatenate.31.scalars, bf16[272,768]{1,0:T(8,128)(2,1)S(1)} %get-tuple-element.302.refs_0_.refs_4_.refs_8_, bf16[272,768]{1,0:T(8,128)(2,1)S(1)} %collective-permute-done.1.refs_1_.refs_5_.refs_9_, ...), custom_call_target="tpu_custom_call" | custom-call | flops 75759616 | bytes 156672 | tf_op jit(solution)/shard_map/attend/pallas_call | solution.py:114
  35.5 4.4 %collective-permute-done.7.x_ref.refs_9_ = bf16[272,1024]{1,0:T(8,128)(2,1)S(1)} collective-permute-done((bf16[272,1024]{1,0:T(8,128)(2,1)S(1)}, bf16[272,1024]{1,0:T(8,128)(2,1)S(1)}, u32[]{:S(2)}, u32[]{:S(2)}) %collective-permute-start.7) | collective-permute-done | bytes 557088 | tf_op jit(solution)/shard_map/ppermute | solution.py:960
  45.7 8.0 %attend.3 = (bf16[544,256]{1,0:T(8,128)(2,1)S(1)}, bf16[544,256]{1,0:T(8,128)(2,1)S(1)}, f32[4,1,1088]{2,1,0:T(1,128)S(1)}) custom-call(s32[8]{0:T(128)S(1)} %concatenate.31.scalars, bf16[272,768]{1,0:T(8,128)(2,1)S(1)} %get-tuple-element.315.refs_0_.refs_4_.refs_8_, bf16[272,768]{1,0:T(8,128)(2,1)S(1)} %collective-permute-done.11.refs_1_.refs_5_.refs_9_, ...), custom_call_target="tpu_custom_call" | custom-call | flops 75759616 | bytes 156672 | tf_op jit(solution)/shard_map/attend/pallas_call | solution.py:114
  62.1 3.6 feed.4
  66.3 9.4 %collective-permute-done.17.x_ref.refs_1_ = bf16[272,1024]{1,0:T(8,128)(2,1)S(1)} collective-permute-done((bf16[272,1024]{1,0:T(8,128)(2,1)S(1)}, bf16[272,1024]{1,0:T(8,128)(2,1)S(1)}, u32[]{:S(2)}, u32[]{:S(2)}) %collective-permute-start.17) | collective-permute-done | bytes 557088 | tf_op jit(solution)/shard_map/ppermute | solution.py:960
  75.6 3.5 feed.5
  81.5 6.1 %collective-permute-done.19.refs_1_ = bf16[272,1024]{1,0:T(8,128)(2,1)S(1)} collective-permute-done((bf16[272,1024]{1,0:T(8,128)(2,1)S(1)}, bf16[272,1024]{1,0:T(8,128)(2,1)S(1)}, u32[]{:S(2)}, u32[]{:S(2)}) %collective-permute-start.19) | collective-permute-done | bytes 557088 | tf_op jit(solution)/shard_map/ppermute | solution.py:960
  89.1 3.6 feed.6
  94.9 4.6 %collective-permute-done.18.refs_1_ = bf16[272,1024]{1,0:T(8,128)(2,1)S(1)} collective-permute-done((bf16[272,1024]{1,0:T(8,128)(2,1)S(1)}, bf16[272,1024]{1,0:T(8,128)(2,1)S(1)}, u32[]{:S(2)}, u32[]{:S(2)}) %collective-permute-start.18) | collective-permute-done | bytes 557088 | tf_op jit(solution)/shard_map/ppermute | solution.py:960
  111.5 3.5 feed.7
  116.8 6.6 %collective-permute-done.28.x_ref.refs_9_ = bf16[272,1024]{1,0:T(8,128)(2,1)S(1)} collective-permute-done((bf16[272,1024]{1,0:T(8,128)(2,1)S(1)}, bf16[272,1024]{1,0:T(8,128)(2,1)S(1)}, u32[]{:S(2)}, u32[]{:S(2)}) %collective-permute-start.28) | collective-permute-done | bytes 557088 | tf_op jit(solution)/shard_map/ppermute | solution.py:960
  127.2 6.4 %collective-permute-done.27.refs_1_ = bf16[272,1024]{1,0:T(8,128)(2,1)S(1)} collective-permute-done((bf16[272,1024]{1,0:T(8,128)(2,1)S(1)}, bf16[272,1024]{1,0:T(8,128)(2,1)S(1)}, u32[]{:S(2)}, u32[]{:S(2)}) %collective-permute-start.27) | collective-permute-done | bytes 557088 | tf_op jit(solution)/shard_map/ppermute | solution.py:960
  142.8 6.3 %collective-permute-done.33.refs_1_ = bf16[272,1024]{1,0:T(8,128)(2,1)S(1)} collective-permute-done((bf16[272,1024]{1,0:T(8,128)(2,1)S(1)}, bf16[272,1024]{1,0:T(8,128)(2,1)S(1)}, u32[]{:S(2)}, u32[]{:S(2)}) %collective-permute-start.33) | collective-permute-done | bytes 557088 | tf_op jit(solution)/shard_map/ppermute | solution.py:960
  153.3 7.7 %collective-permute-done.37.x_ref.refs_13_ = bf16[272,1024]{1,0:T(8,128)(2,1)S(1)} collective-permute-done((bf16[272,1024]{1,0:T(8,128)(2,1)S(1)}, bf16[272,1024]{1,0:T(8,128)(2,1)S(1)}, u32[]{:S(2)}, u32[]{:S(2)}) %collective-permute-start.37) | collective-permute-done | bytes 557088 | tf_op jit(solution)/shard_map/ppermute | solution.py:960
  164.7 5.5 %collective-permute-done.36.refs_1_.refs_17_ = bf16[272,1024]{1,0:T(8,128)(2,1)S(1)} collective-permute-done((bf16[272,1024]{1,0:T(8,128)(2,1)S(1)}, bf16[272,1024]{1,0:T(8,128)(2,1)S(1)}, u32[]{:S(2)}, u32[]{:S(2)}) %collective-permute-start.36) | collective-permute-done | bytes 557088 | tf_op jit(solution)/shard_map/ppermute | solution.py:960
  175.0 8.1 %outer_sum.2 = (bf16[512,1024]{1,0:T(8,128)(2,1)S(1)}, bf16[512,1024]{1,0:T(8,128)(2,1)S(1)}) custom-call(s32[8]{0:T(128)S(1)} %concatenate.31.scalars, bf16[272,1024]{1,0:T(8,128)(2,1)S(1)} %get-tuple-element.389.refs_0_, bf16[272,1024]{1,0:T(8,128)(2,1)S(1)} %get-tuple-element.390.refs_1_, bf16[272,1024]{1,0:T(8,128)(2,1)S(1)} %collective-permute-done.20.refs_2_, ...), custom_call_target="tpu_custom_call" | custom-call | flops 285212672 | bytes 278528 | tf_op jit(solution)/shard_map/outer_sum/pallas_call | solution.py:114
  184.7 8.0 %outer_sum.3 = (bf16[512,1024]{1,0:T(8,128)(2,1)S(1)}, bf16[512,1024]{1,0:T(8,128)(2,1)S(1)}) custom-call(s32[8]{0:T(128)S(1)} %concatenate.31.scalars, bf16[272,1024]{1,0:T(8,128)(2,1)S(1)} %get-tuple-element.407.x_ref.refs_0_, bf16[272,1024]{1,0:T(8,128)(2,1)S(1)} %collective-permute-done.17.x_ref.refs_1_, ...), custom_call_target="tpu_custom_call" | custom-call | flops 285212672 | bytes 278528 | tf_op jit(solution)/shard_map/outer_sum/pallas_call | solution.py:114
  195.6 6.9 %attend_back.4 = (bf16[544,384]{1,0:T(8,128)(2,1)S(1)}, bf16[544,384]{1,0:T(8,128)(2,1)S(1)}) custom-call(s32[8]{0:T(128)S(1)} %concatenate.31.scalars, bf16[272,768]{1,0:T(8,128)(2,1)S(1)} %get-tuple-element.302.refs_0_.refs_4_.refs_8_, bf16[272,768]{1,0:T(8,128)(2,1)S(1)} %collective-permute-done.1.refs_1_.refs_5_.refs_9_, ...), custom_call_target="tpu_custom_call" | custom-call | flops 94699520 | bytes 191760 | tf_op jit(solution)/shard_map/attend_back/pallas_call | solution.py:114
  202.8 6.7 %attend_back.5 = (bf16[544,384]{1,0:T(8,128)(2,1)S(1)}, bf16[544,384]{1,0:T(8,128)(2,1)S(1)}) custom-call(s32[8]{0:T(128)S(1)} %concatenate.31.scalars, bf16[272,768]{1,0:T(8,128)(2,1)S(1)} %get-tuple-element.302.refs_0_.refs_4_.refs_8_, bf16[272,768]{1,0:T(8,128)(2,1)S(1)} %collective-permute-done.1.refs_1_.refs_5_.refs_9_, ...), custom_call_target="tpu_custom_call" | custom-call | flops 94699520 | bytes 191760 | tf_op jit(solution)/shard_map/attend_back/pallas_call | solution.py:114
  216.4 6.7 %attend_back.6 = (bf16[544,384]{1,0:T(8,128)(2,1)S(1)}, bf16[544,384]{1,0:T(8,128)(2,1)S(1)}) custom-call(s32[8]{0:T(128)S(1)} %concatenate.31.scalars, bf16[272,768]{1,0:T(8,128)(2,1)S(1)} %get-tuple-element.315.refs_0_.refs_4_.refs_8_, bf16[272,768]{1,0:T(8,128)(2,1)S(1)} %collective-permute-done.11.refs_1_.refs_5_.refs_9_, ...), custom_call_target="tpu_custom_call" | custom-call | flops 94699520 | bytes 191760 | tf_op jit(solution)/shard_map/attend_back/pallas_call | solution.py:114
  229.3 7.9 %head_outer.2 = (bf16[320,1024]{1,0:T(8,128)(2,1)S(1)}, bf16[320,1024]{1,0:T(8,128)(2,1)S(1)}) custom-call(s32[8]{0:T(128)S(1)} %concatenate.31.scalars, bf16[544,384]{1,0:T(8,128)(2,1)S(1)} %get-tuple-element.482.refs_0_, bf16[544,384]{1,0:T(8,128)(2,1)S(1)} %get-tuple-element.454.refs_1_, bf16[544,384]{1,0:T(8,128)(2,1)S(1)} %get-tuple-element.511.refs_2_.refs_0_, ...), custom_call_target="tpu_custom_call" | custom-call | flops 178257920 | bytes 365568 | tf_op jit(solution)/shard_map/head_outer/pallas_call | solution.py:114
  242.2 6.7 %attend_back.7 = (bf16[544,384]{1,0:T(8,128)(2,1)S(1)}, bf16[544,384]{1,0:T(8,128)(2,1)S(1)}) custom-call(s32[8]{0:T(128)S(1)} %concatenate.31.scalars, bf16[272,768]{1,0:T(8,128)(2,1)S(1)} %get-tuple-element.315.refs_0_.refs_4_.refs_8_, bf16[272,768]{1,0:T(8,128)(2,1)S(1)} %collective-permute-done.11.refs_1_.refs_5_.refs_9_, ...), custom_call_target="tpu_custom_call" | custom-call | flops 94699520 | bytes 191760 | tf_op jit(solution)/shard_map/attend_back/pallas_call | solution.py:114
  252.8 6.0 %head_outer.3 = (bf16[192,1024]{1,0:T(8,128)(2,1)S(1)}, bf16[192,1024]{1,0:T(8,128)(2,1)S(1)}) custom-call(s32[8]{0:T(128)S(1)} %concatenate.31.scalars, bf16[544,384]{1,0:T(8,128)(2,1)S(1)} %get-tuple-element.496.refs_1_.refs_0_, bf16[544,384]{1,0:T(8,128)(2,1)S(1)} %get-tuple-element.497.refs_1_, bf16[544,384]{1,0:T(8,128)(2,1)S(1)} %get-tuple-element.512.refs_2_.refs_1_, ...), custom_call_target="tpu_custom_call" | custom-call | flops 106954752 | bytes 191488 | tf_op jit(solution)/shard_map/head_outer/pallas_call | solution.py:114
  259.9 4.4 %collective-permute-done.63 = bf16[128,1024]{1,0:T(8,128)(2,1)S(1)} collective-permute-done((bf16[128,1024]{1,0:T(8,128)(2,1)S(1)}, bf16[128,1024]{1,0:T(8,128)(2,1)S(1)}, u32[]{:S(2)}, u32[]{:S(2)}) %collective-permute-start.63) | collective-permute-done | bytes 262176 | tf_op jit(solution)/shard_map/ppermute | solution.py:748
  269.0 9.8 %collective-permute-done.62.got_ref = bf16[320,1024]{1,0:T(8,128)(2,1)S(1)} collective-permute-done((bf16[320,1024]{1,0:T(8,128)(2,1)S(1)}, bf16[320,1024]{1,0:T(8,128)(2,1)S(1)}, u32[]{:S(2)}, u32[]{:S(2)}) %collective-permute-start.62) | collective-permute-done | bytes 655392 | tf_op jit(solution)/shard_map/ppermute | solution.py:748
  281.1 5.6 %collective-permute-done.59 = bf16[128,1024]{1,0:T(8,128)(2,1)S(1)} collective-permute-done((bf16[128,1024]{1,0:T(8,128)(2,1)S(1)}, bf16[128,1024]{1,0:T(8,128)(2,1)S(1)}, u32[]{:S(2)}, u32[]{:S(2)}) %collective-permute-start.59) | collective-permute-done | bytes 262176 | tf_op jit(solution)/shard_map/ppermute | solution.py:748
  293.6 8.4 %collective-permute-done.64 = bf16[128,1024]{1,0:T(8,128)(2,1)S(1)} collective-permute-done((bf16[128,1024]{1,0:T(8,128)(2,1)S(1)}, bf16[128,1024]{1,0:T(8,128)(2,1)S(1)}, u32[]{:S(2)}, u32[]{:S(2)}) %collective-permute-start.64) | collective-permute-done | bytes 262176 | tf_op jit(solution)/shard_map/ppermute | solution.py:748
  308.0 10.0 %collective-permute-done.70 = bf16[80,1024]{1,0:T(8,128)(2,1)S(1)} collective-permute-done((bf16[80,1024]{1,0:T(8,128)(2,1)S(1)}, bf16[80,1024]{1,0:T(8,128)(2,1)S(1)}, u32[]{:S(2)}, u32[]{:S(2)}) %collective-permute-start.70) | collective-permute-done | bytes 163872 | tf_op jit(solution)/shard_map/ppermute | solution.py:748
  318.1 3.4 collective-permute-start.74
  321.5 4.2 %collective-permute-done.69.got_ref = bf16[96,1024]{1,0:T(8,128)(2,1)S(1)} collective-permute-done((bf16[96,1024]{1,0:T(8,128)(2,1)S(1)}, bf16[96,1024]{1,0:T(8,128)(2,1)S(1)}, u32[]{:S(2)}, u32[]{:S(2)}) %collective-permute-start.69) | collective-permute-done | bytes 196640 | tf_op jit(solution)/shard_map/ppermute | solution.py:748
  336.6 6.2 %collective-permute-done.75 = bf16[160,1024]{1,0:T(8,128)(2,1)S(1)} collective-permute-done((bf16[160,1024]{1,0:T(8,128)(2,1)S(1)}, bf16[160,1024]{1,0:T(8,128)(2,1)S(1)}, u32[]{:S(2)}, u32[]{:S(2)}) %collective-permute-start.75) | collective-permute-done | bytes 327712 | tf_op jit(solution)/shard_map/ppermute | solution.py:748
  (292 shorter events, 168.5 us)
Async XLA Ops:
  6.0 15.8 %collective-permute-start.2 = (bf16[272,1024]{1,0:T(8,128)(2,1)S(1)}, bf16[272,1024]{1,0:T(8,128)(2,1)S(1)}, u32[]{:S(2)}, u32[]{:S(2)}) collective-permute-start(bf16[272,1024]{1,0:T(8,128)(2,1)S(1)} %get-tuple-element.500.x_ref.refs_4_), channel_id=1, source_target_pairs={{0,2},{2,0},{1,3},{3,1},{4,6},{6,4},{5,7},{7,5},{8,10},{10,8},{9,1... | collective-permute-start | bytes 1671176 | tf_op jit(solution)/shard_map/ppermute | solution.py:960
  24.1 38.1 %collective-permute-start.15 = (bf16[1024,1024]{1,0:T(8,128)(2,1)S(1)}, bf16[1024,1024]{1,0:T(8,128)(2,1)S(1)}, u32[]{:S(2)}, u32[]{:S(2)}) collective-permute-start(bf16[1024,1024]{1,0:T(8,128)(2,1)S(1)} %copy-done), channel_id=1, source_target_pairs={{0,1},{1,0},{2,3},{3,2},{4,5},{5,4},{6,7},{7,6},{8,9},{9,8},{10,11... | collective-permute-start | bytes 6291464 | tf_op jit(solution)/shard_map/ppermute | solution.py:956
  24.5 37.6 %collective-permute-start.16 = (bf16[1024,1024]{1,0:T(8,128)(2,1)S(1)}, bf16[1024,1024]{1,0:T(8,128)(2,1)S(1)}, u32[]{:S(2)}, u32[]{:S(2)}) collective-permute-start(bf16[1024,1024]{1,0:T(8,128)(2,1)S(1)} %copy-done.1), channel_id=1, source_target_pairs={{0,1},{1,0},{2,3},{3,2},{4,5},{5,4},{6,7},{7,6},{8,9},{9,8},{10,11... | collective-permute-start | bytes 6291464 | tf_op jit(solution)/shard_map/ppermute | solution.py:956
  60.0 15.6 %collective-permute-start.17 = (bf16[272,1024]{1,0:T(8,128)(2,1)S(1)}, bf16[272,1024]{1,0:T(8,128)(2,1)S(1)}, u32[]{:S(2)}, u32[]{:S(2)}) collective-permute-start(bf16[272,1024]{1,0:T(8,128)(2,1)S(1)} %get-tuple-element.407.x_ref.refs_0_), channel_id=1, source_target_pairs={{0,2},{2,0},{1,3},{3,1},{4,6},{6,4},{5,7},{7,5},{8,10},{10,8},{9,1... | collective-permute-start | bytes 1671176 | tf_op jit(solution)/shard_map/ppermute | solution.py:960
  61.8 25.8 %collective-permute-start.19 = (bf16[272,1024]{1,0:T(8,128)(2,1)S(1)}, bf16[272,1024]{1,0:T(8,128)(2,1)S(1)}, u32[]{:S(2)}, u32[]{:S(2)}) collective-permute-start(bf16[272,1024]{1,0:T(8,128)(2,1)S(1)} %get-tuple-element.324), channel_id=1, source_target_pairs={{0,2},{2,0},{1,3},{3,1},{4,6},{6,4},{5,7},{7,5},{8,10},{10,8},{9,1... | collective-permute-start | bytes 1671176 | tf_op jit(solution)/shard_map/ppermute | solution.py:960
  62.1 19.4 %collective-permute-start.21 = (bf16[272,1024]{1,0:T(8,128)(2,1)S(1)}, bf16[272,1024]{1,0:T(8,128)(2,1)S(1)}, u32[]{:S(2)}, u32[]{:S(2)}) collective-permute-start(bf16[272,1024]{1,0:T(8,128)(2,1)S(1)} %get-tuple-element.407.x_ref.refs_0_), channel_id=1, source_target_pairs={{0,1},{1,0},{2,3},{3,2},{4,5},{5,4},{6,7},{7,6},{8,9},{9,8},{10,11... | collective-permute-start | bytes 1671176 | tf_op jit(solution)/shard_map/ppermute | solution.py:956
  79.8 19.7 %collective-permute-start.18 = (bf16[272,1024]{1,0:T(8,128)(2,1)S(1)}, bf16[272,1024]{1,0:T(8,128)(2,1)S(1)}, u32[]{:S(2)}, u32[]{:S(2)}) collective-permute-start(bf16[272,1024]{1,0:T(8,128)(2,1)S(1)} %get-tuple-element.331), channel_id=1, source_target_pairs={{0,2},{2,0},{1,3},{3,1},{4,6},{6,4},{5,7},{7,5},{8,10},{10,8},{9,1... | collective-permute-start | bytes 1671176 | tf_op jit(solution)/shard_map/ppermute | solution.py:960
  93.2 18.3 %collective-permute-start.24 = (bf16[272,1024]{1,0:T(8,128)(2,1)S(1)}, bf16[272,1024]{1,0:T(8,128)(2,1)S(1)}, u32[]{:S(2)}, u32[]{:S(2)}) collective-permute-start(bf16[272,1024]{1,0:T(8,128)(2,1)S(1)} %get-tuple-element.411.x_ref.refs_4_), channel_id=1, source_target_pairs={{0,2},{2,0},{1,3},{3,1},{4,6},{6,4},{5,7},{7,5},{8,10},{10,8},{9,1... | collective-permute-start | bytes 1671176 | tf_op jit(solution)/shard_map/ppermute | solution.py:960
  101.8 21.6 %collective-permute-start.28 = (bf16[272,1024]{1,0:T(8,128)(2,1)S(1)}, bf16[272,1024]{1,0:T(8,128)(2,1)S(1)}, u32[]{:S(2)}, u32[]{:S(2)}) collective-permute-start(bf16[272,1024]{1,0:T(8,128)(2,1)S(1)} %get-tuple-element.397.x_ref.refs_8_), channel_id=1, source_target_pairs={{0,2},{2,0},{1,3},{3,1},{4,6},{6,4},{5,7},{7,5},{8,10},{10,8},{9,1... | collective-permute-start | bytes 1671176 | tf_op jit(solution)/shard_map/ppermute | solution.py:960
  107.5 15.9 %collective-permute-start.29 = (bf16[272,1024]{1,0:T(8,128)(2,1)S(1)}, bf16[272,1024]{1,0:T(8,128)(2,1)S(1)}, u32[]{:S(2)}, u32[]{:S(2)}) collective-permute-start(bf16[272,1024]{1,0:T(8,128)(2,1)S(1)} %get-tuple-element.351), channel_id=1, source_target_pairs={{0,1},{1,0},{2,3},{3,2},{4,5},{5,4},{6,7},{7,6},{8,9},{9,8},{10,11... | collective-permute-start | bytes 1671176 | tf_op jit(solution)/shard_map/ppermute | solution.py:956
  107.5 15.9 %collective-permute-start.30 = (bf16[272,1024]{1,0:T(8,128)(2,1)S(1)}, bf16[272,1024]{1,0:T(8,128)(2,1)S(1)}, u32[]{:S(2)}, u32[]{:S(2)}) collective-permute-start(bf16[272,1024]{1,0:T(8,128)(2,1)S(1)} %get-tuple-element.397.x_ref.refs_8_), channel_id=1, source_target_pairs={{0,1},{1,0},{2,3},{3,2},{4,5},{5,4},{6,7},{7,6},{8,9},{9,8},{10,11... | collective-permute-start | bytes 1671176 | tf_op jit(solution)/shard_map/ppermute | solution.py:956
  115.0 18.5 %collective-permute-start.27 = (bf16[272,1024]{1,0:T(8,128)(2,1)S(1)}, bf16[272,1024]{1,0:T(8,128)(2,1)S(1)}, u32[]{:S(2)}, u32[]{:S(2)}) collective-permute-start(bf16[272,1024]{1,0:T(8,128)(2,1)S(1)} %get-tuple-element.350), channel_id=1, source_target_pairs={{0,2},{2,0},{1,3},{3,1},{4,6},{6,4},{5,7},{7,5},{8,10},{10,8},{9,1... | collective-permute-start | bytes 1671176 | tf_op jit(solution)/shard_map/ppermute | solution.py:960
  116.8 18.4 %collective-permute-start.32 = (bf16[272,1024]{1,0:T(8,128)(2,1)S(1)}, bf16[272,1024]{1,0:T(8,128)(2,1)S(1)}, u32[]{:S(2)}, u32[]{:S(2)}) collective-permute-start(bf16[272,1024]{1,0:T(8,128)(2,1)S(1)} %collective-permute-done.24.x_ref.refs_5_), channel_id=1, source_target_pairs={{0,1},{1,0},{2,3},{3,2},{4,5},{5,4},{6,7},{7,6},{8,9},{9,8},{10,11... | collective-permute-start | bytes 1671176 | tf_op jit(solution)/shard_map/ppermute | solution.py:956
  133.5 15.6 %collective-permute-start.33 = (bf16[272,1024]{1,0:T(8,128)(2,1)S(1)}, bf16[272,1024]{1,0:T(8,128)(2,1)S(1)}, u32[]{:S(2)}, u32[]{:S(2)}) collective-permute-start(bf16[272,1024]{1,0:T(8,128)(2,1)S(1)} %get-tuple-element.355), channel_id=1, source_target_pairs={{0,2},{2,0},{1,3},{3,1},{4,6},{6,4},{5,7},{7,5},{8,10},{10,8},{9,1... | collective-permute-start | bytes 1671176 | tf_op jit(solution)/shard_map/ppermute | solution.py:960
  137.2 23.8 %collective-permute-start.37 = (bf16[272,1024]{1,0:T(8,128)(2,1)S(1)}, bf16[272,1024]{1,0:T(8,128)(2,1)S(1)}, u32[]{:S(2)}, u32[]{:S(2)}) collective-permute-start(bf16[272,1024]{1,0:T(8,128)(2,1)S(1)} %get-tuple-element.401.x_ref.refs_12_), channel_id=1, source_target_pairs={{0,2},{2,0},{1,3},{3,1},{4,6},{6,4},{5,7},{7,5},{8,10},{10,8},{9,1... | collective-permute-start | bytes 1671176 | tf_op jit(solution)/shard_map/ppermute | solution.py:960
  142.2 18.8 %collective-permute-start.38 = (bf16[272,1024]{1,0:T(8,128)(2,1)S(1)}, bf16[272,1024]{1,0:T(8,128)(2,1)S(1)}, u32[]{:S(2)}, u32[]{:S(2)}) collective-permute-start(bf16[272,1024]{1,0:T(8,128)(2,1)S(1)} %get-tuple-element.371), channel_id=1, source_target_pairs={{0,1},{1,0},{2,3},{3,2},{4,5},{5,4},{6,7},{7,6},{8,9},{9,8},{10,11... | collective-permute-start | bytes 1671176 | tf_op jit(solution)/shard_map/ppermute | solution.py:956
  142.3 18.7 %collective-permute-start.39 = (bf16[272,1024]{1,0:T(8,128)(2,1)S(1)}, bf16[272,1024]{1,0:T(8,128)(2,1)S(1)}, u32[]{:S(2)}, u32[]{:S(2)}) collective-permute-start(bf16[272,1024]{1,0:T(8,128)(2,1)S(1)} %get-tuple-element.401.x_ref.refs_12_), channel_id=1, source_target_pairs={{0,1},{1,0},{2,3},{3,2},{4,5},{5,4},{6,7},{7,6},{8,9},{9,8},{10,11... | collective-permute-start | bytes 1671176 | tf_op jit(solution)/shard_map/ppermute | solution.py:956
  151.5 18.7 %collective-permute-start.36 = (bf16[272,1024]{1,0:T(8,128)(2,1)S(1)}, bf16[272,1024]{1,0:T(8,128)(2,1)S(1)}, u32[]{:S(2)}, u32[]{:S(2)}) collective-permute-start(bf16[272,1024]{1,0:T(8,128)(2,1)S(1)} %get-tuple-element.469.refs_0_.refs_16_), channel_id=1, source_target_pairs={{0,2},{2,0},{1,3},{3,1},{4,6},{6,4},{5,7},{7,5},{8,10},{10,8},{9,1... | collective-permute-start | bytes 1671176 | tf_op jit(solution)/shard_map/ppermute | solution.py:960
  170.7 22.0 %collective-permute-start.41 = (bf16[272,1024]{1,0:T(8,128)(2,1)S(1)}, bf16[272,1024]{1,0:T(8,128)(2,1)S(1)}, u32[]{:S(2)}, u32[]{:S(2)}) collective-permute-start(bf16[272,1024]{1,0:T(8,128)(2,1)S(1)} %get-tuple-element.375), channel_id=1, source_target_pairs={{0,2},{2,0},{1,3},{3,1},{4,6},{6,4},{5,7},{7,5},{8,10},{10,8},{9,1... | collective-permute-start | bytes 1671176 | tf_op jit(solution)/shard_map/ppermute | solution.py:960
  183.1 27.1 %collective-permute-start.50 = (bf16[512,1024]{1,0:T(8,128)(2,1)S(1)}, bf16[512,1024]{1,0:T(8,128)(2,1)S(1)}, u32[]{:S(2)}, u32[]{:S(2)}) collective-permute-start(bf16[512,1024]{1,0:T(8,128)(2,1)S(1)} %get-tuple-element.406), channel_id=1, source_target_pairs={{0,4},{4,0},{8,12},{12,8},{16,20},{20,16},{24,28},{28,24},{1,5},{5... | collective-permute-start | bytes 3145736 | tf_op jit(solution)/shard_map/ppermute | solution.py:748
  195.0 16.3 %collective-permute-start.49 = (bf16[272,1024]{1,0:T(8,128)(2,1)S(1)}, bf16[272,1024]{1,0:T(8,128)(2,1)S(1)}, u32[]{:S(2)}, u32[]{:S(2)}) collective-permute-start(bf16[272,1024]{1,0:T(8,128)(2,1)S(1)} %get-tuple-element.473.refs_0_.refs_20_), channel_id=1, source_target_pairs={{0,2},{2,0},{1,3},{3,1},{4,6},{6,4},{5,7},{7,5},{8,10},{10,8},{9,1... | collective-permute-start | bytes 1671176 | tf_op jit(solution)/shard_map/ppermute | solution.py:960
  209.8 27.4 %collective-permute-start.48 = (bf16[512,1024]{1,0:T(8,128)(2,1)S(1)}, bf16[512,1024]{1,0:T(8,128)(2,1)S(1)}, u32[]{:S(2)}, u32[]{:S(2)}) collective-permute-start(bf16[512,1024]{1,0:T(8,128)(2,1)S(1)} %get-tuple-element.424), channel_id=1, source_target_pairs={{0,4},{4,0},{8,12},{12,8},{16,20},{20,16},{24,28},{28,24},{1,5},{5... | collective-permute-start | bytes 3145736 | tf_op jit(solution)/shard_map/ppermute | solution.py:748
  226.6 15.5 %collective-permute-start.58 = (bf16[128,1024]{1,0:T(8,128)(2,1)S(1)}, bf16[128,1024]{1,0:T(8,128)(2,1)S(1)}, u32[]{:S(2)}, u32[]{:S(2)}) collective-permute-start(bf16[128,1024]{1,0:T(8,128)(2,1)S(1)} %get-tuple-element.452), channel_id=1, source_target_pairs={{0,16},{4,20},{8,24},{12,28},{16,0},{20,4},{24,8},{28,12},{1,17},{... | collective-permute-start | bytes 786440 | tf_op jit(solution)/shard_map/ppermute | solution.py:748
  249.6 29.1 %collective-permute-start.62 = (bf16[320,1024]{1,0:T(8,128)(2,1)S(1)}, bf16[320,1024]{1,0:T(8,128)(2,1)S(1)}, u32[]{:S(2)}, u32[]{:S(2)}) collective-permute-start(bf16[320,1024]{1,0:T(8,128)(2,1)S(1)} %get-tuple-element.478), channel_id=1, source_target_pairs={{0,8},{4,12},{8,0},{12,4},{16,24},{20,28},{24,16},{28,20},{1,9},{5... | collective-permute-start | bytes 1966088 | tf_op jit(solution)/shard_map/ppermute | solution.py:748
  258.9 21.6 %collective-permute-start.61 = (bf16[192,1024]{1,0:T(8,128)(2,1)S(1)}, bf16[192,1024]{1,0:T(8,128)(2,1)S(1)}, u32[]{:S(2)}, u32[]{:S(2)}) collective-permute-start(bf16[192,1024]{1,0:T(8,128)(2,1)S(1)} %get-tuple-element.509), channel_id=1, source_target_pairs={{0,4},{4,0},{8,12},{12,8},{16,20},{20,16},{24,28},{28,24},{1,5},{5... | collective-permute-start | bytes 1179656 | tf_op jit(solution)/shard_map/ppermute | solution.py:748
  264.3 26.0 %collective-permute-start.66 = (bf16[256,1024]{1,0:T(8,128)(2,1)S(1)}, bf16[256,1024]{1,0:T(8,128)(2,1)S(1)}, u32[]{:S(2)}, u32[]{:S(2)}) collective-permute-start(bf16[256,1024]{1,0:T(8,128)(2,1)S(1)} %pad_maximum_fusion.5), channel_id=1, source_target_pairs={{0,8},{4,12},{8,0},{12,4},{16,24},{20,28},{24,16},{28,20},{1,9},{5... | collective-permute-start | bytes 1572872 | tf_op jit(solution)/shard_map/ppermute | solution.py:748
  264.4 22.4 %collective-permute-start.59 = (bf16[128,1024]{1,0:T(8,128)(2,1)S(1)}, bf16[128,1024]{1,0:T(8,128)(2,1)S(1)}, u32[]{:S(2)}, u32[]{:S(2)}) collective-permute-start(bf16[128,1024]{1,0:T(8,128)(2,1)S(1)} %get-tuple-element.495), channel_id=1, source_target_pairs={{0,16},{4,20},{8,24},{12,28},{16,0},{20,4},{24,8},{28,12},{1,17},{... | collective-permute-start | bytes 786440 | tf_op jit(solution)/shard_map/ppermute | solution.py:748
  290.4 37.7 %collective-permute-start.72 = (bf16[512,1024]{1,0:T(8,128)(2,1)S(1)}, bf16[512,1024]{1,0:T(8,128)(2,1)S(1)}, u32[]{:S(2)}, u32[]{:S(2)}) collective-permute-start(bf16[512,1024]{1,0:T(8,128)(2,1)S(1)} %pad_maximum_fusion.2.refs_0_), channel_id=1, source_target_pairs={{0,4},{4,0},{8,12},{12,8},{16,20},{20,16},{24,28},{28,24},{1,5},{5... | collective-permute-start | bytes 3145736 | tf_op jit(solution)/shard_map/ppermute | solution.py:748
  302.1 24.4 %collective-permute-start.68 = (bf16[256,1024]{1,0:T(8,128)(2,1)S(1)}, bf16[256,1024]{1,0:T(8,128)(2,1)S(1)}, u32[]{:S(2)}, u32[]{:S(2)}) collective-permute-start(bf16[256,1024]{1,0:T(8,128)(2,1)S(1)} %pad_maximum_fusion.6), channel_id=1, source_target_pairs={{0,8},{4,12},{8,0},{12,4},{16,24},{20,28},{24,16},{28,20},{1,9},{5... | collective-permute-start | bytes 1572872 | tf_op jit(solution)/shard_map/ppermute | solution.py:748
  302.1 24.4 %collective-permute-start.67 = (bf16[272,1024]{1,0:T(8,128)(2,1)S(1)}, bf16[272,1024]{1,0:T(8,128)(2,1)S(1)}, u32[]{:S(2)}, u32[]{:S(2)}) collective-permute-start(bf16[272,1024]{1,0:T(8,128)(2,1)S(1)} %get-tuple-element.516), channel_id=1, source_target_pairs={{0,2},{2,0},{1,3},{3,1},{4,6},{6,4},{5,7},{7,5},{8,10},{10,8},{9,1... | collective-permute-start | bytes 1671176 | tf_op jit(solution)/shard_map/ppermute | solution.py:960
  306.5 19.3 %collective-permute-start.69 = (bf16[96,1024]{1,0:T(8,128)(2,1)S(1)}, bf16[96,1024]{1,0:T(8,128)(2,1)S(1)}, u32[]{:S(2)}, u32[]{:S(2)}) collective-permute-start(bf16[96,1024]{1,0:T(8,128)(2,1)S(1)} %get-tuple-element.522), channel_id=1, source_target_pairs={{0,8},{4,12},{8,0},{12,4},{16,24},{20,28},{24,16},{28,20},{1,9},{5... | collective-permute-start | bytes 589832 | tf_op jit(solution)/shard_map/ppermute | solution.py:748
  333.4 30.9 %collective-permute-start.81 = (bf16[512,1024]{1,0:T(8,128)(2,1)S(1)}, bf16[512,1024]{1,0:T(8,128)(2,1)S(1)}, u32[]{:S(2)}, u32[]{:S(2)}) collective-permute-start(bf16[512,1024]{1,0:T(8,128)(2,1)S(1)} %pad_maximum_fusion.3.refs_0_), channel_id=1, source_target_pairs={{0,4},{4,0},{8,12},{12,8},{16,20},{20,16},{24,28},{28,24},{1,5},{5... | collective-permute-start | bytes 3145736 | tf_op jit(solution)/shard_map/ppermute | solution.py:748
  (94 other events, 751.6 us)
